TPU v7x, 512 devices: a whole 4x4x16 slice. The times are simulated.
512 devices in a mesh: pipe: 16 (over y, z_lo), dp: 32 (over z_hi, x, core).
Axes of the slice: x: 4, y: 4, z: 16 (z_hi: 4, z_lo: 4; z = z_hi * 4 + z_lo), core: 2. Of those that a mesh axis runs over, the one named last changes fastest.
Arguments:
- grad_out: bfloat16 [16, 2, 2, 128, 3584], P('pipe', None, None, 'dp'), may hold values from -6 to 6
- hidden: bfloat16 [16, 2, 2, 128, 9216], P('pipe', None, None, None, 'dp'), may hold values from -5 to 5
- weights: bfloat16 [16, 9216, 3584], P('pipe', 'dp'), may hold values from -5 to 5
- counts: int32 [16, 2, 2, 32], P('pipe', None, None, 'dp'), may hold values from 1 to 4
Outputs:
- grad_hidden: bfloat16 [16, 2, 2, 128, 9216], P('pipe', None, None, None, 'dp')
- new_weights: bfloat16 [16, 9216, 3584], P('pipe', 'dp')
All inputs are finite; a program needn't handle non-finite values.
Results may differ from a plain program's by a relative error of at most 0.0034.
Values may be sent and summed in bfloat16 or wider, within the bound.
No kernel may reach another device: no remote copies, remote signals or barrier semaphores. Data moves between devices by JAX's collectives and lax.ppermute only.
A program may use at most 64 MiB of HBM per device.

v0:
```python
import jax
import jax.numpy as jnp
from jax import lax
from jax.sharding import PartitionSpec as P

step_rate = 2.0


def from_partner(block, axis, apart):
    count = lax.axis_size(axis)
    route = []
    for low in range(count):
        high = low | 1 << apart
        if high != low and high < count:
            route += [(low, high), (high, low)]
    return lax.ppermute(block, axis, route)


def shards(grad_out, hidden, weights, counts):
    row_total = grad_out.shape[3]
    full_width = grad_out.shape[4]
    micro = hidden.shape[2]
    group_rows = hidden.shape[3]
    share = hidden.shape[4]
    scale_factor = float(full_width) ** (-0.5)
    slot_index = lax.broadcasted_iota(jnp.int32, (1, 1, 1, row_total), 3)
    live_rows = slot_index < counts
    masked = jnp.where(live_rows[..., None], grad_out, jnp.zeros_like(grad_out))
    own_weight = weights[0]
    pipe_bits = lax.axis_size("pipe").bit_length() - 1
    outgoing = jnp.concatenate(
        [masked[0, 1].reshape(micro, -1), hidden[0, 1].reshape(micro, -1)], axis=1
    )
    incoming = outgoing
    for fetch_bit_index in range(pipe_bits):
        incoming = from_partner(incoming, "pipe", fetch_bit_index)
    split_at = row_total * full_width
    mirror_masked = incoming[:, :split_at].reshape(micro, row_total, full_width)
    mirror_hidden = incoming[:, split_at:].reshape(micro, group_rows, share)
    mirror_masked, mirror_hidden = (mirror_masked, mirror_hidden)
    both_masked = jnp.stack([masked[0, 0], mirror_masked], axis=0)
    both_hidden = jnp.stack([hidden[0, 0], mirror_hidden], axis=0)
    piece = lax.all_gather(both_masked, "dp", axis=2, tiled=True)
    rows_out = jnp.einsum("rmkd,hd->rmkh", piece, own_weight, preferred_element_type=jnp.float32)
    grad_acc = rows_out
    weight_acc = jnp.einsum(
        "rmkh,rmkd->rhd", both_hidden, piece, preferred_element_type=jnp.float32
    )
    grad_acc, weight_acc = (grad_acc, weight_acc)
    grad_rows = (grad_acc * scale_factor).astype(jnp.bfloat16)
    partial_value = (weight_acc * scale_factor).astype(jnp.bfloat16)
    gradient = partial_value[0].astype(jnp.float32) + partial_value[1].astype(jnp.float32)
    new_weight = (own_weight.astype(jnp.float32) - step_rate * gradient).astype(jnp.bfloat16)
    returned = grad_rows[1]
    for bit_index in range(pipe_bits):
        returned = from_partner(returned, "pipe", bit_index)
    grad_hidden = jnp.stack([grad_rows[0], returned], axis=0)[None]
    return (grad_hidden, new_weight[None])


def solution(mesh):
    return jax.shard_map(
        shards,
        mesh=mesh,
        in_specs=(
            P("pipe", None, None, "dp", None),
            P("pipe", None, None, None, "dp"),
            P("pipe", "dp", None),
            P("pipe", None, None, "dp"),
        ),
        out_specs=(P("pipe", None, None, None, "dp"), P("pipe", "dp", None)),
        check_vma=False,
    )
```

profile of v0, /device:TPU:1, one launch (start us, length us, event | category | flops | bytes accessed | tf_op | source)
XLA Modules:
  0.0 191.8 jit_solution(3951308479756435278)
XLA Ops:
  7.2 0.7 iota_compare_fusion
  7.9 1.1 broadcast_select_fusion
  9.0 0.1 slice_bitcast_fusion.2
  9.0 1.0 slice_bitcast_fusion.1
  10.1 0.2 copy.9
  10.2 0.3 reshape_squeeze.7
  10.5 0.2 pad_maximum_fusion
  10.7 4.4 %collective-permute-start = (bf16[2,51200]{1,0:T(2,128)(2,1)S(1)}, bf16[2,51200]{1,0:T(2,128)(2,1)S(1)}, u32[]{:S(2)}, u32[]{:S(2)}) collective-permute-start(bf16[2,51200]{1,0:T(2,128)(2,1)S(1)} %pad_maximum_fusion), channel_id=1, source_target_pairs={{0,32},{32,0},{64,96},{96,64},{128,160},{160,128},{192,224},{224,1... | collective-permute-start | bytes 614408 | tf_op jit(solution)/shard_map/ppermute | solution.py:16
  15.1 3.1 %collective-permute-done = bf16[2,51200]{1,0:T(2,128)(2,1)S(1)} collective-permute-done((bf16[2,51200]{1,0:T(2,128)(2,1)S(1)}, bf16[2,51200]{1,0:T(2,128)(2,1)S(1)}, u32[]{:S(2)}, u32[]{:S(2)}) %collective-permute-start) | collective-permute-done | bytes 204832 | tf_op jit(solution)/shard_map/ppermute | solution.py:16
  18.2 6.4 %collective-permute-start.1 = (bf16[2,51200]{1,0:T(2,128)(2,1)S(1)}, bf16[2,51200]{1,0:T(2,128)(2,1)S(1)}, u32[]{:S(2)}, u32[]{:S(2)}) collective-permute-start(bf16[2,51200]{1,0:T(2,128)(2,1)S(1)} %collective-permute-done), channel_id=1, source_target_pairs={{0,64},{64,0},{32,96},{96,32},{128,192},{192,128},{160,224},{224,1... | collective-permute-start | bytes 614408 | tf_op jit(solution)/shard_map/ppermute | solution.py:16
  24.7 5.3 %collective-permute-done.1 = bf16[2,51200]{1,0:T(2,128)(2,1)S(1)} collective-permute-done((bf16[2,51200]{1,0:T(2,128)(2,1)S(1)}, bf16[2,51200]{1,0:T(2,128)(2,1)S(1)}, u32[]{:S(2)}, u32[]{:S(2)}) %collective-permute-start.1) | collective-permute-done | bytes 204832 | tf_op jit(solution)/shard_map/ppermute | solution.py:16
  30.0 6.7 %collective-permute-start.2 = (bf16[2,51200]{1,0:T(2,128)(2,1)S(1)}, bf16[2,51200]{1,0:T(2,128)(2,1)S(1)}, u32[]{:S(2)}, u32[]{:S(2)}) collective-permute-start(bf16[2,51200]{1,0:T(2,128)(2,1)S(1)} %collective-permute-done.1), channel_id=1, source_target_pairs={{0,128},{128,0},{32,160},{160,32},{64,192},{192,64},{96,224},{224,... | collective-permute-start | bytes 614408 | tf_op jit(solution)/shard_map/ppermute | solution.py:16
  36.8 3.1 %collective-permute-done.2 = bf16[2,51200]{1,0:T(2,128)(2,1)S(1)} collective-permute-done((bf16[2,51200]{1,0:T(2,128)(2,1)S(1)}, bf16[2,51200]{1,0:T(2,128)(2,1)S(1)}, u32[]{:S(2)}, u32[]{:S(2)}) %collective-permute-start.2) | collective-permute-done | bytes 204832 | tf_op jit(solution)/shard_map/ppermute | solution.py:16
  39.9 5.4 %collective-permute-start.3 = (bf16[2,51200]{1,0:T(2,128)(2,1)S(1)}, bf16[2,51200]{1,0:T(2,128)(2,1)S(1)}, u32[]{:S(2)}, u32[]{:S(2)}) collective-permute-start(bf16[2,51200]{1,0:T(2,128)(2,1)S(1)} %collective-permute-done.2), channel_id=1, source_target_pairs={{0,256},{256,0},{32,288},{288,32},{64,320},{320,64},{96,352},{352,... | collective-permute-start | bytes 614408 | tf_op jit(solution)/shard_map/ppermute | solution.py:16
  45.3 3.1 %collective-permute-done.3 = bf16[2,51200]{1,0:T(2,128)(2,1)S(1)} collective-permute-done((bf16[2,51200]{1,0:T(2,128)(2,1)S(1)}, bf16[2,51200]{1,0:T(2,128)(2,1)S(1)}, u32[]{:S(2)}, u32[]{:S(2)}) %collective-permute-start.3) | collective-permute-done | bytes 204832 | tf_op jit(solution)/shard_map/ppermute | solution.py:16
  48.5 0.8 pad_maximum_fusion.1
  49.3 98.0 %all-gather.2.cloned.1.call-done = bf16[2,2,128,3584]{3,1,0,2:T(2,128)(2,1)} async-done(((bf16[2,2,4,3584]{3,1,0,2:T(2,128)(2,1)}), bf16[2,2,128,3584]{3,1,0,2:T(2,128)(2,1)}) %all-gather.2.cloned.1.call-update) | async-done | bytes 3670032 | tf_op jit(solution)/shard_map/all_gather | solution.py:43
  147.4 4.0 %fusion.10 = bf16[2,2,128,288]{2,3,1,0:T(8,128)(2,1)S(1)} fusion(bf16[1,288,3584]{2,1,0:T(8,128)(2,1)} %param.6, bf16[2,2,128,3584]{3,1,0,2:T(2,128)(2,1)} %all-gather.2.cloned.1.call-done), kind=kOutput, calls=%fused_computation.8 | convolution fusion | flops 1057259520 | bytes 6029312 | tf_op jit(solution)/shard_map/rmkd,hd->rmkh/dot_general | solution.py:44
  151.4 1.9 %collective-permute-start.4 = (bf16[2,128,288]{1,2,0:T(8,128)(2,1)S(1)}, bf16[2,128,288]{1,2,0:T(8,128)(2,1)S(1)}, u32[]{:S(2)}, u32[]{:S(2)}) collective-permute-start(bf16[2,128,288]{1,2,0:T(8,128)(2,1)S(1)} %get-tuple-element.5), channel_id=1, source_target_pairs={{0,32},{32,0},{64,96},{96,64},{128,160},{160,128},{192,224},{224,1... | collective-permute-start | bytes 442376 | tf_op jit(solution)/shard_map/ppermute | solution.py:16
  153.3 5.2 %collective-permute-done.4 = bf16[2,128,288]{1,2,0:T(8,128)(2,1)S(1)} collective-permute-done((bf16[2,128,288]{1,2,0:T(8,128)(2,1)S(1)}, bf16[2,128,288]{1,2,0:T(8,128)(2,1)S(1)}, u32[]{:S(2)}, u32[]{:S(2)}) %collective-permute-start.4) | collective-permute-done | bytes 147488 | tf_op jit(solution)/shard_map/ppermute | solution.py:16
  158.5 1.9 collective-permute-start.5
  160.4 0.1 slice.45
  160.5 0.3 stack_reshape.7
  160.8 0.2 copy.12
  161.0 9.1 %collective-permute-done.5 = bf16[2,128,288]{1,2,0:T(8,128)(2,1)S(1)} collective-permute-done((bf16[2,128,288]{1,2,0:T(8,128)(2,1)S(1)}, bf16[2,128,288]{1,2,0:T(8,128)(2,1)S(1)}, u32[]{:S(2)}, u32[]{:S(2)}) %collective-permute-start.5) | collective-permute-done | bytes 147488 | tf_op jit(solution)/shard_map/ppermute | solution.py:16
  170.1 2.4 %collective-permute-start.6 = (bf16[2,128,288]{1,2,0:T(8,128)(2,1)S(1)}, bf16[2,128,288]{1,2,0:T(8,128)(2,1)S(1)}, u32[]{:S(2)}, u32[]{:S(2)}) collective-permute-start(bf16[2,128,288]{1,2,0:T(8,128)(2,1)S(1)} %collective-permute-done.5), channel_id=1, source_target_pairs={{0,128},{128,0},{32,160},{160,32},{64,192},{192,64},{96,224},{224,... | collective-permute-start | bytes 442376 | tf_op jit(solution)/shard_map/ppermute | solution.py:16
  172.5 4.1 %fusion = bf16[2,288,3584]{2,1,0:T(8,128)(2,1)S(1)} fusion(bf16[2,2,128,3584]{3,1,0,2:T(2,128)(2,1)} %all-gather.2.cloned.1.call-done, bf16[1,2,128,288]{2,3,1,0:T(8,128)(2,1)S(1)} %copy.12, bf16[1,2,128,288]{2,3,1,0:T(8,128)(2,1)S(1)} %get-tuple-element.2), kind=kOutput, calls=%fused_computation.1 | convolution fusion | flops 1061240832 | bytes 8093696 | tf_op jit(solution)/shard_map/rmkh,rmkd->rhd/dot_general | solution.py:46
  176.6 0.2 collective-permute-done.6
  176.9 4.2 %collective-permute-start.7 = (bf16[2,128,288]{1,2,0:T(8,128)(2,1)S(1)}, bf16[2,128,288]{1,2,0:T(8,128)(2,1)S(1)}, u32[]{:S(2)}, u32[]{:S(2)}) collective-permute-start(bf16[2,128,288]{1,2,0:T(8,128)(2,1)S(1)} %collective-permute-done.6), channel_id=1, source_target_pairs={{0,256},{256,0},{32,288},{288,32},{64,320},{320,64},{96,352},{352,... | collective-permute-start | bytes 442376 | tf_op jit(solution)/shard_map/ppermute | solution.py:16
  181.1 2.2 %subtract_convert_fusion = bf16[1,288,3584]{2,1,0:T(8,128)(2,1)} fusion(bf16[1,288,3584]{2,1,0:T(8,128)(2,1)S(1)} %copy-done, bf16[2,288,3584]{2,1,0:T(8,128)(2,1)S(1)} %fusion), kind=kLoop, calls=%fused_computation.2 | loop fusion | flops 7225344 | bytes 8257536 | tf_op jit(solution)/shard_map/convert_element_type | solution.py:53
  183.2 1.0 collective-permute-done.7
  184.3 0.7 maximum_bitcast_fusion
  (6 shorter events, 0.1 us)
Async XLA Ops:
  7.2 140.2 %all-gather.2.cloned.1.call-start = ((), (), s32[]{:S(2)}) async-start(), calls=%async_computation | async-start | bytes 3784704 | tf_op jit(solution)/shard_map/all_gather | solution.py:43
  10.7 7.5 %collective-permute-start = (bf16[2,51200]{1,0:T(2,128)(2,1)S(1)}, bf16[2,51200]{1,0:T(2,128)(2,1)S(1)}, u32[]{:S(2)}, u32[]{:S(2)}) collective-permute-start(bf16[2,51200]{1,0:T(2,128)(2,1)S(1)} %pad_maximum_fusion), channel_id=1, source_target_pairs={{0,32},{32,0},{64,96},{96,64},{128,160},{160,128},{192,224},{224,1... | collective-permute-start | bytes 614408 | tf_op jit(solution)/shard_map/ppermute | solution.py:16
  18.2 11.8 %collective-permute-start.1 = (bf16[2,51200]{1,0:T(2,128)(2,1)S(1)}, bf16[2,51200]{1,0:T(2,128)(2,1)S(1)}, u32[]{:S(2)}, u32[]{:S(2)}) collective-permute-start(bf16[2,51200]{1,0:T(2,128)(2,1)S(1)} %collective-permute-done), channel_id=1, source_target_pairs={{0,64},{64,0},{32,96},{96,32},{128,192},{192,128},{160,224},{224,1... | collective-permute-start | bytes 614408 | tf_op jit(solution)/shard_map/ppermute | solution.py:16
  30.0 9.9 %collective-permute-start.2 = (bf16[2,51200]{1,0:T(2,128)(2,1)S(1)}, bf16[2,51200]{1,0:T(2,128)(2,1)S(1)}, u32[]{:S(2)}, u32[]{:S(2)}) collective-permute-start(bf16[2,51200]{1,0:T(2,128)(2,1)S(1)} %collective-permute-done.1), channel_id=1, source_target_pairs={{0,128},{128,0},{32,160},{160,32},{64,192},{192,64},{96,224},{224,... | collective-permute-start | bytes 614408 | tf_op jit(solution)/shard_map/ppermute | solution.py:16
  39.9 8.5 %collective-permute-start.3 = (bf16[2,51200]{1,0:T(2,128)(2,1)S(1)}, bf16[2,51200]{1,0:T(2,128)(2,1)S(1)}, u32[]{:S(2)}, u32[]{:S(2)}) collective-permute-start(bf16[2,51200]{1,0:T(2,128)(2,1)S(1)} %collective-permute-done.2), channel_id=1, source_target_pairs={{0,256},{256,0},{32,288},{288,32},{64,320},{320,64},{96,352},{352,... | collective-permute-start | bytes 614408 | tf_op jit(solution)/shard_map/ppermute | solution.py:16
  151.4 7.1 %collective-permute-start.4 = (bf16[2,128,288]{1,2,0:T(8,128)(2,1)S(1)}, bf16[2,128,288]{1,2,0:T(8,128)(2,1)S(1)}, u32[]{:S(2)}, u32[]{:S(2)}) collective-permute-start(bf16[2,128,288]{1,2,0:T(8,128)(2,1)S(1)} %get-tuple-element.5), channel_id=1, source_target_pairs={{0,32},{32,0},{64,96},{96,64},{128,160},{160,128},{192,224},{224,1... | collective-permute-start | bytes 442376 | tf_op jit(solution)/shard_map/ppermute | solution.py:16
  158.5 11.7 %collective-permute-start.5 = (bf16[2,128,288]{1,2,0:T(8,128)(2,1)S(1)}, bf16[2,128,288]{1,2,0:T(8,128)(2,1)S(1)}, u32[]{:S(2)}, u32[]{:S(2)}) collective-permute-start(bf16[2,128,288]{1,2,0:T(8,128)(2,1)S(1)} %collective-permute-done.4), channel_id=1, source_target_pairs={{0,64},{64,0},{32,96},{96,32},{128,192},{192,128},{160,224},{224,1... | collective-permute-start | bytes 442376 | tf_op jit(solution)/shard_map/ppermute | solution.py:16
  170.1 6.7 %collective-permute-start.6 = (bf16[2,128,288]{1,2,0:T(8,128)(2,1)S(1)}, bf16[2,128,288]{1,2,0:T(8,128)(2,1)S(1)}, u32[]{:S(2)}, u32[]{:S(2)}) collective-permute-start(bf16[2,128,288]{1,2,0:T(8,128)(2,1)S(1)} %collective-permute-done.5), channel_id=1, source_target_pairs={{0,128},{128,0},{32,160},{160,32},{64,192},{192,64},{96,224},{224,... | collective-permute-start | bytes 442376 | tf_op jit(solution)/shard_map/ppermute | solution.py:16
  172.5 8.5 %copy-start = (bf16[1,288,3584]{2,1,0:T(8,128)(2,1)S(1)}, bf16[1,288,3584]{2,1,0:T(8,128)(2,1)}, u32[]{:S(2)}) copy-start(bf16[1,288,3584]{2,1,0:T(8,128)(2,1)} %param.6) | copy-start | bytes 6193156
  176.9 7.4 %collective-permute-start.7 = (bf16[2,128,288]{1,2,0:T(8,128)(2,1)S(1)}, bf16[2,128,288]{1,2,0:T(8,128)(2,1)S(1)}, u32[]{:S(2)}, u32[]{:S(2)}) collective-permute-start(bf16[2,128,288]{1,2,0:T(8,128)(2,1)S(1)} %collective-permute-done.6), channel_id=1, source_target_pairs={{0,256},{256,0},{32,288},{288,32},{64,320},{320,64},{96,352},{352,... | collective-permute-start | bytes 442376 | tf_op jit(solution)/shard_map/ppermute | solution.py:16
Sparse Core Ops, SparseCore 0:
  49.4 97.8 all-gather.1
where the time goes:
time: 194 us; the launch traced here: 192 us
  waiting for transfers between devices  128 us (66%)
  starting transfers between devices  33.4 us (17%)
  between operations  14.2 us (7%)
  matrix products  8.08 us (4%)
  other arithmetic  5.64 us (3%)
  local copies, waits for them, and re-layouts  2.22 us (1%)
    all_gather x1, waiting for transfers between devices, shards(): piece = lax.all_gather(both_masked, 'dp', axis=2, tiled=True)  98 us
    ppermute x8, starting transfers between devices, from_partner(): return lax.ppermute(block, axis, route)  33.3 us
    ppermute x8, waiting for transfers between devices, from_partner(): return lax.ppermute(block, axis, route)  30.3 us
    dot_general x1, matrix products, shards(): jnp.einsum('rmkh,rmkd->rhd', both_hidden, piece, preferred_element_type=j...  4.11 us
    dot_general x1, matrix products, shards(): jnp.einsum('rmkd,hd->rmkh', piece, own_weight, preferred_element_type=jnp...  3.97 us
  transfers between devices with their start and end apart: 9, of which 9 were waited for; matrix products, arithmetic and copies ran while one was open for 4% of the time, Pallas kernels for 0%

commit v1 on v0

v1 whole, which is shorter than its diff:
```python
import numpy as np

import jax
import jax.numpy as jnp
from jax import lax
from jax.sharding import Mesh
from jax.sharding import PartitionSpec as P

step_rate = 2.0

PIPE = ("py", "pz")
DP = ("dz", "dx", "dc")


def mirror(block):
    count = lax.axis_size(PIPE)
    route = [(low, count - 1 - low) for low in range(count)]
    return lax.ppermute(block, PIPE, route)


def gather_rows(block):
    lead = block.ndim - 2
    out = block
    out = lax.all_gather(out, "dz", axis=0)
    out = lax.all_gather(out, "dx", axis=1)
    out = lax.all_gather(out, "dc", axis=2)
    perm = tuple(range(3, 3 + lead)) + (0, 1, 2, 3 + lead, 4 + lead)
    out = jnp.transpose(out, perm)
    shape = out.shape
    return out.reshape(shape[:lead] + (-1, shape[-1]))


def shards(grad_out, hidden, weights, counts):
    row_total = grad_out.shape[3]
    full_width = grad_out.shape[4]
    scale_factor = float(full_width) ** (-0.5)
    slot_index = lax.broadcasted_iota(jnp.int32, (1, 1, 1, row_total), 3)
    live_rows = slot_index < counts
    masked = jnp.where(live_rows[..., None], grad_out, jnp.zeros_like(grad_out))
    own_weight = weights[0]
    mirror_masked, mirror_hidden = mirror((masked[0, 1], hidden[0, 1]))
    both_masked = jnp.stack([masked[0, 0], mirror_masked], axis=0)
    both_hidden = jnp.stack([hidden[0, 0], mirror_hidden], axis=0)
    piece = gather_rows(both_masked)
    grad_acc = jnp.einsum("rmkd,hd->rmkh", piece, own_weight, preferred_element_type=jnp.float32)
    weight_acc = jnp.einsum(
        "rmkh,rmkd->rhd", both_hidden, piece, preferred_element_type=jnp.float32
    )
    grad_rows = (grad_acc * scale_factor).astype(jnp.bfloat16)
    partial_value = (weight_acc * scale_factor).astype(jnp.bfloat16)
    gradient = partial_value[0].astype(jnp.float32) + partial_value[1].astype(jnp.float32)
    new_weight = (own_weight.astype(jnp.float32) - step_rate * gradient).astype(jnp.bfloat16)
    returned = mirror(grad_rows[1])
    grad_hidden = jnp.stack([grad_rows[0], returned], axis=0)[None]
    return (grad_hidden, new_weight[None])


def solution(mesh):
    n_pipe, n_dp = mesh.devices.shape
    fine = Mesh(mesh.devices.reshape(4, n_pipe // 4, 4, 4, n_dp // 16), PIPE + DP)
    return jax.shard_map(
        shards,
        mesh=fine,
        in_specs=(
            P(PIPE, None, None, DP, None),
            P(PIPE, None, None, None, DP),
            P(PIPE, DP, None),
            P(PIPE, None, None, DP),
        ),
        out_specs=(P(PIPE, None, None, None, DP), P(PIPE, DP, None)),
        check_vma=False,
    )
```

time: 194 us -> 147 us (0.76)
  waiting for transfers between devices: 128 us -> 60.5 us
  blocking collectives: 0 us -> 26.5 us
  local copies, waits for them, and re-layouts: 2.22 us -> 12.5 us
  starting transfers between devices: 33.4 us -> 23.3 us
  matrix products: 8.08 us -> 4.69 us
    all_gather x1 -> x2, waiting for transfers between devices: 98 us -> 57.5 us  [the longest x1 37.9 us: gather_rows(): out = lax.all_gather(out, 'dx', axis=1)]
    ppermute x8 -> x3, waiting for transfers between devices: 30.3 us -> 2.95 us  [mirror(): return lax.ppermute(block, PIPE, route)]
    all_gather x0 -> x1, blocking collectives: none -> 26.5 us  [gather_rows(): out = lax.all_gather(out, 'dz', axis=0)]
    ppermute x8 -> x3, starting transfers between devices: 33.3 us -> 23.2 us  [mirror(): return lax.ppermute(block, PIPE, route)]
    reshape x0 -> x1, local copies, waits for them, and re-layouts: none -> 6.87 us  [gather_rows(): return out.reshape(shape[:lead] + (-1, shape[-1]))]
    transpose x0 -> x1, local copies, waits for them, and re-layouts: none -> 5.58 us  [gather_rows(): out = jnp.transpose(out, perm)]
    dot_general x1, matrix products: 4.11 us -> 1.24 us  [shards(): jnp.einsum('rmkh,rmkd->rhd', both_hidden, piece, preferred_element_type=j...]
  transfers between devices with their start and end apart: 9 -> 5, of which waited for: 9 -> 4; matrix products, arithmetic and copies ran while one was open for 4% -> 13% of each run, Pallas kernels for 0% -> 0%
where the time goes in v1:
time: 147 us; the launch traced here: 146 us
  waiting for transfers between devices  60.5 us (41%)
  blocking collectives  26.5 us (18%)
  starting transfers between devices  23.3 us (16%)
  between operations  14.1 us (10%)
  local copies, waits for them, and re-layouts  12.5 us (9%)
  other arithmetic  4.8 us (3%)
  matrix products  4.69 us (3%)
    all_gather x1, waiting for transfers between devices, gather_rows(): out = lax.all_gather(out, 'dx', axis=1)  37.9 us
    all_gather x1, blocking collectives, gather_rows(): out = lax.all_gather(out, 'dz', axis=0)  26.5 us
    ppermute x3, starting transfers between devices, mirror(): return lax.ppermute(block, PIPE, route)  23.2 us
    all_gather x1, waiting for transfers between devices, gather_rows(): out = lax.all_gather(out, 'dc', axis=2)  19.6 us
    reshape x1, local copies, waits for them, and re-layouts, gather_rows(): return out.reshape(shape[:lead] + (-1, shape[-1]))  6.87 us
    transpose x1, local copies, waits for them, and re-layouts, gather_rows(): out = jnp.transpose(out, perm)  5.58 us
    dot_general x1, matrix products, shards(): jnp.einsum('rmkd,hd->rmkh', piece, own_weight, preferred_element_type=jnp...  3.45 us
    ppermute x3, waiting for transfers between devices, mirror(): return lax.ppermute(block, PIPE, route)  2.95 us
  transfers between devices with their start and end apart: 5, of which 4 were waited for; matrix products, arithmetic and copies ran while one was open for 13% of the time, Pallas kernels for 0%

profile of v1, /device:TPU:1, one launch (start us, length us, event | category | flops | bytes accessed | tf_op | source)
XLA Modules:
  0.0 146.4 jit_solution(12520768031078948741)
XLA Ops:
  7.2 0.0 copy-start.2
  7.2 0.0 all-gather.6.cloned.1.call-start
  7.2 0.8 iota_compare_fusion
  8.0 1.0 broadcast_select_fusion
  9.1 9.5 %collective-permute-start = (bf16[2,4,3584]{2,1,0:T(4,128)(2,1)S(1)}, bf16[2,4,3584]{2,1,0:T(4,128)(2,1)S(1)}, u32[]{:S(2)}, u32[]{:S(2)}) collective-permute-start(bf16[2,4,3584]{2,1,0:T(4,128)(2,1)S(1)} %get-tuple-element.7), channel_id=1, source_target_pairs={{0,480},{32,448},{64,416},{96,384},{128,352},{160,320},{192,288},{... | collective-permute-start | bytes 172040 | tf_op jit(solution)/shard_map/ppermute | solution.py:18
  18.6 1.7 %collective-permute-done = bf16[2,4,3584]{2,1,0:T(4,128)(2,1)S(1)} collective-permute-done((bf16[2,4,3584]{2,1,0:T(4,128)(2,1)S(1)}, bf16[2,4,3584]{2,1,0:T(4,128)(2,1)S(1)}, u32[]{:S(2)}, u32[]{:S(2)}) %collective-permute-start) | collective-permute-done | bytes 57376 | tf_op jit(solution)/shard_map/ppermute | solution.py:18
  20.3 0.1 pad_maximum_fusion
  20.4 26.5 %all-gather = bf16[8,2,4,3584]{3,2,1,0:T(4,128)(2,1)} all-gather(bf16[2,2,4,3584]{3,2,1,0:T(4,128)(2,1)S(1)} %pad_maximum_fusion), channel_id=2, replica_groups=mesh['py'=4,'pz'=4,'dz'=4,'dx'=4,'dc'=2] {'dz'}, dimensions={0}, use_global_device_ids=true | all-gather | bytes 573440 | tf_op jit(solution)/shard_map/all_gather | solution.py:24
  46.9 0.0 all-gather.6.cloned.1.call-update
  46.9 0.0 all-gather.8.cloned.1.call-start
  46.9 37.9 %all-gather.6.cloned.1.call-done = bf16[4,8,2,4,3584]{4,3,2,1,0:T(4,128)(2,1)} async-done(((bf16[4,2,2,4,3584]{4,3,2,1,0:T(4,128)(2,1)}), bf16[4,8,2,4,3584]{4,3,2,1,0:T(4,128)(2,1)}) %all-gather.6.cloned.1.call-update) | async-done | bytes 1835024 | tf_op jit(solution)/shard_map/all_gather | solution.py:25
  84.8 0.0 all-gather.8.cloned.1.call-update
  84.9 0.0 copy-done.2
  84.9 7.3 %collective-permute-start.2 = (bf16[2,128,288]{1,2,0:T(8,128)(2,1)S(1)}, bf16[2,128,288]{1,2,0:T(8,128)(2,1)S(1)}, u32[]{:S(2)}, u32[]{:S(2)}) collective-permute-start(bf16[2,128,288]{1,2,0:T(8,128)(2,1)S(1)} %get-tuple-element.3), channel_id=1, source_target_pairs={{0,480},{32,448},{64,416},{96,384},{128,352},{160,320},{192,288},{... | collective-permute-start | bytes 442376 | tf_op jit(solution)/shard_map/ppermute | solution.py:18
  92.2 19.6 %all-gather.8.cloned.1.call-done = bf16[4,4,4,2,4,3584]{5,4,3,2,1,0:T(4,128)(2,1)} async-done(((bf16[4,4,2,2,4,3584]{5,4,3,2,1,0:T(4,128)(2,1)}), bf16[4,4,4,2,4,3584]{5,4,3,2,1,0:T(4,128)(2,1)}) %all-gather.8.cloned.1.call-update) | async-done | bytes 3670032 | tf_op jit(solution)/shard_map/all_gather | solution.py:26
  111.8 5.6 %copy.7 = bf16[2,2,4,4,2,4,3584]{6,5,4,3,2,1,0:T(4,128)(2,1)} copy(bf16[2,2,4,4,2,4,3584]{6,5,1,0,4,3,2:T(4,128)(2,1)} %bitcast.39) | data formatting | bytes 7340032 | tf_op jit(solution)/shard_map/transpose | solution.py:28
  117.4 0.0 copy-start.1
  117.4 6.9 %reshape.16 = bf16[2,2,128,3584]{3,2,1,0:T(8,128)(2,1)} reshape(bf16[2,2,4,4,2,4,3584]{6,5,4,3,2,1,0:T(4,128)(2,1)} %copy.7) | data formatting | bytes 7340032 | tf_op jit(solution)/shard_map/reshape | solution.py:30
  124.3 0.0 copy-done.1
  124.3 0.0 copy-start
  124.3 3.4 %fusion.6 = bf16[2,2,128,288]{2,3,1,0:T(8,128)(2,1)S(1)} fusion(bf16[2,2,128,3584]{3,2,1,0:T(8,128)(2,1)} %reshape.16, bf16[1,288,3584]{2,1,0:T(8,128)(2,1)S(1)} %copy-done.1), kind=kOutput, calls=%fused_computation.6 | convolution fusion | flops 1057259520 | bytes 6029312 | tf_op jit(solution)/shard_map/rmkd,hd->rmkh/dot_general | solution.py:45
  127.8 6.3 %collective-permute-start.1 = (bf16[2,128,288]{1,2,0:T(8,128)(2,1)S(1)}, bf16[2,128,288]{1,2,0:T(8,128)(2,1)S(1)}, u32[]{:S(2)}, u32[]{:S(2)}) collective-permute-start(bf16[2,128,288]{1,2,0:T(8,128)(2,1)S(1)} %get-tuple-element.5), channel_id=1, source_target_pairs={{0,480},{32,448},{64,416},{96,384},{128,352},{160,320},{192,288},{... | collective-permute-start | bytes 442376 | tf_op jit(solution)/shard_map/ppermute | solution.py:18
  134.1 0.0 collective-permute-done.2
  134.1 0.0 copy-done
  134.1 1.2 fusion
  135.4 2.2 %subtract_convert_fusion = bf16[1,288,3584]{2,1,0:T(8,128)(2,1)} fusion(bf16[1,288,3584]{2,1,0:T(8,128)(2,1)S(1)} %copy-done.1, bf16[2,288,3584]{2,1,0:T(8,128)(2,1)S(1)} %fusion), kind=kLoop, calls=%fused_computation.2 | loop fusion | flops 7225344 | bytes 8257536 | tf_op jit(solution)/shard_map/convert_element_type | solution.py:52
  137.6 1.3 collective-permute-done.1
  138.8 0.7 maximum_bitcast_fusion
  (3 shorter events, 0.1 us)
Async XLA Ops:
  7.2 77.7 %copy-start.2 = (bf16[1,2,2,128,288]{3,4,2,1,0:T(8,128)(2,1)S(1)}, bf16[1,2,2,128,288]{3,4,2,1,0:T(8,128)(2,1)}, u32[]{:S(2)}) copy-start(bf16[1,2,2,128,288]{3,4,2,1,0:T(8,128)(2,1)} %param.5) | copy-start | bytes 884740
  7.2 77.7 %all-gather.6.cloned.1.call-start = ((), (), s32[]{:S(2)}) async-start(), calls=%async_computation | async-start | bytes 2293760 | tf_op jit(solution)/shard_map/all_gather | solution.py:25
  9.1 11.2 %collective-permute-start = (bf16[2,4,3584]{2,1,0:T(4,128)(2,1)S(1)}, bf16[2,4,3584]{2,1,0:T(4,128)(2,1)S(1)}, u32[]{:S(2)}, u32[]{:S(2)}) collective-permute-start(bf16[2,4,3584]{2,1,0:T(4,128)(2,1)S(1)} %get-tuple-element.7), channel_id=1, source_target_pairs={{0,480},{32,448},{64,416},{96,384},{128,352},{160,320},{192,288},{... | collective-permute-start | bytes 172040 | tf_op jit(solution)/shard_map/ppermute | solution.py:18
  46.9 64.9 %all-gather.8.cloned.1.call-start = ((), (), s32[]{:S(2)}) async-start(), calls=%async_computation.1 | async-start | bytes 5505024 | tf_op jit(solution)/shard_map/all_gather | solution.py:26
  84.9 49.2 %collective-permute-start.2 = (bf16[2,128,288]{1,2,0:T(8,128)(2,1)S(1)}, bf16[2,128,288]{1,2,0:T(8,128)(2,1)S(1)}, u32[]{:S(2)}, u32[]{:S(2)}) collective-permute-start(bf16[2,128,288]{1,2,0:T(8,128)(2,1)S(1)} %get-tuple-element.3), channel_id=1, source_target_pairs={{0,480},{32,448},{64,416},{96,384},{128,352},{160,320},{192,288},{... | collective-permute-start | bytes 442376 | tf_op jit(solution)/shard_map/ppermute | solution.py:18
  117.4 6.9 %copy-start.1 = (bf16[1,288,3584]{2,1,0:T(8,128)(2,1)S(1)}, bf16[1,288,3584]{2,1,0:T(8,128)(2,1)}, u32[]{:S(2)}) copy-start(bf16[1,288,3584]{2,1,0:T(8,128)(2,1)} %param.6) | copy-start | bytes 6193156
  124.3 9.9 %copy-start = (bf16[2,2,128,3584]{3,2,1,0:T(8,128)(2,1)S(1)}, bf16[2,2,128,3584]{3,2,1,0:T(8,128)(2,1)}, u32[]{:S(2)}) copy-start(bf16[2,2,128,3584]{3,2,1,0:T(8,128)(2,1)} %reshape.16) | copy-start | bytes 11010052
  127.8 11.1 %collective-permute-start.1 = (bf16[2,128,288]{1,2,0:T(8,128)(2,1)S(1)}, bf16[2,128,288]{1,2,0:T(8,128)(2,1)S(1)}, u32[]{:S(2)}, u32[]{:S(2)}) collective-permute-start(bf16[2,128,288]{1,2,0:T(8,128)(2,1)S(1)} %get-tuple-element.5), channel_id=1, source_target_pairs={{0,480},{32,448},{64,416},{96,384},{128,352},{160,320},{192,288},{... | collective-permute-start | bytes 442376 | tf_op jit(solution)/shard_map/ppermute | solution.py:18
Sparse Core Ops, SparseCore 0:
  47.0 37.7 all-gather.5
  86.9 24.8 all-gather.7

commit v2 on v1

v2 whole, which is shorter than its diff:
```python
import jax
import jax.numpy as jnp
from jax import lax
from jax.sharding import Mesh
from jax.sharding import PartitionSpec as P

step_rate = 2.0

PIPE = ("py", "pz")
DP = ("dz", "dx", "dc")


def mirror(block):
    count = lax.axis_size(PIPE)
    route = [(low, count - 1 - low) for low in range(count)]
    return lax.ppermute(block, PIPE, route)


def gather_rows(block):
    out = lax.all_gather(block, "dz", axis=0)
    out = lax.all_gather(out, "dx", axis=1)
    out = lax.all_gather(out, "dc", axis=2)
    return out.reshape(-1, block.shape[-1])


def one_slot(rows, acts, weight, scale_factor):
    micro, tok, width = rows.shape
    share = acts.shape[-1]
    piece = gather_rows(rows.reshape(micro * tok, width))
    ranks = piece.shape[0] // (micro * tok)
    grad = jnp.dot(piece, weight.T, preferred_element_type=jnp.float32)
    grad = (grad * scale_factor).astype(jnp.bfloat16)
    grad = grad.reshape(ranks, micro, tok, share).transpose(1, 0, 2, 3).reshape(micro, ranks * tok, share)
    acts_rows = acts.reshape(micro, ranks, tok, share).transpose(1, 0, 2, 3).reshape(ranks * micro * tok, share)
    part = jnp.dot(acts_rows.T, piece, preferred_element_type=jnp.float32)
    part = (part * scale_factor).astype(jnp.bfloat16)
    return grad, part


def shards(grad_out, hidden, weights, counts):
    row_total = grad_out.shape[3]
    full_width = grad_out.shape[4]
    scale_factor = float(full_width) ** (-0.5)
    slot_index = lax.broadcasted_iota(jnp.int32, (1, 1, 1, row_total), 3)
    live_rows = slot_index < counts
    masked = jnp.where(live_rows[..., None], grad_out, jnp.zeros_like(grad_out))
    own_weight = weights[0]
    mirror_masked, mirror_hidden = mirror((masked[0, 1], hidden[0, 1]))
    grad_own, part_own = one_slot(masked[0, 0], hidden[0, 0], own_weight, scale_factor)
    grad_mirror, part_mirror = one_slot(mirror_masked, mirror_hidden, own_weight, scale_factor)
    gradient = part_own.astype(jnp.float32) + part_mirror.astype(jnp.float32)
    new_weight = (own_weight.astype(jnp.float32) - step_rate * gradient).astype(jnp.bfloat16)
    returned = mirror(grad_mirror)
    grad_hidden = jnp.stack([grad_own, returned], axis=0)[None]
    return (grad_hidden, new_weight[None])


def solution(mesh):
    n_pipe, n_dp = mesh.devices.shape
    fine = Mesh(mesh.devices.reshape(4, n_pipe // 4, 4, 4, n_dp // 16), PIPE + DP)
    return jax.shard_map(
        shards,
        mesh=fine,
        in_specs=(
            P(PIPE, None, None, DP, None),
            P(PIPE, None, None, None, DP),
            P(PIPE, DP, None),
            P(PIPE, None, None, DP),
        ),
        out_specs=(P(PIPE, None, None, None, DP), P(PIPE, DP, None)),
        check_vma=False,
    )
```

time: 147 us -> 137 us (0.932)
  blocking collectives: 26.5 us -> 66.2 us
  waiting for transfers between devices: 60.5 us -> 24.2 us
  local copies, waits for them, and re-layouts: 12.5 us -> 2.69 us
  starting transfers between devices: 23.3 us -> 18.3 us
  matrix products: 4.69 us -> 8.42 us
  other arithmetic: 4.8 us -> 2.37 us
    all_gather x1 -> x4, blocking collectives: 26.5 us -> 66.2 us  [the longest x2 42.4 us: gather_rows(): out = lax.all_gather(block, 'dz', axis=0)]
    all_gather x1 -> x0, waiting for transfers between devices: 37.9 us -> none  [gather_rows(): out = lax.all_gather(out, 'dx', axis=1)]
    reshape x1 -> x4, local copies, waits for them, and re-layouts: 6.87 us -> 0.3 us  [the longest x2 0.18 us: one_slot(): acts.reshape(micro, ranks, tok, share).transpose(1, 0, 2, 3)]
    ppermute x3, waiting for transfers between devices: 2.95 us -> 9.29 us  [mirror(): return lax.ppermute(block, PIPE, route)]
    transpose x1 -> x4, local copies, waits for them, and re-layouts: 5.58 us -> 0.46 us  [the longest x2 0.31 us: one_slot(): grad.reshape(ranks, micro, tok, share).transpose(1, 0, 2, 3)]
    ppermute x3, starting transfers between devices: 23.2 us -> 18.2 us  [mirror(): return lax.ppermute(block, PIPE, route)]
    all_gather x1 -> x2, waiting for transfers between devices: 19.6 us -> 14.9 us  [gather_rows(): out = lax.all_gather(out, 'dc', axis=2)]
    dot_general x2 -> x4, matrix products: 4.69 us -> 8.42 us  [the longest x2 5.21 us: one_slot(): grad = jnp.dot(piece, weight.T, preferred_element_type=jnp.float32)]
  transfers between devices with their start and end apart: 5 -> 5, of which waited for: 4 -> 4; matrix products, arithmetic and copies ran while one was open for 13% -> 5% of each run, Pallas kernels for 0% -> 0%
where the time goes in v2:
time: 137 us; the launch traced here: 136 us
  blocking collectives  66.2 us (48%)
  waiting for transfers between devices  24.2 us (18%)
  starting transfers between devices  18.3 us (13%)
  between operations  14.3 us (10%)
  matrix products  8.42 us (6%)
  local copies, waits for them, and re-layouts  2.69 us (2%)
  other arithmetic  2.37 us (2%)
    all_gather x2, blocking collectives, gather_rows(): out = lax.all_gather(block, 'dz', axis=0)  42.4 us
    all_gather x2, blocking collectives, gather_rows(): out = lax.all_gather(out, 'dx', axis=1)  23.8 us
    ppermute x3, starting transfers between devices, mirror(): return lax.ppermute(block, PIPE, route)  18.2 us
    all_gather x2, waiting for transfers between devices, gather_rows(): out = lax.all_gather(out, 'dc', axis=2)  14.9 us
    ppermute x3, waiting for transfers between devices, mirror(): return lax.ppermute(block, PIPE, route)  9.29 us
    dot_general x2, matrix products, one_slot(): grad = jnp.dot(piece, weight.T, preferred_element_type=jnp.float32)  5.21 us
    dot_general x2, matrix products, one_slot(): part = jnp.dot(acts_rows.T, piece, preferred_element_type=jnp.float32)  3.21 us
  transfers between devices with their start and end apart: 5, of which 4 were waited for; matrix products, arithmetic and copies ran while one was open for 5% of the time, Pallas kernels for 0%

profile of v2, /device:TPU:1, one launch (start us, length us, event | category | flops | bytes accessed | tf_op | source)
XLA Modules:
  0.0 136.4 jit_solution(6915690259053038759)
XLA Ops:
  7.2 0.8 iota_compare_fusion
  8.0 1.0 broadcast_select_fusion
  9.1 25.2 %all_gather.30 = bf16[4,8,3584]{2,1,0:T(8,128)(2,1)S(1)} all-gather(bf16[1,8,3584]{2,1,0:T(8,128)(2,1)S(1)} %all_gather_reshape_squeeze.3), channel_id=1, replica_groups=mesh['py'=4,'pz'=4,'dz'=4,'dx'=4,'dc'=2] {'dz'}, dimensions={0}, use_global_device_ids=true | all-gather | bytes 286720 | tf_op jit(solution)/shard_map/all_gather | solution.py:20
  34.2 12.4 %all-gather = bf16[4,32,3584]{2,1,0:T(8,128)(2,1)} all-gather(bf16[4,8,3584]{2,1,0:T(8,128)(2,1)S(1)} %all_gather.30), channel_id=2, replica_groups=mesh['py'=4,'pz'=4,'dz'=4,'dx'=4,'dc'=2] {'dx'}, dimensions={1}, use_global_device_ids=true | all-gather | bytes 1146880 | tf_op jit(solution)/shard_map/all_gather | solution.py:21
  46.6 0.0 all-gather.9.cloned.1.call-start
  46.7 6.0 %collective-permute-start = (bf16[2,4,3584]{2,1,0:T(4,128)(2,1)S(1)}, bf16[2,4,3584]{2,1,0:T(4,128)(2,1)S(1)}, u32[]{:S(2)}, u32[]{:S(2)}) collective-permute-start(bf16[2,4,3584]{2,1,0:T(4,128)(2,1)S(1)} %get-tuple-element.9), channel_id=1, source_target_pairs={{0,480},{32,448},{64,416},{96,384},{128,352},{160,320},{192,288},{... | collective-permute-start | bytes 172040 | tf_op jit(solution)/shard_map/ppermute | solution.py:16
  52.7 2.8 %collective-permute-done = bf16[2,4,3584]{2,1,0:T(4,128)(2,1)S(1)} collective-permute-done((bf16[2,4,3584]{2,1,0:T(4,128)(2,1)S(1)}, bf16[2,4,3584]{2,1,0:T(4,128)(2,1)S(1)}, u32[]{:S(2)}, u32[]{:S(2)}) %collective-permute-start) | collective-permute-done | bytes 57376 | tf_op jit(solution)/shard_map/ppermute | solution.py:16
  55.5 17.2 %all_gather.35 = bf16[4,8,3584]{2,1,0:T(8,128)(2,1)S(1)} all-gather(bf16[1,8,3584]{2,1,0:T(8,128)(2,1)S(1)} %all_gather_reshape.3), channel_id=1, replica_groups=mesh['py'=4,'pz'=4,'dz'=4,'dx'=4,'dc'=2] {'dz'}, dimensions={0}, use_global_device_ids=true | all-gather | bytes 286720 | tf_op jit(solution)/shard_map/all_gather | solution.py:20
  72.7 11.5 %all-gather.2 = bf16[4,32,3584]{2,1,0:T(8,128)(2,1)} all-gather(bf16[4,8,3584]{2,1,0:T(8,128)(2,1)S(1)} %all_gather.35), channel_id=4, replica_groups=mesh['py'=4,'pz'=4,'dz'=4,'dx'=4,'dc'=2] {'dx'}, dimensions={1}, use_global_device_ids=true | all-gather | bytes 1146880 | tf_op jit(solution)/shard_map/all_gather | solution.py:21
  84.3 5.6 %collective-permute-start.2 = (bf16[2,128,288]{1,2,0:T(8,128)(2,1)S(1)}, bf16[2,128,288]{1,2,0:T(8,128)(2,1)S(1)}, u32[]{:S(2)}, u32[]{:S(2)}) collective-permute-start(bf16[2,128,288]{1,2,0:T(8,128)(2,1)S(1)} %get-tuple-element.7), channel_id=1, source_target_pairs={{0,480},{32,448},{64,416},{96,384},{128,352},{160,320},{192,288},{... | collective-permute-start | bytes 442376 | tf_op jit(solution)/shard_map/ppermute | solution.py:16
  89.8 0.2 copy.21
  90.0 0.1 copy.22
  90.1 0.1 reshape.42
  90.2 4.0 %collective-permute-done.2 = bf16[2,128,288]{1,2,0:T(8,128)(2,1)S(1)} collective-permute-done((bf16[2,128,288]{1,2,0:T(8,128)(2,1)S(1)}, bf16[2,128,288]{1,2,0:T(8,128)(2,1)S(1)}, u32[]{:S(2)}, u32[]{:S(2)}) %collective-permute-start.2) | collective-permute-done | bytes 147488 | tf_op jit(solution)/shard_map/ppermute | solution.py:16
  94.2 0.2 copy.23
  94.4 0.1 copy.24
  94.5 0.1 reshape.44
  94.6 2.2 %fusion.23 = bf16[256,288]{0,1:T(8,128)(2,1)S(1)} fusion(bf16[256,3584]{1,0:T(8,128)(2,1)} %bitcast.56, bf16[1,288,3584]{2,1,0:T(8,128)(2,1)S(1)} %copy-done.1), kind=kOutput, calls=%fused_computation.19 | convolution fusion | flops 528629760 | bytes 4046848 | tf_op jit(solution)/shard_map/dot_general | solution.py:31
  96.8 0.2 copy.17
  97.0 0.1 reshape.38
  97.1 0.2 copy.18
  97.2 14.8 %all-gather.9.cloned.1.call-done = bf16[4,4,16,3584]{3,2,1,0:T(8,128)(2,1)} async-done(((bf16[4,4,8,3584]{3,2,1,0:T(8,128)(2,1)}), bf16[4,4,16,3584]{3,2,1,0:T(8,128)(2,1)}) %all-gather.9.cloned.1.call-update) | async-done | bytes 1835024 | tf_op jit(solution)/shard_map/all_gather | solution.py:22
  112.1 3.0 %fusion.20 = bf16[256,288]{0,1:T(8,128)(2,1)S(1)} fusion(bf16[256,3584]{1,0:T(8,128)(2,1)} %bitcast.52, bf16[1,288,3584]{2,1,0:T(8,128)(2,1)} %param.6), kind=kOutput, calls=%fused_computation.18 | convolution fusion | flops 528629760 | bytes 4046848 | tf_op jit(solution)/shard_map/dot_general | solution.py:31
  115.1 0.2 copy.19
  115.2 0.1 reshape.40
  115.3 0.2 copy.20
  115.5 6.6 %collective-permute-start.1 = (bf16[2,128,288]{2,0,1:T(2,128)(2,1)S(1)}, bf16[2,128,288]{2,0,1:T(2,128)(2,1)S(1)}, u32[]{:S(2)}, u32[]{:S(2)}) collective-permute-start(bf16[2,128,288]{2,0,1:T(2,128)(2,1)S(1)} %bitcast.63), channel_id=1, source_target_pairs={{0,480},{32,448},{64,416},{96,384},{128,352},{160,320},{192,288},{... | collective-permute-start | bytes 442376 | tf_op jit(solution)/shard_map/ppermute | solution.py:16
  122.1 0.7 fusion.8
  122.9 2.5 %fusion.9 = bf16[1,288,3584]{2,1,0:T(8,128)(2,1)} fusion(f32[3584,288]{0,1:T(8,128)S(1)} %fusion.8, bf16[256,3584]{1,0:T(8,128)(2,1)S(1)} %bitcast.57, bf16[256,288]{1,0:T(8,128)(2,1)S(1)} %reshape.42, bf16[1,288,3584]{2,1,0:T(8,128)(2,1)S(1)} %copy-done.2), kind=kOutput, calls=%fused_computation.11 | convolution fusion | flops 536739840 | bytes 10240000 | tf_op jit(solution)/shard_map/dot_general | solution.py:35
  125.3 2.5 %collective-permute-done.1 = bf16[2,128,288]{2,0,1:T(2,128)(2,1)S(1)} collective-permute-done((bf16[2,128,288]{2,0,1:T(2,128)(2,1)S(1)}, bf16[2,128,288]{2,0,1:T(2,128)(2,1)S(1)}, u32[]{:S(2)}, u32[]{:S(2)}) %collective-permute-start.1) | collective-permute-done | bytes 147488 | tf_op jit(solution)/shard_map/ppermute | solution.py:16
  127.9 0.6 maximum_bitcast_fusion
  128.5 1.1 copy.25
  (18 shorter events, 0.2 us)
Async XLA Ops:
  7.2 87.4 %all-gather.7.cloned.1.call-start = ((), (), s32[]{:S(2)}) async-start(), calls=%async_computation | async-start | bytes 2752512 | tf_op jit(solution)/shard_map/all_gather | solution.py:22
  34.2 50.0 %copy-start.4 = (bf16[1,2,2,128,288]{3,4,2,1,0:T(8,128)(2,1)S(1)}, bf16[1,2,2,128,288]{3,4,2,1,0:T(8,128)(2,1)}, u32[]{:S(2)}) copy-start(bf16[1,2,2,128,288]{3,4,2,1,0:T(8,128)(2,1)} %param.5) | copy-start | bytes 884740
  46.6 65.4 %all-gather.9.cloned.1.call-start = ((), (), s32[]{:S(2)}) async-start(), calls=%async_computation.1 | async-start | bytes 2752512 | tf_op jit(solution)/shard_map/all_gather | solution.py:22
  46.7 8.8 %collective-permute-start = (bf16[2,4,3584]{2,1,0:T(4,128)(2,1)S(1)}, bf16[2,4,3584]{2,1,0:T(4,128)(2,1)S(1)}, u32[]{:S(2)}, u32[]{:S(2)}) collective-permute-start(bf16[2,4,3584]{2,1,0:T(4,128)(2,1)S(1)} %get-tuple-element.9), channel_id=1, source_target_pairs={{0,480},{32,448},{64,416},{96,384},{128,352},{160,320},{192,288},{... | collective-permute-start | bytes 172040 | tf_op jit(solution)/shard_map/ppermute | solution.py:16
  84.2 10.4 %copy-start.1 = (bf16[1,288,3584]{2,1,0:T(8,128)(2,1)S(1)}, bf16[1,288,3584]{2,1,0:T(8,128)(2,1)}, u32[]{:S(2)}) copy-start(bf16[1,288,3584]{2,1,0:T(8,128)(2,1)} %param.6) | copy-start | bytes 6193156
  84.3 9.9 %collective-permute-start.2 = (bf16[2,128,288]{1,2,0:T(8,128)(2,1)S(1)}, bf16[2,128,288]{1,2,0:T(8,128)(2,1)S(1)}, u32[]{:S(2)}, u32[]{:S(2)}) collective-permute-start(bf16[2,128,288]{1,2,0:T(8,128)(2,1)S(1)} %get-tuple-element.7), channel_id=1, source_target_pairs={{0,480},{32,448},{64,416},{96,384},{128,352},{160,320},{192,288},{... | collective-permute-start | bytes 442376 | tf_op jit(solution)/shard_map/ppermute | solution.py:16
  112.1 10.0 %copy-start = (bf16[4,4,16,3584]{3,2,1,0:T(8,128)(2,1)S(1)}, bf16[4,4,16,3584]{3,2,1,0:T(8,128)(2,1)}, u32[]{:S(2)}) copy-start(bf16[4,4,16,3584]{3,2,1,0:T(8,128)(2,1)} %all-gather.9.cloned.1.call-done) | copy-start | bytes 5505028
  115.5 7.4 %copy-start.2 = (bf16[1,288,3584]{2,1,0:T(8,128)(2,1)S(1)}, bf16[1,288,3584]{2,1,0:T(8,128)(2,1)}, u32[]{:S(2)}) copy-start(bf16[1,288,3584]{2,1,0:T(8,128)(2,1)} %param.6) | copy-start | bytes 6193156
  115.5 7.4 %copy-start.3 = (bf16[4,4,16,3584]{3,2,1,0:T(8,128)(2,1)S(1)}, bf16[4,4,16,3584]{3,2,1,0:T(8,128)(2,1)}, u32[]{:S(2)}) copy-start(bf16[4,4,16,3584]{3,2,1,0:T(8,128)(2,1)} %all-gather.7.cloned.1.call-done) | copy-start | bytes 5505028
  115.5 12.4 %collective-permute-start.1 = (bf16[2,128,288]{2,0,1:T(2,128)(2,1)S(1)}, bf16[2,128,288]{2,0,1:T(2,128)(2,1)S(1)}, u32[]{:S(2)}, u32[]{:S(2)}) collective-permute-start(bf16[2,128,288]{2,0,1:T(2,128)(2,1)S(1)} %bitcast.63), channel_id=1, source_target_pairs={{0,480},{32,448},{64,416},{96,384},{128,352},{160,320},{192,288},{... | collective-permute-start | bytes 442376 | tf_op jit(solution)/shard_map/ppermute | solution.py:16
Sparse Core Ops, SparseCore 0:
  46.7 22.5 all-gather.6
  84.3 27.6 all-gather.8

commit v3 on v2

v3 whole, which is shorter than its diff:
```python
import jax
import jax.numpy as jnp
from jax import lax
from jax.sharding import Mesh
from jax.sharding import PartitionSpec as P

step_rate = 2.0

PIPE = ("py", "pz")
DP = ("dz", "dx", "dc")


def mirror(block):
    count = lax.axis_size(PIPE)
    route = [(low, count - 1 - low) for low in range(count)]
    return lax.ppermute(block, PIPE, route)


def gather_rows(block):
    out = lax.all_gather(block, "dz", axis=0)
    out = lax.all_gather(out, "dx", axis=1)
    out = lax.all_gather(out, "dc", axis=2)
    return out.reshape(-1, block.shape[-1])


def shards(grad_out, hidden, weights, counts):
    row_total = grad_out.shape[3]
    full_width = grad_out.shape[4]
    micro = grad_out.shape[2]
    tokens = hidden.shape[3]
    share = hidden.shape[4]
    scale_factor = float(full_width) ** (-0.5)
    slot_index = lax.broadcasted_iota(jnp.int32, (1, 1, 1, row_total), 3)
    live_rows = slot_index < counts
    masked = jnp.where(live_rows[..., None], grad_out, jnp.zeros_like(grad_out))
    own_weight = weights[0]
    mirror_masked, mirror_hidden = mirror((masked[0, 1], hidden[0, 1]))
    both_masked = jnp.stack([masked[0, 0], mirror_masked], axis=0)
    both_hidden = jnp.stack([hidden[0, 0], mirror_hidden], axis=0)
    piece = gather_rows(both_masked.reshape(-1, full_width))
    ranks = tokens // row_total
    acts = both_hidden.reshape(2, micro, ranks, row_total, share).transpose(2, 0, 1, 3, 4).reshape(-1, share)
    grad = jnp.dot(piece, own_weight.T, preferred_element_type=jnp.float32)
    grad = (grad * scale_factor).astype(jnp.bfloat16)
    grad = grad.reshape(ranks, 2, micro, row_total, share).transpose(1, 2, 0, 3, 4).reshape(2, micro, tokens, share)
    total = jnp.dot(acts.T, piece, preferred_element_type=jnp.float32)
    gradient = total * scale_factor
    new_weight = (own_weight.astype(jnp.float32) - step_rate * gradient).astype(jnp.bfloat16)
    returned = mirror(grad[1])
    grad_hidden = jnp.stack([grad[0], returned], axis=0)[None]
    return (grad_hidden, new_weight[None])


def solution(mesh):
    n_pipe, n_dp = mesh.devices.shape
    fine = Mesh(mesh.devices.reshape(4, n_pipe // 4, 4, 4, n_dp // 16), PIPE + DP)
    return jax.shard_map(
        shards,
        mesh=fine,
        in_specs=(
            P(PIPE, None, None, DP, None),
            P(PIPE, None, None, None, DP),
            P(PIPE, DP, None),
            P(PIPE, None, None, DP),
        ),
        out_specs=(P(PIPE, None, None, None, DP), P(PIPE, DP, None)),
        check_vma=False,
    )
```

time: 137 us -> 137 us (level)
  blocking collectives: 66.2 us -> 26.5 us
  waiting for transfers between devices: 24.2 us -> 58.8 us
  starting transfers between devices: 18.3 us -> 23.3 us
    all_gather x0 -> x1, waiting for transfers between devices: none -> 37.9 us  [gather_rows(): out = lax.all_gather(out, 'dx', axis=1)]
    all_gather x2 -> x0, blocking collectives: 23.8 us -> none  [gather_rows(): out = lax.all_gather(out, 'dx', axis=1)]
    all_gather x2 -> x1, blocking collectives: 42.4 us -> 26.5 us  [gather_rows(): out = lax.all_gather(block, 'dz', axis=0)]
    ppermute x3, starting transfers between devices: 18.2 us -> 23.2 us  [mirror(): return lax.ppermute(block, PIPE, route)]
    ppermute x3, waiting for transfers between devices: 9.29 us -> 5.86 us  [mirror(): return lax.ppermute(block, PIPE, route)]
    dot_general x4 -> x2, matrix products: 8.42 us -> 7.94 us  [the longest x1 4.64 us: shards(): total = jnp.dot(acts.T, piece, preferred_element_type=jnp.float32)]
    all_gather x2 -> x1, waiting for transfers between devices: 14.9 us -> 15 us  [gather_rows(): out = lax.all_gather(out, 'dc', axis=2)]
  transfers between devices with their start and end apart: 5 -> 5, of which waited for: 4 -> 5; matrix products, arithmetic and copies ran while one was open for 5% -> 5% of each run, Pallas kernels for 0% -> 0%
where the time goes in v3:
time: 137 us
  waiting for transfers between devices  58.8 us (43%)
  blocking collectives  26.5 us (19%)
  starting transfers between devices  23.3 us (17%)
  between operations  14.2 us (10%)
  matrix products  7.94 us (6%)
  other arithmetic  3.24 us (2%)
  local copies, waits for them, and re-layouts  2.7 us (2%)
    all_gather x1, waiting for transfers between devices, gather_rows(): out = lax.all_gather(out, 'dx', axis=1)  37.9 us
    all_gather x1, blocking collectives, gather_rows(): out = lax.all_gather(block, 'dz', axis=0)  26.5 us
    ppermute x3, starting transfers between devices, mirror(): return lax.ppermute(block, PIPE, route)  23.2 us
    all_gather x1, waiting for transfers between devices, gather_rows(): out = lax.all_gather(out, 'dc', axis=2)  15 us
    ppermute x3, waiting for transfers between devices, mirror(): return lax.ppermute(block, PIPE, route)  5.86 us
    dot_general x1, matrix products, shards(): total = jnp.dot(acts.T, piece, preferred_element_type=jnp.float32)  4.64 us
    dot_general x1, matrix products, shards(): grad = jnp.dot(piece, own_weight.T, preferred_element_type=jnp.float32)  3.3 us
  transfers between devices with their start and end apart: 5, of which 5 were waited for; matrix products, arithmetic and copies ran while one was open for 5% of the time, Pallas kernels for 0%

profile of v3, /device:TPU:1, one launch (start us, length us, event | category | flops | bytes accessed | tf_op | source)
XLA Modules:
  0.0 136.6 jit_solution(12191642454586928486)
XLA Ops:
  7.2 0.0 copy-start.1
  7.2 0.0 all-gather.5.cloned.1.call-start
  7.2 0.8 iota_compare_fusion
  8.0 1.2 broadcast_select_fusion
  9.2 9.5 %collective-permute-start = (bf16[2,4,3584]{2,1,0:T(4,128)(2,1)S(1)}, bf16[2,4,3584]{2,1,0:T(4,128)(2,1)S(1)}, u32[]{:S(2)}, u32[]{:S(2)}) collective-permute-start(bf16[2,4,3584]{2,1,0:T(4,128)(2,1)S(1)} %get-tuple-element.11), channel_id=1, source_target_pairs={{0,480},{32,448},{64,416},{96,384},{128,352},{160,320},{192,288},{... | collective-permute-start | bytes 172040 | tf_op jit(solution)/shard_map/ppermute | solution.py:16
  18.8 1.7 %collective-permute-done = bf16[2,4,3584]{2,1,0:T(4,128)(2,1)S(1)} collective-permute-done((bf16[2,4,3584]{2,1,0:T(4,128)(2,1)S(1)}, bf16[2,4,3584]{2,1,0:T(4,128)(2,1)S(1)}, u32[]{:S(2)}, u32[]{:S(2)}) %collective-permute-start) | collective-permute-done | bytes 57376 | tf_op jit(solution)/shard_map/ppermute | solution.py:16
  20.4 0.1 pad_maximum_fusion
  20.5 26.5 %all_gather.15 = bf16[4,16,3584]{2,1,0:T(8,128)(2,1)} all-gather(bf16[1,16,3584]{2,1,0:T(8,128)(2,1)S(1)} %all_gather_reshape.3), channel_id=1, replica_groups=mesh['py'=4,'pz'=4,'dz'=4,'dx'=4,'dc'=2] {'dz'}, dimensions={0}, use_global_device_ids=true | all-gather | bytes 573440 | tf_op jit(solution)/shard_map/all_gather | solution.py:20
  47.0 0.0 all-gather.5.cloned.1.call-update
  47.1 0.0 all-gather.7.cloned.1.call-start
  47.1 37.9 %all-gather.5.cloned.1.call-done = bf16[4,64,3584]{2,1,0:T(8,128)(2,1)} async-done(((bf16[4,16,3584]{2,1,0:T(8,128)(2,1)}), bf16[4,64,3584]{2,1,0:T(8,128)(2,1)}) %all-gather.5.cloned.1.call-update) | async-done | bytes 1835024 | tf_op jit(solution)/shard_map/all_gather | solution.py:21
  85.0 0.0 all-gather.7.cloned.1.call-update
  85.1 7.3 %collective-permute-start.2 = (bf16[2,128,288]{1,2,0:T(8,128)(2,1)S(1)}, bf16[2,128,288]{1,2,0:T(8,128)(2,1)S(1)}, u32[]{:S(2)}, u32[]{:S(2)}) collective-permute-start(bf16[2,128,288]{1,2,0:T(8,128)(2,1)S(1)} %get-tuple-element.9), channel_id=1, source_target_pairs={{0,480},{32,448},{64,416},{96,384},{128,352},{160,320},{192,288},{... | collective-permute-start | bytes 442376 | tf_op jit(solution)/shard_map/ppermute | solution.py:16
  92.4 0.2 copy.18
  92.6 3.2 %collective-permute-done.2 = bf16[2,128,288]{1,2,0:T(8,128)(2,1)S(1)} collective-permute-done((bf16[2,128,288]{1,2,0:T(8,128)(2,1)S(1)}, bf16[2,128,288]{1,2,0:T(8,128)(2,1)S(1)}, u32[]{:S(2)}, u32[]{:S(2)}) %collective-permute-start.2) | collective-permute-done | bytes 147488 | tf_op jit(solution)/shard_map/ppermute | solution.py:16
  95.8 0.2 copy.19
  96.0 0.6 maximum_bitcast_fusion.1
  96.7 0.2 copy.20
  96.8 0.2 reshape.33
  97.0 15.0 %all-gather.7.cloned.1.call-done = bf16[4,4,32,3584]{3,2,1,0:T(8,128)(2,1)} async-done(((bf16[4,4,16,3584]{3,2,1,0:T(8,128)(2,1)}), bf16[4,4,32,3584]{3,2,1,0:T(8,128)(2,1)}) %all-gather.7.cloned.1.call-update) | async-done | bytes 3670032 | tf_op jit(solution)/shard_map/all_gather | solution.py:22
  112.0 0.0 copy-done
  112.0 3.3 %fusion.8 = bf16[512,288]{0,1:T(8,128)(2,1)S(1)} fusion(bf16[512,3584]{1,0:T(8,128)(2,1)} %bitcast.33, bf16[1,288,3584]{2,1,0:T(8,128)(2,1)S(1)} %copy-done), kind=kOutput, calls=%fused_computation.7 | convolution fusion | flops 1057259520 | bytes 6029312 | tf_op jit(solution)/shard_map/dot_general | solution.py:43
  115.3 0.2 copy.15
  115.5 0.1 reshape.32
  115.6 0.1 fusion.11
  115.8 0.2 copy.17
  116.0 6.3 %collective-permute-start.1 = (bf16[2,128,288]{2,0,1:T(2,128)(2,1)S(1)}, bf16[2,128,288]{2,0,1:T(2,128)(2,1)S(1)}, u32[]{:S(2)}, u32[]{:S(2)}) collective-permute-start(bf16[2,128,288]{2,0,1:T(2,128)(2,1)S(1)} %bitcast.40), channel_id=1, source_target_pairs={{0,480},{32,448},{64,416},{96,384},{128,352},{160,320},{192,288},{... | collective-permute-start | bytes 442376 | tf_op jit(solution)/shard_map/ppermute | solution.py:16
  122.3 4.6 %fusion.2 = bf16[1,288,3584]{2,1,0:T(8,128)(2,1)} fusion(bf16[512,288]{1,0:T(8,128)(2,1)S(1)} %reshape.33, bf16[512,3584]{1,0:T(8,128)(2,1)} %bitcast.34, bf16[1,288,3584]{2,1,0:T(8,128)(2,1)S(1)} %copy-done), kind=kOutput, calls=%fused_computation.3 | convolution fusion | flops 1061093376 | bytes 8093696 | tf_op jit(solution)/shard_map/dot_general | solution.py:46
  126.9 0.2 copy.16
  127.1 1.0 collective-permute-done.1
  128.1 0.6 maximum_bitcast_fusion
  128.7 1.1 copy.21
  (5 shorter events, 0.1 us)
Async XLA Ops:
  7.2 77.9 %copy-start.1 = (bf16[1,2,2,128,288]{3,4,2,1,0:T(8,128)(2,1)S(1)}, bf16[1,2,2,128,288]{3,4,2,1,0:T(8,128)(2,1)}, u32[]{:S(2)}) copy-start(bf16[1,2,2,128,288]{3,4,2,1,0:T(8,128)(2,1)} %param.5) | copy-start | bytes 884740
  7.2 77.8 %all-gather.5.cloned.1.call-start = ((), (), s32[]{:S(2)}) async-start(), calls=%async_computation | async-start | bytes 2293760 | tf_op jit(solution)/shard_map/all_gather | solution.py:21
  8.0 104.0 %copy-start = (bf16[1,288,3584]{2,1,0:T(8,128)(2,1)S(1)}, bf16[1,288,3584]{2,1,0:T(8,128)(2,1)}, u32[]{:S(2)}) copy-start(bf16[1,288,3584]{2,1,0:T(8,128)(2,1)} %param.6) | copy-start | bytes 6193156
  9.2 11.2 %collective-permute-start = (bf16[2,4,3584]{2,1,0:T(4,128)(2,1)S(1)}, bf16[2,4,3584]{2,1,0:T(4,128)(2,1)S(1)}, u32[]{:S(2)}, u32[]{:S(2)}) collective-permute-start(bf16[2,4,3584]{2,1,0:T(4,128)(2,1)S(1)} %get-tuple-element.11), channel_id=1, source_target_pairs={{0,480},{32,448},{64,416},{96,384},{128,352},{160,320},{192,288},{... | collective-permute-start | bytes 172040 | tf_op jit(solution)/shard_map/ppermute | solution.py:16
  47.1 64.9 %all-gather.7.cloned.1.call-start = ((), (), s32[]{:S(2)}) async-start(), calls=%async_computation.1 | async-start | bytes 5505024 | tf_op jit(solution)/shard_map/all_gather | solution.py:22
  85.1 10.8 %collective-permute-start.2 = (bf16[2,128,288]{1,2,0:T(8,128)(2,1)S(1)}, bf16[2,128,288]{1,2,0:T(8,128)(2,1)S(1)}, u32[]{:S(2)}, u32[]{:S(2)}) collective-permute-start(bf16[2,128,288]{1,2,0:T(8,128)(2,1)S(1)} %get-tuple-element.9), channel_id=1, source_target_pairs={{0,480},{32,448},{64,416},{96,384},{128,352},{160,320},{192,288},{... | collective-permute-start | bytes 442376 | tf_op jit(solution)/shard_map/ppermute | solution.py:16
  116.0 12.1 %collective-permute-start.1 = (bf16[2,128,288]{2,0,1:T(2,128)(2,1)S(1)}, bf16[2,128,288]{2,0,1:T(2,128)(2,1)S(1)}, u32[]{:S(2)}, u32[]{:S(2)}) collective-permute-start(bf16[2,128,288]{2,0,1:T(2,128)(2,1)S(1)} %bitcast.40), channel_id=1, source_target_pairs={{0,480},{32,448},{64,416},{96,384},{128,352},{160,320},{192,288},{... | collective-permute-start | bytes 442376 | tf_op jit(solution)/shard_map/ppermute | solution.py:16
Sparse Core Ops, SparseCore 0:
  47.2 37.7 all-gather.4
  87.1 24.8 all-gather.6

commit v4 on v3

--- a/solution.py
+++ b/solution.py
@@ -18,8 +18,7 @@
 
 def gather_rows(block):
     out = lax.all_gather(block, "dz", axis=0)
-    out = lax.all_gather(out, "dx", axis=1)
-    out = lax.all_gather(out, "dc", axis=2)
+    out = lax.all_gather(out, ("dx", "dc"), axis=1)
     return out.reshape(-1, block.shape[-1])
 
 

time: 137 us -> 113 us (0.82)
  waiting for transfers between devices: 58.8 us -> 33 us
    all_gather x2 -> x1, waiting for transfers between devices: 52.9 us -> 27.6 us  [gather_rows(): out = lax.all_gather(out, ('dx', 'dc'), axis=1)]
  transfers between devices with their start and end apart: 5 -> 4, of which waited for: 5 -> 4; matrix products, arithmetic and copies ran while one was open for 5% -> 6% of each run, Pallas kernels for 0% -> 0%
where the time goes in v4:
time: 113 us; the launch traced here: 111 us
  waiting for transfers between devices  33 us (29%)
  blocking collectives  26.5 us (23%)
  starting transfers between devices  22.9 us (20%)
  between operations  14.2 us (13%)
  matrix products  7.93 us (7%)
  local copies, waits for them, and re-layouts  3.68 us (3%)
  other arithmetic  3.2 us (3%)
    all_gather x1, waiting for transfers between devices, gather_rows(): out = lax.all_gather(out, ('dx', 'dc'), axis=1)  27.6 us
    all_gather x1, blocking collectives, gather_rows(): out = lax.all_gather(block, 'dz', axis=0)  26.5 us
    ppermute x3, starting transfers between devices, mirror(): return lax.ppermute(block, PIPE, route)  22.8 us
    ppermute x3, waiting for transfers between devices, mirror(): return lax.ppermute(block, PIPE, route)  5.38 us
    dot_general x1, matrix products, shards(): total = jnp.dot(acts.T, piece, preferred_element_type=jnp.float32)  4.64 us
    dot_general x1, matrix products, shards(): grad = jnp.dot(piece, own_weight.T, preferred_element_type=jnp.float32)  3.3 us
  transfers between devices with their start and end apart: 4, of which 4 were waited for; matrix products, arithmetic and copies ran while one was open for 6% of the time, Pallas kernels for 0%

profile of v4, /device:TPU:1, one launch (start us, length us, event | category | flops | bytes accessed | tf_op | source)
XLA Modules:
  0.0 111.4 jit_solution(13993921279849907162)
XLA Ops:
  7.2 0.0 copy-start
  7.2 0.0 all-gather.3.cloned.1.call-start
  7.2 0.9 iota_compare_fusion
  8.1 1.0 broadcast_select_fusion
  9.2 9.5 %collective-permute-start = (bf16[2,4,3584]{2,1,0:T(4,128)(2,1)S(1)}, bf16[2,4,3584]{2,1,0:T(4,128)(2,1)S(1)}, u32[]{:S(2)}, u32[]{:S(2)}) collective-permute-start(bf16[2,4,3584]{2,1,0:T(4,128)(2,1)S(1)} %get-tuple-element.11), channel_id=1, source_target_pairs={{0,480},{32,448},{64,416},{96,384},{128,352},{160,320},{192,288},{... | collective-permute-start | bytes 172040 | tf_op jit(solution)/shard_map/ppermute | solution.py:16
  18.7 1.7 %collective-permute-done = bf16[2,4,3584]{2,1,0:T(4,128)(2,1)S(1)} collective-permute-done((bf16[2,4,3584]{2,1,0:T(4,128)(2,1)S(1)}, bf16[2,4,3584]{2,1,0:T(4,128)(2,1)S(1)}, u32[]{:S(2)}, u32[]{:S(2)}) %collective-permute-start) | collective-permute-done | bytes 57376 | tf_op jit(solution)/shard_map/ppermute | solution.py:16
  20.4 0.1 pad_maximum_fusion
  20.5 26.5 %all_gather.9 = bf16[4,16,3584]{2,1,0:T(8,128)(2,1)} all-gather(bf16[1,16,3584]{2,1,0:T(8,128)(2,1)S(1)} %all_gather_reshape.3), channel_id=1, replica_groups=mesh['py'=4,'pz'=4,'dz'=4,'dx'=4,'dc'=2] {'dz'}, dimensions={0}, use_global_device_ids=true | all-gather | bytes 573440 | tf_op jit(solution)/shard_map/all_gather | solution.py:20
  47.0 0.0 all-gather.3.cloned.1.call-update
  47.0 1.0 fusion.12
  48.0 6.0 %collective-permute-start.2 = (bf16[2,128,288]{1,2,0:T(8,128)(2,1)S(1)}, bf16[2,128,288]{1,2,0:T(8,128)(2,1)S(1)}, u32[]{:S(2)}, u32[]{:S(2)}) collective-permute-start(bf16[2,128,288]{1,2,0:T(8,128)(2,1)S(1)} %get-tuple-element.9), channel_id=1, source_target_pairs={{0,480},{32,448},{64,416},{96,384},{128,352},{160,320},{192,288},{... | collective-permute-start | bytes 442376 | tf_op jit(solution)/shard_map/ppermute | solution.py:16
  54.0 0.2 copy.18
  54.2 3.6 %collective-permute-done.2 = bf16[2,128,288]{1,2,0:T(8,128)(2,1)S(1)} collective-permute-done((bf16[2,128,288]{1,2,0:T(8,128)(2,1)S(1)}, bf16[2,128,288]{1,2,0:T(8,128)(2,1)S(1)}, u32[]{:S(2)}, u32[]{:S(2)}) %collective-permute-start.2) | collective-permute-done | bytes 147488 | tf_op jit(solution)/shard_map/ppermute | solution.py:16
  57.8 0.2 copy.19
  58.0 0.6 maximum_bitcast_fusion.1
  58.6 0.2 copy.20
  58.8 0.2 reshape.33
  59.0 27.6 %all-gather.3.cloned.1.call-done = bf16[4,128,3584]{2,1,0:T(8,128)(2,1)} async-done(((bf16[4,16,3584]{2,1,0:T(8,128)(2,1)}), bf16[4,128,3584]{2,1,0:T(8,128)(2,1)}) %all-gather.3.cloned.1.call-update) | async-done | bytes 3670032 | tf_op jit(solution)/shard_map/all_gather | solution.py:21
  86.6 0.0 copy-done
  86.6 3.3 %fusion.8 = bf16[512,288]{0,1:T(8,128)(2,1)S(1)} fusion(bf16[512,3584]{1,0:T(8,128)(2,1)} %bitcast.32, bf16[1,288,3584]{2,1,0:T(8,128)(2,1)S(1)} %copy-done), kind=kOutput, calls=%fused_computation.7 | convolution fusion | flops 1057259520 | bytes 6029312 | tf_op jit(solution)/shard_map/dot_general | solution.py:42
  89.9 0.2 copy.15
  90.2 0.1 reshape.32
  90.3 0.1 fusion.11
  90.4 0.2 copy.17
  90.6 7.3 %collective-permute-start.1 = (bf16[2,128,288]{2,0,1:T(2,128)(2,1)S(1)}, bf16[2,128,288]{2,0,1:T(2,128)(2,1)S(1)}, u32[]{:S(2)}, u32[]{:S(2)}) collective-permute-start(bf16[2,128,288]{2,0,1:T(2,128)(2,1)S(1)} %bitcast.38), channel_id=1, source_target_pairs={{0,480},{32,448},{64,416},{96,384},{128,352},{160,320},{192,288},{... | collective-permute-start | bytes 442376 | tf_op jit(solution)/shard_map/ppermute | solution.py:16
  97.9 4.6 %fusion.2 = bf16[1,288,3584]{2,1,0:T(8,128)(2,1)} fusion(bf16[512,288]{1,0:T(8,128)(2,1)S(1)} %reshape.33, bf16[512,3584]{1,0:T(8,128)(2,1)} %bitcast.33, bf16[1,288,3584]{2,1,0:T(8,128)(2,1)S(1)} %copy-done), kind=kOutput, calls=%fused_computation.3 | convolution fusion | flops 1061093376 | bytes 8093696 | tf_op jit(solution)/shard_map/dot_general | solution.py:45
  102.6 0.2 copy.16
  102.7 0.1 collective-permute-done.1
  102.8 0.6 maximum_bitcast_fusion
  103.4 1.1 copy.21
  (2 shorter events, 0.1 us)
Async XLA Ops:
  7.2 79.5 %copy-start = (bf16[1,288,3584]{2,1,0:T(8,128)(2,1)S(1)}, bf16[1,288,3584]{2,1,0:T(8,128)(2,1)}, u32[]{:S(2)}) copy-start(bf16[1,288,3584]{2,1,0:T(8,128)(2,1)} %param.6) | copy-start | bytes 6193156
  7.2 79.5 %all-gather.3.cloned.1.call-start = ((), (), s32[]{:S(2)}) async-start(), calls=%async_computation | async-start | bytes 4128768 | tf_op jit(solution)/shard_map/all_gather | solution.py:21
  9.2 11.2 %collective-permute-start = (bf16[2,4,3584]{2,1,0:T(4,128)(2,1)S(1)}, bf16[2,4,3584]{2,1,0:T(4,128)(2,1)S(1)}, u32[]{:S(2)}, u32[]{:S(2)}) collective-permute-start(bf16[2,4,3584]{2,1,0:T(4,128)(2,1)S(1)} %get-tuple-element.11), channel_id=1, source_target_pairs={{0,480},{32,448},{64,416},{96,384},{128,352},{160,320},{192,288},{... | collective-permute-start | bytes 172040 | tf_op jit(solution)/shard_map/ppermute | solution.py:16
  48.0 9.8 %collective-permute-start.2 = (bf16[2,128,288]{1,2,0:T(8,128)(2,1)S(1)}, bf16[2,128,288]{1,2,0:T(8,128)(2,1)S(1)}, u32[]{:S(2)}, u32[]{:S(2)}) collective-permute-start(bf16[2,128,288]{1,2,0:T(8,128)(2,1)S(1)} %get-tuple-element.9), channel_id=1, source_target_pairs={{0,480},{32,448},{64,416},{96,384},{128,352},{160,320},{192,288},{... | collective-permute-start | bytes 442376 | tf_op jit(solution)/shard_map/ppermute | solution.py:16
  90.6 12.2 %collective-permute-start.1 = (bf16[2,128,288]{2,0,1:T(2,128)(2,1)S(1)}, bf16[2,128,288]{2,0,1:T(2,128)(2,1)S(1)}, u32[]{:S(2)}, u32[]{:S(2)}) collective-permute-start(bf16[2,128,288]{2,0,1:T(2,128)(2,1)S(1)} %bitcast.38), channel_id=1, source_target_pairs={{0,480},{32,448},{64,416},{96,384},{128,352},{160,320},{192,288},{... | collective-permute-start | bytes 442376 | tf_op jit(solution)/shard_map/ppermute | solution.py:16
Sparse Core Ops, SparseCore 0:
  47.1 39.4 all-gather.2

commit v5 on v4

v5 whole, which is shorter than its diff:
```python
import jax
import jax.numpy as jnp
from jax import lax
from jax.sharding import Mesh
from jax.sharding import PartitionSpec as P

step_rate = 2.0

PIPE = ("py", "pz")
DP = ("dz", "dx", "dc")


def mirror(block):
    count = lax.axis_size(PIPE)
    route = [(low, count - 1 - low) for low in range(count)]
    return lax.ppermute(block, PIPE, route)


def shards(grad_out, hidden, weights, counts):
    row_total = grad_out.shape[3]
    full_width = grad_out.shape[4]
    micro = grad_out.shape[2]
    tokens = hidden.shape[3]
    share = hidden.shape[4]
    ranks = tokens // row_total
    scale_factor = float(full_width) ** (-0.5)
    slot_index = lax.broadcasted_iota(jnp.int32, (1, 1, 1, row_total), 3)
    live_rows = slot_index < counts
    masked = jnp.where(live_rows[..., None], grad_out, jnp.zeros_like(grad_out))
    own_weight = weights[0]
    own_rows = lax.all_gather(masked[0].reshape(2, -1, full_width), "dz", axis=1)
    mirror_rows, mirror_hidden = mirror((own_rows[1], hidden[0, 1]))
    pieces = [lax.all_gather(own_rows[0], ("dx", "dc"), axis=1), lax.all_gather(mirror_rows, ("dx", "dc"), axis=1)]
    pieces = [piece.reshape(-1, full_width) for piece in pieces]
    grads = []
    total = None
    for piece, acts in zip(pieces, (hidden[0, 0], mirror_hidden)):
        grad = jnp.dot(piece, own_weight.T, preferred_element_type=jnp.float32)
        grad = (grad * scale_factor).astype(jnp.bfloat16)
        grads.append(grad.reshape(ranks, micro, row_total, share).transpose(1, 0, 2, 3).reshape(micro, tokens, share))
        rows = acts.reshape(micro, ranks, row_total, share).transpose(1, 0, 2, 3).reshape(-1, share)
        part = jnp.dot(rows.T, piece, preferred_element_type=jnp.float32)
        total = part if total is None else total + part
    gradient = total * scale_factor
    new_weight = (own_weight.astype(jnp.float32) - step_rate * gradient).astype(jnp.bfloat16)
    returned = mirror(grads[1])
    grad_hidden = jnp.stack([grads[0], returned], axis=0)[None]
    return (grad_hidden, new_weight[None])


def solution(mesh):
    n_pipe, n_dp = mesh.devices.shape
    fine = Mesh(mesh.devices.reshape(4, n_pipe // 4, 4, 4, n_dp // 16), PIPE + DP)
    return jax.shard_map(
        shards,
        mesh=fine,
        in_specs=(
            P(PIPE, None, None, DP, None),
            P(PIPE, None, None, None, DP),
            P(PIPE, DP, None),
            P(PIPE, None, None, DP),
        ),
        out_specs=(P(PIPE, None, None, None, DP), P(PIPE, DP, None)),
        check_vma=False,
    )
```

time: 113 us -> 133 us (1.18)
  waiting for transfers between devices: 33 us -> 48.7 us
  matrix products: 7.93 us -> 13.5 us
  starting transfers between devices: 22.9 us -> 19.5 us
  blocking collectives: 26.5 us -> 29.5 us
    all_gather x1 -> x2, waiting for transfers between devices: 27.6 us -> 40.7 us  [the longest x1 29.4 us: shards(): lax.all_gather(mirror_rows, ('dx', 'dc'), axis=1)]
    ppermute x3, starting transfers between devices: 22.8 us -> 19.4 us  [mirror(): return lax.ppermute(block, PIPE, route)]
    all_gather x1, blocking collectives: 26.5 us -> 29.5 us  [shards(): lax.all_gather(masked[0].reshape(2, -1, full_width), 'dz', axis=1)]
    dot_general x1 -> x2, matrix products: 4.64 us -> 7.52 us  [shards(): part = jnp.dot(rows.T, piece, preferred_element_type=jnp.float32)]
    dot_general x1 -> x2, matrix products: 3.3 us -> 5.99 us  [shards(): grad = jnp.dot(piece, own_weight.T, preferred_element_type=jnp.float32)]
    ppermute x3, waiting for transfers between devices: 5.38 us -> 7.89 us  [mirror(): return lax.ppermute(block, PIPE, route)]
  transfers between devices with their start and end apart: 4 -> 5, of which waited for: 4 -> 4; matrix products, arithmetic and copies ran while one was open for 6% -> 9% of each run, Pallas kernels for 0% -> 0%
where the time goes in v5:
time: 133 us; the launch traced here: 132 us
  waiting for transfers between devices  48.7 us (37%)
  blocking collectives  29.5 us (22%)
  starting transfers between devices  19.5 us (15%)
  between operations  14.2 us (11%)
  matrix products  13.5 us (10%)
  local copies, waits for them, and re-layouts  4.04 us (3%)
  other arithmetic  2.41 us (2%)
    all_gather x1, blocking collectives, shards(): lax.all_gather(masked[0].reshape(2, -1, full_width), 'dz', axis=1)  29.5 us
    all_gather x1, waiting for transfers between devices, shards(): lax.all_gather(mirror_rows, ('dx', 'dc'), axis=1)  29.4 us
    ppermute x3, starting transfers between devices, mirror(): return lax.ppermute(block, PIPE, route)  19.4 us
    all_gather x1, waiting for transfers between devices, shards(): lax.all_gather(own_rows[0], ('dx', 'dc'), axis=1)  11.3 us
    ppermute x3, waiting for transfers between devices, mirror(): return lax.ppermute(block, PIPE, route)  7.89 us
    dot_general x2, matrix products, shards(): part = jnp.dot(rows.T, piece, preferred_element_type=jnp.float32)  7.52 us
    dot_general x2, matrix products, shards(): grad = jnp.dot(piece, own_weight.T, preferred_element_type=jnp.float32)  5.99 us
  transfers between devices with their start and end apart: 5, of which 4 were waited for; matrix products, arithmetic and copies ran while one was open for 9% of the time, Pallas kernels for 0%

profile of v5, /device:TPU:1, one launch (start us, length us, event | category | flops | bytes accessed | tf_op | source)
XLA Modules:
  0.0 131.8 jit_solution(9300279788151625873)
XLA Ops:
  7.2 0.8 iota_compare_fusion
  8.0 1.0 broadcast_select_fusion
  9.1 29.5 %all_gather.12 = bf16[2,4,8,3584]{3,2,0,1:T(8,128)(2,1)S(1)} all-gather(bf16[2,1,8,3584]{3,2,0,1:T(8,128)(2,1)S(1)} %all_gather_reshape_squeeze.3), channel_id=1, replica_groups=mesh['py'=4,'pz'=4,'dz'=4,'dx'=4,'dc'=2] {'dz'}, dimensions={1}, use_global_device_ids=true | all-gather | bytes 573440 | tf_op jit(solution)/shard_map/all_gather | solution.py:31
  38.6 0.7 fusion.21
  39.3 0.0 all-gather.7.cloned.1.call-start
  39.4 6.1 %collective-permute-start = (bf16[4,8,3584]{2,1,0:T(8,128)(2,1)S(1)}, bf16[4,8,3584]{2,1,0:T(8,128)(2,1)S(1)}, u32[]{:S(2)}, u32[]{:S(2)}) collective-permute-start(bf16[4,8,3584]{2,1,0:T(8,128)(2,1)S(1)} %get-tuple-element.7), channel_id=1, source_target_pairs={{0,480},{32,448},{64,416},{96,384},{128,352},{160,320},{192,288},{... | collective-permute-start | bytes 688136 | tf_op jit(solution)/shard_map/ppermute | solution.py:16
  45.5 4.6 %collective-permute-done = bf16[4,8,3584]{2,1,0:T(8,128)(2,1)S(1)} collective-permute-done((bf16[4,8,3584]{2,1,0:T(8,128)(2,1)S(1)}, bf16[4,8,3584]{2,1,0:T(8,128)(2,1)S(1)}, u32[]{:S(2)}, u32[]{:S(2)}) %collective-permute-start) | collective-permute-done | bytes 229408 | tf_op jit(solution)/shard_map/ppermute | solution.py:16
  50.1 0.7 copy-done.3
  50.8 6.1 %collective-permute-start.2 = (bf16[2,128,288]{1,2,0:T(8,128)(2,1)S(1)}, bf16[2,128,288]{1,2,0:T(8,128)(2,1)S(1)}, u32[]{:S(2)}, u32[]{:S(2)}) collective-permute-start(bf16[2,128,288]{1,2,0:T(8,128)(2,1)S(1)} %get-tuple-element.8), channel_id=1, source_target_pairs={{0,480},{32,448},{64,416},{96,384},{128,352},{160,320},{192,288},{... | collective-permute-start | bytes 442376 | tf_op jit(solution)/shard_map/ppermute | solution.py:16
  56.9 0.2 copy.21
  57.1 0.1 copy.22
  57.2 0.1 reshape.42
  57.3 3.3 %collective-permute-done.2 = bf16[2,128,288]{1,2,0:T(8,128)(2,1)S(1)} collective-permute-done((bf16[2,128,288]{1,2,0:T(8,128)(2,1)S(1)}, bf16[2,128,288]{1,2,0:T(8,128)(2,1)S(1)}, u32[]{:S(2)}, u32[]{:S(2)}) %collective-permute-start.2) | collective-permute-done | bytes 147488 | tf_op jit(solution)/shard_map/ppermute | solution.py:16
  60.6 0.2 copy.23
  60.8 0.1 copy.24
  60.9 0.1 reshape.44
  61.0 11.3 %all-gather.5.cloned.1.call-done = bf16[1,4,64,3584]{3,2,0,1:T(8,128)(2,1)} async-done(((bf16[1,4,8,3584]{3,2,0,1:T(8,128)(2,1)}), bf16[1,4,64,3584]{3,2,0,1:T(8,128)(2,1)}) %all-gather.5.cloned.1.call-update) | async-done | bytes 1835024 | tf_op jit(solution)/shard_map/all_gather | solution.py:33
  72.3 3.0 %fusion.18 = bf16[256,288]{0,1:T(8,128)(2,1)S(1)} fusion(bf16[256,3584]{1,0:T(8,128)(2,1)} %bitcast.50, bf16[1,288,3584]{2,1,0:T(8,128)(2,1)} %param.6), kind=kOutput, calls=%fused_computation.13 | convolution fusion | flops 528629760 | bytes 4046848 | tf_op jit(solution)/shard_map/dot_general | solution.py:38
  75.3 0.2 copy.17
  75.4 0.1 reshape.38
  75.5 0.2 copy.18
  75.7 2.7 %fusion.22 = f32[3584,288]{0,1:T(8,128)} fusion(bf16[256,3584]{1,0:T(8,128)(2,1)S(1)} %bitcast.51, bf16[256,288]{1,0:T(8,128)(2,1)S(1)} %reshape.42), kind=kOutput, calls=%fused_computation.20 | convolution fusion | flops 528482304 | bytes 6111232 | tf_op jit(solution)/shard_map/dot_general | solution.py:42
  78.3 29.4 %all-gather.7.cloned.1.call-done = bf16[4,64,3584]{2,1,0:T(8,128)(2,1)} async-done(((bf16[4,8,3584]{2,1,0:T(8,128)(2,1)}), bf16[4,64,3584]{2,1,0:T(8,128)(2,1)}) %all-gather.7.cloned.1.call-update) | async-done | bytes 1835024 | tf_op jit(solution)/shard_map/all_gather | solution.py:33
  107.8 3.0 %fusion.15 = bf16[256,288]{0,1:T(8,128)(2,1)S(1)} fusion(bf16[256,3584]{1,0:T(8,128)(2,1)} %bitcast.52, bf16[1,288,3584]{2,1,0:T(8,128)(2,1)} %param.6), kind=kOutput, calls=%fused_computation.12 | convolution fusion | flops 528629760 | bytes 4046848 | tf_op jit(solution)/shard_map/dot_general | solution.py:38
  110.8 0.2 copy.19
  111.0 0.1 reshape.40
  111.0 0.2 copy.20
  111.2 7.2 %collective-permute-start.1 = (bf16[2,128,288]{2,0,1:T(2,128)(2,1)S(1)}, bf16[2,128,288]{2,0,1:T(2,128)(2,1)S(1)}, u32[]{:S(2)}, u32[]{:S(2)}) collective-permute-start(bf16[2,128,288]{2,0,1:T(2,128)(2,1)S(1)} %bitcast.59), channel_id=1, source_target_pairs={{0,480},{32,448},{64,416},{96,384},{128,352},{160,320},{192,288},{... | collective-permute-start | bytes 442376 | tf_op jit(solution)/shard_map/ppermute | solution.py:16
  118.4 4.9 %fusion.4 = bf16[1,288,3584]{2,1,0:T(8,128)(2,1)} fusion(f32[3584,288]{0,1:T(8,128)} %fusion.22, bf16[256,3584]{1,0:T(8,128)(2,1)} %bitcast.53, bf16[256,288]{1,0:T(8,128)(2,1)S(1)} %reshape.44, bf16[1,288,3584]{2,1,0:T(8,128)(2,1)S(1)} %copy-done.1), kind=kOutput, calls=%fused_computation.5 | convolution fusion | flops 533643264 | bytes 10240000 | tf_op jit(solution)/shard_map/dot_general | solution.py:42
  123.2 0.0 collective-permute-done.1
  123.3 0.6 maximum_bitcast_fusion
  123.9 1.1 copy.25
  (12 shorter events, 0.1 us)
Async XLA Ops:
  7.2 43.6 %copy-start.2 = (bf16[1,2,2,128,288]{3,4,2,1,0:T(8,128)(2,1)S(1)}, bf16[1,2,2,128,288]{3,4,2,1,0:T(8,128)(2,1)}, u32[]{:S(2)}) copy-start(bf16[1,2,2,128,288]{3,4,2,1,0:T(8,128)(2,1)} %param.5) | copy-start | bytes 884740
  7.2 65.1 %all-gather.5.cloned.1.call-start = ((), (), s32[]{:S(2)}) async-start(), calls=%async_computation | async-start | bytes 2064384 | tf_op jit(solution)/shard_map/all_gather | solution.py:33
  39.3 68.4 %all-gather.7.cloned.1.call-start = ((), (), s32[]{:S(2)}) async-start(), calls=%async_computation.1 | async-start | bytes 2064384 | tf_op jit(solution)/shard_map/all_gather | solution.py:33
  39.4 10.7 %collective-permute-start = (bf16[4,8,3584]{2,1,0:T(8,128)(2,1)S(1)}, bf16[4,8,3584]{2,1,0:T(8,128)(2,1)S(1)}, u32[]{:S(2)}, u32[]{:S(2)}) collective-permute-start(bf16[4,8,3584]{2,1,0:T(8,128)(2,1)S(1)} %get-tuple-element.7), channel_id=1, source_target_pairs={{0,480},{32,448},{64,416},{96,384},{128,352},{160,320},{192,288},{... | collective-permute-start | bytes 688136 | tf_op jit(solution)/shard_map/ppermute | solution.py:16
  50.1 0.7 copy-start.3
  50.8 9.8 %collective-permute-start.2 = (bf16[2,128,288]{1,2,0:T(8,128)(2,1)S(1)}, bf16[2,128,288]{1,2,0:T(8,128)(2,1)S(1)}, u32[]{:S(2)}, u32[]{:S(2)}) collective-permute-start(bf16[2,128,288]{1,2,0:T(8,128)(2,1)S(1)} %get-tuple-element.8), channel_id=1, source_target_pairs={{0,480},{32,448},{64,416},{96,384},{128,352},{160,320},{192,288},{... | collective-permute-start | bytes 442376 | tf_op jit(solution)/shard_map/ppermute | solution.py:16
  72.3 3.4 %copy-start = (bf16[1,4,64,3584]{3,2,0,1:T(8,128)(2,1)S(1)}, bf16[1,4,64,3584]{3,2,0,1:T(8,128)(2,1)}, u32[]{:S(2)}) copy-start(bf16[1,4,64,3584]{3,2,0,1:T(8,128)(2,1)} %all-gather.5.cloned.1.call-done) | copy-start | bytes 5505028
  107.8 10.6 %copy-start.1 = (bf16[1,288,3584]{2,1,0:T(8,128)(2,1)S(1)}, bf16[1,288,3584]{2,1,0:T(8,128)(2,1)}, u32[]{:S(2)}) copy-start(bf16[1,288,3584]{2,1,0:T(8,128)(2,1)} %param.6) | copy-start | bytes 6193156
  111.2 12.1 %collective-permute-start.1 = (bf16[2,128,288]{2,0,1:T(2,128)(2,1)S(1)}, bf16[2,128,288]{2,0,1:T(2,128)(2,1)S(1)}, u32[]{:S(2)}, u32[]{:S(2)}) collective-permute-start(bf16[2,128,288]{2,0,1:T(2,128)(2,1)S(1)} %bitcast.59), channel_id=1, source_target_pairs={{0,480},{32,448},{64,416},{96,384},{128,352},{160,320},{192,288},{... | collective-permute-start | bytes 442376 | tf_op jit(solution)/shard_map/ppermute | solution.py:16
Sparse Core Ops, SparseCore 0:
  39.5 32.7 all-gather.4
  75.0 32.7 all-gather.6

commit v6 on v4

--- a/solution.py
+++ b/solution.py
@@ -1,6 +1,10 @@
+import functools
+
 import jax
 import jax.numpy as jnp
 from jax import lax
+from jax.experimental import pallas as pl
+from jax.experimental.pallas import tpu as pltpu
 from jax.sharding import Mesh
 from jax.sharding import PartitionSpec as P
 
@@ -22,6 +26,42 @@
     return out.reshape(-1, block.shape[-1])
 
 
+def tail_kernel(piece_ref, w_ref, acts_ref, grad_ref, neww_ref, acc_ref, *, scale, rate):
+    i = pl.program_id(0)
+
+    @pl.when(i == 0)
+    def _():
+        acc_ref[...] = jnp.zeros_like(acc_ref)
+
+    rows = piece_ref[...]
+    weight = w_ref[...]
+    acc_ref[...] += lax.dot_general(rows, weight, (((1,), (1,)), ((), ())), preferred_element_type=jnp.float32)
+    part = jnp.dot(acts_ref[...], rows, preferred_element_type=jnp.float32)
+    neww_ref[...] = (weight.astype(jnp.float32) - rate * (part * scale)).astype(neww_ref.dtype)
+
+    @pl.when(i == pl.num_programs(0) - 1)
+    def _():
+        grad_ref[...] = (acc_ref[...] * scale).astype(grad_ref.dtype)
+
+
+def tail(piece, weight, acts_t, scale, rate, chunk=512):
+    rows, width = piece.shape
+    share = weight.shape[0]
+    return pl.pallas_call(
+        functools.partial(tail_kernel, scale=scale, rate=rate),
+        grid=(width // chunk,),
+        in_specs=[pl.BlockSpec((rows, chunk), lambda i: (0, i)),
+                  pl.BlockSpec((share, chunk), lambda i: (0, i)),
+                  pl.BlockSpec((share, rows), lambda i: (0, 0))],
+        out_specs=[pl.BlockSpec((rows, share), lambda i: (0, 0)),
+                   pl.BlockSpec((share, chunk), lambda i: (0, i))],
+        out_shape=[jax.ShapeDtypeStruct((rows, share), jnp.bfloat16),
+                   jax.ShapeDtypeStruct((share, width), jnp.bfloat16)],
+        scratch_shapes=[pltpu.VMEM((rows, share), jnp.float32)],
+        compiler_params=pltpu.CompilerParams(dimension_semantics=("arbitrary",)),
+    )(piece, weight, acts_t)
+
+
 def shards(grad_out, hidden, weights, counts):
     row_total = grad_out.shape[3]
     full_width = grad_out.shape[4]
@@ -39,12 +79,8 @@
     piece = gather_rows(both_masked.reshape(-1, full_width))
     ranks = tokens // row_total
     acts = both_hidden.reshape(2, micro, ranks, row_total, share).transpose(2, 0, 1, 3, 4).reshape(-1, share)
-    grad = jnp.dot(piece, own_weight.T, preferred_element_type=jnp.float32)
-    grad = (grad * scale_factor).astype(jnp.bfloat16)
+    grad, new_weight = tail(piece, own_weight, acts.T, scale_factor, step_rate)
     grad = grad.reshape(ranks, 2, micro, row_total, share).transpose(1, 2, 0, 3, 4).reshape(2, micro, tokens, share)
-    total = jnp.dot(acts.T, piece, preferred_element_type=jnp.float32)
-    gradient = total * scale_factor
-    new_weight = (own_weight.astype(jnp.float32) - step_rate * gradient).astype(jnp.bfloat16)
     returned = mirror(grad[1])
     grad_hidden = jnp.stack([grad[0], returned], axis=0)[None]
     return (grad_hidden, new_weight[None])

time: 113 us -> 119 us (1.053)
  Pallas kernels: 0 us -> 8.48 us
  matrix products: 7.93 us -> 0 us
  waiting for transfers between devices: 33 us -> 37.8 us
    pallas_call x0 -> x1, Pallas kernels: none -> 8.48 us  [tail(): pl.pallas_call(functools.partial(tail_kernel, scale=scale, rate=rate), gr...]
    dot_general x2 -> x0, matrix products: 7.93 us -> none  [the longest x1 4.64 us: shards(): total = jnp.dot(acts.T, piece, preferred_element_type=jnp.float32)]
    ppermute x3, waiting for transfers between devices: 5.38 us -> 10 us  [mirror(): return lax.ppermute(block, PIPE, route)]
  transfers between devices with their start and end apart: 4 -> 4, of which waited for: 4 -> 4; matrix products, arithmetic and copies ran while one was open for 6% -> 2% of each run, Pallas kernels for 0% -> 0%
where the time goes in v6:
time: 119 us; the launch traced here: 117 us
  waiting for transfers between devices  37.8 us (32%)
  blocking collectives  26.5 us (22%)
  starting transfers between devices  22.9 us (19%)
  between operations  14.2 us (12%)
  Pallas kernels  8.48 us (7%)
  local copies, waits for them, and re-layouts  4.36 us (4%)
  other arithmetic  3.09 us (3%)
    all_gather x1, waiting for transfers between devices, gather_rows(): out = lax.all_gather(out, ('dx', 'dc'), axis=1)  27.7 us
    all_gather x1, blocking collectives, gather_rows(): out = lax.all_gather(block, 'dz', axis=0)  26.5 us
    ppermute x3, starting transfers between devices, mirror(): return lax.ppermute(block, PIPE, route)  22.8 us
    ppermute x3, waiting for transfers between devices, mirror(): return lax.ppermute(block, PIPE, route)  10 us
    pallas_call x1, Pallas kernels, tail(): pl.pallas_call(functools.partial(tail_kernel, scale=scale, rate=rate), gr...  8.48 us
  transfers between devices with their start and end apart: 4, of which 4 were waited for; matrix products, arithmetic and copies ran while one was open for 2% of the time, Pallas kernels for 0%

profile of v6, /device:TPU:1, one launch (start us, length us, event | category | flops | bytes accessed | tf_op | source)
XLA Modules:
  0.0 117.2 jit_solution(11095728097771507002)
XLA Ops:
  7.2 0.0 copy-start
  7.2 0.0 all-gather.3.cloned.1.call-start
  7.2 0.8 iota_compare_fusion
  8.0 1.0 broadcast_select_fusion
  9.1 9.5 %collective-permute-start = (bf16[2,4,3584]{2,1,0:T(4,128)(2,1)S(1)}, bf16[2,4,3584]{2,1,0:T(4,128)(2,1)S(1)}, u32[]{:S(2)}, u32[]{:S(2)}) collective-permute-start(bf16[2,4,3584]{2,1,0:T(4,128)(2,1)S(1)} %get-tuple-element.15), channel_id=1, source_target_pairs={{0,480},{32,448},{64,416},{96,384},{128,352},{160,320},{192,288},{... | collective-permute-start | bytes 172040 | tf_op jit(solution)/shard_map/ppermute | solution.py:20
  18.6 1.7 %collective-permute-done = bf16[2,4,3584]{2,1,0:T(4,128)(2,1)S(1)} collective-permute-done((bf16[2,4,3584]{2,1,0:T(4,128)(2,1)S(1)}, bf16[2,4,3584]{2,1,0:T(4,128)(2,1)S(1)}, u32[]{:S(2)}, u32[]{:S(2)}) %collective-permute-start) | collective-permute-done | bytes 57376 | tf_op jit(solution)/shard_map/ppermute | solution.py:20
  20.3 0.1 pad_maximum_fusion
  20.4 26.5 %all_gather.9 = bf16[4,16,3584]{2,1,0:T(8,128)(2,1)} all-gather(bf16[1,16,3584]{2,1,0:T(8,128)(2,1)S(1)} %all_gather_reshape.3), channel_id=1, replica_groups=mesh['py'=4,'pz'=4,'dz'=4,'dx'=4,'dc'=2] {'dz'}, dimensions={0}, use_global_device_ids=true | all-gather | bytes 573440 | tf_op jit(solution)/shard_map/all_gather | solution.py:24
  46.9 0.0 all-gather.3.cloned.1.call-update
  46.9 0.0 copy-done
  47.0 6.0 %collective-permute-start.1 = (bf16[2,128,288]{1,2,0:T(8,128)(2,1)S(1)}, bf16[2,128,288]{1,2,0:T(8,128)(2,1)S(1)}, u32[]{:S(2)}, u32[]{:S(2)}) collective-permute-start(bf16[2,128,288]{1,2,0:T(8,128)(2,1)S(1)} %get-tuple-element.13), channel_id=1, source_target_pairs={{0,480},{32,448},{64,416},{96,384},{128,352},{160,320},{192,288},{... | collective-permute-start | bytes 442376 | tf_op jit(solution)/shard_map/ppermute | solution.py:20
  52.9 0.2 copy.17
  53.1 3.6 %collective-permute-done.1 = bf16[2,128,288]{1,2,0:T(8,128)(2,1)S(1)} collective-permute-done((bf16[2,128,288]{1,2,0:T(8,128)(2,1)S(1)}, bf16[2,128,288]{1,2,0:T(8,128)(2,1)S(1)}, u32[]{:S(2)}, u32[]{:S(2)}) %collective-permute-start.1) | collective-permute-done | bytes 147488 | tf_op jit(solution)/shard_map/ppermute | solution.py:20
  56.8 0.2 copy.18
  57.0 0.6 maximum_bitcast_fusion
  57.6 0.2 copy.19
  57.7 0.2 reshape.32
  57.9 0.9 copy.20
  58.8 27.7 %all-gather.3.cloned.1.call-done = bf16[4,128,3584]{2,1,0:T(8,128)(2,1)} async-done(((bf16[4,16,3584]{2,1,0:T(8,128)(2,1)}), bf16[4,128,3584]{2,1,0:T(8,128)(2,1)}) %all-gather.3.cloned.1.call-update) | async-done | bytes 3670032 | tf_op jit(solution)/shard_map/all_gather | solution.py:25
  86.5 8.5 %shard_map.59 = (bf16[512,288]{1,0:T(8,128)(2,1)}, bf16[288,3584]{1,0:T(8,128)(2,1)}) custom-call(bf16[512,3584]{1,0:T(8,128)(2,1)} %bitcast.22, bf16[288,3584]{1,0:T(8,128)(2,1)} %bitcast.23, bf16[288,512]{1,0:T(8,128)(2,1)} %bitcast.25), custom_call_target="tpu_custom_call" | custom-call | tf_op jit(solution)/shard_map/pallas_call | solution.py:50
  95.0 1.1 reshape.33
  96.1 0.1 fusion
  96.3 0.2 copy.22
  96.4 7.3 %collective-permute-start.2 = (bf16[2,128,288]{2,0,1:T(2,128)(2,1)S(1)}, bf16[2,128,288]{2,0,1:T(2,128)(2,1)S(1)}, u32[]{:S(2)}, u32[]{:S(2)}) collective-permute-start(bf16[2,128,288]{2,0,1:T(2,128)(2,1)S(1)} %bitcast.29), channel_id=1, source_target_pairs={{0,480},{32,448},{64,416},{96,384},{128,352},{160,320},{192,288},{... | collective-permute-start | bytes 442376 | tf_op jit(solution)/shard_map/ppermute | solution.py:20
  103.8 0.2 copy.21
  103.9 4.7 %collective-permute-done.2 = bf16[2,128,288]{2,0,1:T(2,128)(2,1)S(1)} collective-permute-done((bf16[2,128,288]{2,0,1:T(2,128)(2,1)S(1)}, bf16[2,128,288]{2,0,1:T(2,128)(2,1)S(1)}, u32[]{:S(2)}, u32[]{:S(2)}) %collective-permute-start.2) | collective-permute-done | bytes 147488 | tf_op jit(solution)/shard_map/ppermute | solution.py:20
  108.7 0.6 maximum_bitcast_fusion.1
  109.3 1.1 copy.23
  (3 shorter events, 0.1 us)
Async XLA Ops:
  7.2 39.8 %copy-start = (bf16[1,2,2,128,288]{3,4,2,1,0:T(8,128)(2,1)S(1)}, bf16[1,2,2,128,288]{3,4,2,1,0:T(8,128)(2,1)}, u32[]{:S(2)}) copy-start(bf16[1,2,2,128,288]{3,4,2,1,0:T(8,128)(2,1)} %param.5) | copy-start | bytes 884740
  7.2 79.4 %all-gather.3.cloned.1.call-start = ((), (), s32[]{:S(2)}) async-start(), calls=%async_computation | async-start | bytes 4128768 | tf_op jit(solution)/shard_map/all_gather | solution.py:25
  9.1 11.2 %collective-permute-start = (bf16[2,4,3584]{2,1,0:T(4,128)(2,1)S(1)}, bf16[2,4,3584]{2,1,0:T(4,128)(2,1)S(1)}, u32[]{:S(2)}, u32[]{:S(2)}) collective-permute-start(bf16[2,4,3584]{2,1,0:T(4,128)(2,1)S(1)} %get-tuple-element.15), channel_id=1, source_target_pairs={{0,480},{32,448},{64,416},{96,384},{128,352},{160,320},{192,288},{... | collective-permute-start | bytes 172040 | tf_op jit(solution)/shard_map/ppermute | solution.py:20
  47.0 9.8 %collective-permute-start.1 = (bf16[2,128,288]{1,2,0:T(8,128)(2,1)S(1)}, bf16[2,128,288]{1,2,0:T(8,128)(2,1)S(1)}, u32[]{:S(2)}, u32[]{:S(2)}) collective-permute-start(bf16[2,128,288]{1,2,0:T(8,128)(2,1)S(1)} %get-tuple-element.13), channel_id=1, source_target_pairs={{0,480},{32,448},{64,416},{96,384},{128,352},{160,320},{192,288},{... | collective-permute-start | bytes 442376 | tf_op jit(solution)/shard_map/ppermute | solution.py:20
  96.4 12.2 %collective-permute-start.2 = (bf16[2,128,288]{2,0,1:T(2,128)(2,1)S(1)}, bf16[2,128,288]{2,0,1:T(2,128)(2,1)S(1)}, u32[]{:S(2)}, u32[]{:S(2)}) collective-permute-start(bf16[2,128,288]{2,0,1:T(2,128)(2,1)S(1)} %bitcast.29), channel_id=1, source_target_pairs={{0,480},{32,448},{64,416},{96,384},{128,352},{160,320},{192,288},{... | collective-permute-start | bytes 442376 | tf_op jit(solution)/shard_map/ppermute | solution.py:20
Sparse Core Ops, SparseCore 0:
  47.0 39.4 all-gather.2

commit v7 on v4

--- a/solution.py
+++ b/solution.py
@@ -17,9 +17,17 @@
 
 
 def gather_rows(block):
+    half = block.shape[-1] // 2
     out = lax.all_gather(block, "dz", axis=0)
-    out = lax.all_gather(out, ("dx", "dc"), axis=1)
-    return out.reshape(-1, block.shape[-1])
+    out = jnp.concatenate(
+        [lax.all_gather(out[..., :half], "dx", axis=1), lax.all_gather(out[..., half:], "dx", axis=1)], axis=-1
+    )
+    other = lax.ppermute(out, "dc", [(0, 1), (1, 0)])
+    return jnp.stack([out, other], axis=0)
+
+
+def own_first(array):
+    return jnp.where(lax.axis_index("dc") == 0, array, array[::-1])
 
 
 def shards(grad_out, hidden, weights, counts):
@@ -28,6 +36,7 @@
     micro = grad_out.shape[2]
     tokens = hidden.shape[3]
     share = hidden.shape[4]
+    n_z, n_x, n_c = (lax.axis_size(name) for name in DP)
     scale_factor = float(full_width) ** (-0.5)
     slot_index = lax.broadcasted_iota(jnp.int32, (1, 1, 1, row_total), 3)
     live_rows = slot_index < counts
@@ -36,12 +45,13 @@
     mirror_masked, mirror_hidden = mirror((masked[0, 1], hidden[0, 1]))
     both_masked = jnp.stack([masked[0, 0], mirror_masked], axis=0)
     both_hidden = jnp.stack([hidden[0, 0], mirror_hidden], axis=0)
-    piece = gather_rows(both_masked.reshape(-1, full_width))
-    ranks = tokens // row_total
-    acts = both_hidden.reshape(2, micro, ranks, row_total, share).transpose(2, 0, 1, 3, 4).reshape(-1, share)
+    piece = gather_rows(both_masked.reshape(-1, full_width)).reshape(-1, full_width)
+    acts = both_hidden.reshape(2, micro, n_z, n_x, n_c, row_total, share).transpose(4, 2, 3, 0, 1, 5, 6)
+    acts = own_first(acts).reshape(-1, share)
     grad = jnp.dot(piece, own_weight.T, preferred_element_type=jnp.float32)
     grad = (grad * scale_factor).astype(jnp.bfloat16)
-    grad = grad.reshape(ranks, 2, micro, row_total, share).transpose(1, 2, 0, 3, 4).reshape(2, micro, tokens, share)
+    grad = own_first(grad.reshape(n_c, n_z, n_x, 2, micro, row_total, share))
+    grad = grad.transpose(3, 4, 1, 2, 0, 5, 6).reshape(2, micro, tokens, share)
     total = jnp.dot(acts.T, piece, preferred_element_type=jnp.float32)
     gradient = total * scale_factor
     new_weight = (own_weight.astype(jnp.float32) - step_rate * gradient).astype(jnp.bfloat16)

time: 113 us -> 111 us (0.982)
  waiting for transfers between devices: 33 us -> 7.86 us
  blocking collectives: 26.5 us -> 49.8 us
  between operations: 14.2 us -> 0.86 us
  starting transfers between devices: 22.9 us -> 34.1 us
  other arithmetic: 3.2 us -> 6.73 us
  matrix products: 7.93 us -> 5.9 us
    all_gather x1 -> x0, waiting for transfers between devices: 27.6 us -> none  [gather_rows(): out = lax.all_gather(out, ('dx', 'dc'), axis=1)]
    all_gather x0 -> x2, blocking collectives: none -> 23.6 us  [the longest x1 12.1 us: gather_rows(): lax.all_gather(out[..., half:], 'dx', axis=1)]
    ppermute x0 -> x1, starting transfers between devices: none -> 13.1 us  [gather_rows(): other = lax.ppermute(out, 'dc', [(0, 1), (1, 0)])]
    another operation x0 -> x2, other arithmetic: none -> 3.65 us  [gather_rows(): return jnp.stack([out, other], axis=0)]
    ppermute x3, waiting for transfers between devices: 5.38 us -> 7.86 us  [mirror(): return lax.ppermute(block, PIPE, route)]
    dot_general x1, matrix products: 3.3 us -> 1.26 us  [shards(): grad = jnp.dot(piece, own_weight.T, preferred_element_type=jnp.float32)]
    ppermute x3, starting transfers between devices: 22.8 us -> 21 us  [mirror(): return lax.ppermute(block, PIPE, route)]
    unnamed x3 -> x9, local copies, waits for them, and re-layouts: 1.1 us -> 2.9 us
  transfers between devices with their start and end apart: 4 -> 4, of which waited for: 4 -> 3; matrix products, arithmetic and copies ran while one was open for 6% -> 5% of each run, Pallas kernels for 0% -> 0%
where the time goes in v7:
time: 111 us; the launch traced here: 110 us
  blocking collectives  49.8 us (45%)
  starting transfers between devices  34.1 us (31%)
  waiting for transfers between devices  7.86 us (7%)
  other arithmetic  6.73 us (6%)
  matrix products  5.9 us (5%)
  local copies, waits for them, and re-layouts  4.52 us (4%)
    all_gather x1, blocking collectives, gather_rows(): out = lax.all_gather(block, 'dz', axis=0)  26.2 us
    ppermute x3, starting transfers between devices, mirror(): return lax.ppermute(block, PIPE, route)  21 us
    ppermute x1, starting transfers between devices, gather_rows(): other = lax.ppermute(out, 'dc', [(0, 1), (1, 0)])  13.1 us
    all_gather x1, blocking collectives, gather_rows(): lax.all_gather(out[..., half:], 'dx', axis=1)  12.1 us
    all_gather x1, blocking collectives, gather_rows(): lax.all_gather(out[..., :half], 'dx', axis=1)  11.5 us
    ppermute x3, waiting for transfers between devices, mirror(): return lax.ppermute(block, PIPE, route)  7.86 us
    dot_general x1, matrix products, shards(): total = jnp.dot(acts.T, piece, preferred_element_type=jnp.float32)  4.64 us
    another operation x2, other arithmetic, gather_rows(): return jnp.stack([out, other], axis=0)  3.65 us
  transfers between devices with their start and end apart: 4, of which 3 were waited for; matrix products, arithmetic and copies ran while one was open for 5% of the time, Pallas kernels for 0%

profile of v7, /device:TPU:1, one launch (start us, length us, event | category | flops | bytes accessed | tf_op | source)
XLA Modules:
  0.0 109.7 jit_solution(10293409518655007561)
XLA Ops:
  0.6 0.8 iota_compare_fusion
  1.4 1.0 broadcast_select_fusion
  2.5 9.5 %collective-permute-start = (bf16[2,4,3584]{2,1,0:T(4,128)(2,1)S(1)}, bf16[2,4,3584]{2,1,0:T(4,128)(2,1)S(1)}, u32[]{:S(2)}, u32[]{:S(2)}) collective-permute-start(bf16[2,4,3584]{2,1,0:T(4,128)(2,1)S(1)} %get-tuple-element.15), channel_id=1, source_target_pairs={{0,480},{32,448},{64,416},{96,384},{128,352},{160,320},{192,288},{... | collective-permute-start | bytes 172040 | tf_op jit(solution)/shard_map/ppermute | solution.py:16
  12.0 1.7 %collective-permute-done = bf16[2,4,3584]{2,1,0:T(4,128)(2,1)S(1)} collective-permute-done((bf16[2,4,3584]{2,1,0:T(4,128)(2,1)S(1)}, bf16[2,4,3584]{2,1,0:T(4,128)(2,1)S(1)}, u32[]{:S(2)}, u32[]{:S(2)}) %collective-permute-start) | collective-permute-done | bytes 57376 | tf_op jit(solution)/shard_map/ppermute | solution.py:16
  13.6 0.1 pad_maximum_fusion.2
  13.8 26.2 %all_gather.15 = bf16[4,16,3584]{2,1,0:T(8,128)(2,1)S(1)} all-gather(bf16[1,16,3584]{2,1,0:T(8,128)(2,1)S(1)} %all_gather_reshape.3), channel_id=1, replica_groups=mesh['py'=4,'pz'=4,'dz'=4,'dx'=4,'dc'=2] {'dz'}, dimensions={0}, use_global_device_ids=true | all-gather | bytes 573440 | tf_op jit(solution)/shard_map/all_gather | solution.py:21
  40.0 11.5 %all-gather = bf16[4,64,1792]{2,1,0:T(8,128)(2,1)S(1)} all-gather(bf16[4,16,1792]{2,1,0:T(8,128)(2,1)S(1)} %get-tuple-element.8), channel_id=2, replica_groups=mesh['py'=4,'pz'=4,'dz'=4,'dx'=4,'dc'=2] {'dx'}, dimensions={1}, use_global_device_ids=true | all-gather | bytes 1146880 | tf_op jit(solution)/shard_map/all_gather | solution.py:23
  51.4 12.1 %all-gather.1 = bf16[4,64,1792]{2,1,0:T(8,128)(2,1)S(1)} all-gather(bf16[4,16,1792]{2,1,0:T(8,128)(2,1)S(1)} %get-tuple-element.9), channel_id=3, replica_groups=mesh['py'=4,'pz'=4,'dz'=4,'dx'=4,'dc'=2] {'dx'}, dimensions={1}, use_global_device_ids=true | all-gather | bytes 1146880 | tf_op jit(solution)/shard_map/all_gather | solution.py:23
  63.6 1.7 %fusion.12 = (bf16[1,4,4,16,3584]{4,3,2,1,0:T(8,128)(2,1)S(1)}, bf16[4,4,16,3584]{3,2,1,0:T(8,128)(2,1)}) fusion(bf16[4,4,16,1792]{3,2,1,0:T(8,128)(2,1)S(1)} %bitcast.41, bf16[4,4,16,1792]{3,2,1,0:T(8,128)(2,1)S(1)} %bitcast.40), kind=kLoop, calls=%fused_computation.21 | loop fusion | flops 3670016 | bytes 5505024 | tf_op jit(solution)/shard_map/stack | solution.py:26
  65.2 13.1 %collective-permute-start.1 = (bf16[4,4,16,3584]{3,2,1,0:T(8,128)(2,1)}, bf16[4,4,16,3584]{3,2,1,0:T(8,128)(2,1)}, u32[]{:S(2)}, u32[]{:S(2)}) collective-permute-start(bf16[4,4,16,3584]{3,2,1,0:T(8,128)(2,1)} %get-tuple-element.7), channel_id=1, source_target_pairs={{0,1},{1,0},{2,3},{3,2},{4,5},{5,4},{6,7},{7,6},{8,9},{9,8},{10,11... | collective-permute-start | bytes 5505032 | tf_op jit(solution)/shard_map/ppermute | solution.py:25
  78.4 5.7 %collective-permute-start.3 = (bf16[2,128,288]{1,2,0:T(8,128)(2,1)S(1)}, bf16[2,128,288]{1,2,0:T(8,128)(2,1)S(1)}, u32[]{:S(2)}, u32[]{:S(2)}) collective-permute-start(bf16[2,128,288]{1,2,0:T(8,128)(2,1)S(1)} %get-tuple-element.13), channel_id=1, source_target_pairs={{0,480},{32,448},{64,416},{96,384},{128,352},{160,320},{192,288},{... | collective-permute-start | bytes 442376 | tf_op jit(solution)/shard_map/ppermute | solution.py:16
  84.2 0.2 copy.21
  84.3 0.1 copy.23
  84.4 5.3 %collective-permute-done.3 = bf16[2,128,288]{1,2,0:T(8,128)(2,1)S(1)} collective-permute-done((bf16[2,128,288]{1,2,0:T(8,128)(2,1)S(1)}, bf16[2,128,288]{1,2,0:T(8,128)(2,1)S(1)}, u32[]{:S(2)}, u32[]{:S(2)}) %collective-permute-start.3) | collective-permute-done | bytes 147488 | tf_op jit(solution)/shard_map/ppermute | solution.py:16
  89.7 0.2 copy.22
  90.0 0.3 maximum_bitcast_fusion.1
  90.3 0.2 reverse_select_fusion
  90.5 0.2 reshape.33
  90.7 2.0 %pad_maximum_fusion = bf16[2,4,4,16,3584]{4,3,2,1,0:T(8,128)(2,1)S(1)} fusion(bf16[1,4,4,16,3584]{4,3,2,1,0:T(8,128)(2,1)} %bitcast.7, bf16[1,4,4,16,3584]{4,3,2,1,0:T(8,128)(2,1)S(1)} %get-tuple-element.6), kind=kLoop, calls=%fused_computation.4 | loop fusion | flops 1835008 | bytes 7340032 | tf_op jit(solution)/shard_map/stack | solution.py:26
  92.7 1.8 %copy-done = bf16[2,4,4,16,3584]{4,3,2,1,0:T(8,128)(2,1)} copy-done((bf16[2,4,4,16,3584]{4,3,2,1,0:T(8,128)(2,1)}, bf16[2,4,4,16,3584]{4,3,2,1,0:T(8,128)(2,1)S(1)}, u32[]{:S(2)}) %copy-start) | copy-done | bytes 3670040
  94.5 1.3 %fusion.8 = bf16[512,288]{0,1:T(8,128)(2,1)S(1)} fusion(bf16[512,3584]{1,0:T(8,128)(2,1)S(1)} %bitcast.38, bf16[1,288,3584]{2,1,0:T(8,128)(2,1)S(1)} %copy-done.1), kind=kOutput, calls=%fused_computation.9 | convolution fusion | flops 1057259520 | bytes 6029312 | tf_op jit(solution)/shard_map/dot_general | solution.py:51
  95.8 0.2 copy.18
  96.0 0.1 reshape.32
  96.1 0.2 fusion.11
  96.3 0.1 fusion.14
  96.4 0.2 copy.20
  96.6 5.7 %collective-permute-start.2 = (bf16[2,128,288]{2,0,1:T(2,128)(2,1)S(1)}, bf16[2,128,288]{2,0,1:T(2,128)(2,1)S(1)}, u32[]{:S(2)}, u32[]{:S(2)}) collective-permute-start(bf16[2,128,288]{2,0,1:T(2,128)(2,1)S(1)} %bitcast.45), channel_id=1, source_target_pairs={{0,480},{32,448},{64,416},{96,384},{128,352},{160,320},{192,288},{... | collective-permute-start | bytes 442376 | tf_op jit(solution)/shard_map/ppermute | solution.py:16
  102.3 4.6 %fusion.2 = bf16[1,288,3584]{2,1,0:T(8,128)(2,1)} fusion(bf16[512,288]{1,0:T(8,128)(2,1)S(1)} %reshape.33, bf16[512,3584]{1,0:T(8,128)(2,1)} %bitcast.39, bf16[1,288,3584]{2,1,0:T(8,128)(2,1)S(1)} %copy-done.2), kind=kOutput, calls=%fused_computation.3 | convolution fusion | flops 1061093376 | bytes 8093696 | tf_op jit(solution)/shard_map/dot_general | solution.py:55
  107.0 0.2 copy.19
  107.1 0.9 collective-permute-done.2
  108.0 0.6 maximum_bitcast_fusion
  108.7 1.1 copy.25
  (13 shorter events, 0.2 us)
Async XLA Ops:
  2.5 11.2 %collective-permute-start = (bf16[2,4,3584]{2,1,0:T(4,128)(2,1)S(1)}, bf16[2,4,3584]{2,1,0:T(4,128)(2,1)S(1)}, u32[]{:S(2)}, u32[]{:S(2)}) collective-permute-start(bf16[2,4,3584]{2,1,0:T(4,128)(2,1)S(1)} %get-tuple-element.15), channel_id=1, source_target_pairs={{0,480},{32,448},{64,416},{96,384},{128,352},{160,320},{192,288},{... | collective-permute-start | bytes 172040 | tf_op jit(solution)/shard_map/ppermute | solution.py:16
  40.0 38.4 %copy-start.3 = (bf16[1,2,2,128,288]{3,4,2,1,0:T(8,128)(2,1)S(1)}, bf16[1,2,2,128,288]{3,4,2,1,0:T(8,128)(2,1)}, u32[]{:S(2)}) copy-start(bf16[1,2,2,128,288]{3,4,2,1,0:T(8,128)(2,1)} %param.5) | copy-start | bytes 884740
  65.2 25.4 %collective-permute-start.1 = (bf16[4,4,16,3584]{3,2,1,0:T(8,128)(2,1)}, bf16[4,4,16,3584]{3,2,1,0:T(8,128)(2,1)}, u32[]{:S(2)}, u32[]{:S(2)}) collective-permute-start(bf16[4,4,16,3584]{3,2,1,0:T(8,128)(2,1)} %get-tuple-element.7), channel_id=1, source_target_pairs={{0,1},{1,0},{2,3},{3,2},{4,5},{5,4},{6,7},{7,6},{8,9},{9,8},{10,11... | collective-permute-start | bytes 5505032 | tf_op jit(solution)/shard_map/ppermute | solution.py:25
  78.4 11.3 %collective-permute-start.3 = (bf16[2,128,288]{1,2,0:T(8,128)(2,1)S(1)}, bf16[2,128,288]{1,2,0:T(8,128)(2,1)S(1)}, u32[]{:S(2)}, u32[]{:S(2)}) collective-permute-start(bf16[2,128,288]{1,2,0:T(8,128)(2,1)S(1)} %get-tuple-element.13), channel_id=1, source_target_pairs={{0,480},{32,448},{64,416},{96,384},{128,352},{160,320},{192,288},{... | collective-permute-start | bytes 442376 | tf_op jit(solution)/shard_map/ppermute | solution.py:16
  90.7 3.8 %copy-start.1 = (bf16[1,288,3584]{2,1,0:T(8,128)(2,1)S(1)}, bf16[1,288,3584]{2,1,0:T(8,128)(2,1)}, u32[]{:S(2)}) copy-start(bf16[1,288,3584]{2,1,0:T(8,128)(2,1)} %param.6) | copy-start | bytes 6193156
  92.7 1.8 %copy-start = (bf16[2,4,4,16,3584]{4,3,2,1,0:T(8,128)(2,1)}, bf16[2,4,4,16,3584]{4,3,2,1,0:T(8,128)(2,1)S(1)}, u32[]{:S(2)}) copy-start(bf16[2,4,4,16,3584]{4,3,2,1,0:T(8,128)(2,1)S(1)} %pad_maximum_fusion) | copy-start | bytes 11010052
  94.5 7.8 %copy-start.2 = (bf16[1,288,3584]{2,1,0:T(8,128)(2,1)S(1)}, bf16[1,288,3584]{2,1,0:T(8,128)(2,1)}, u32[]{:S(2)}) copy-start(bf16[1,288,3584]{2,1,0:T(8,128)(2,1)} %param.6) | copy-start | bytes 6193156
  96.6 11.5 %collective-permute-start.2 = (bf16[2,128,288]{2,0,1:T(2,128)(2,1)S(1)}, bf16[2,128,288]{2,0,1:T(2,128)(2,1)S(1)}, u32[]{:S(2)}, u32[]{:S(2)}) collective-permute-start(bf16[2,128,288]{2,0,1:T(2,128)(2,1)S(1)} %bitcast.45), channel_id=1, source_target_pairs={{0,480},{32,448},{64,416},{96,384},{128,352},{160,320},{192,288},{... | collective-permute-start | bytes 442376 | tf_op jit(solution)/shard_map/ppermute | solution.py:16

commit v8 on v5

v8 whole, which is shorter than its diff:
```python
import jax
import jax.numpy as jnp
from jax import lax
from jax.sharding import Mesh
from jax.sharding import PartitionSpec as P

step_rate = 2.0

PIPE = ("py", "pz")
DP = ("dz", "dx", "dc")


def mirror(block):
    count = lax.axis_size(PIPE)
    route = [(low, count - 1 - low) for low in range(count)]
    return lax.ppermute(block, PIPE, route)


def mirror_pair(rows, acts):
    lane = 128
    flat = jnp.concatenate([rows.reshape(-1, lane), acts.reshape(-1, lane)], axis=0)
    flat = mirror(flat)
    split_at = rows.size // lane
    return flat[:split_at].reshape(rows.shape), flat[split_at:].reshape(acts.shape)


def pick_core(array, axis, core):
    return lax.dynamic_index_in_dim(array, core, axis=axis, keepdims=False)


def shards(grad_out, hidden, weights, counts):
    row_total = grad_out.shape[3]
    full_width = grad_out.shape[4]
    micro = grad_out.shape[2]
    tokens = hidden.shape[3]
    share = hidden.shape[4]
    n_z, n_x, n_c = (lax.axis_size(name) for name in DP)
    scale_factor = float(full_width) ** (-0.5)
    slot_index = lax.broadcasted_iota(jnp.int32, (1, 1, 1, row_total), 3)
    live_rows = slot_index < counts
    masked = jnp.where(live_rows[..., None], grad_out, jnp.zeros_like(grad_out))
    own_weight = weights[0]
    mirror_masked, mirror_hidden = mirror_pair(masked[0, 1], hidden[0, 1])
    rows = jnp.stack([masked[0, 0], mirror_masked], axis=0).reshape(2, -1, full_width)
    rows = lax.all_gather(rows, "dz", axis=1)
    core = lax.axis_index("dc")
    cores = (core, n_c - 1 - core)
    grads = []
    total = None
    for slot, acts in enumerate((hidden[0, 0], mirror_hidden)):
        own = lax.all_gather(rows[slot], "dx", axis=1)
        other = lax.ppermute(own, "dc", [(0, 1), (1, 0)])
        acts = acts.reshape(micro, n_z, n_x, n_c, row_total, share)
        parts = []
        for piece, which in zip((own, other), cores):
            piece = piece.reshape(-1, full_width)
            grad = jnp.dot(piece, own_weight.T, preferred_element_type=jnp.float32)
            parts.append((grad * scale_factor).astype(jnp.bfloat16))
            part_acts = pick_core(acts, 3, which).transpose(1, 2, 0, 3, 4).reshape(-1, share)
            part = jnp.dot(part_acts.T, piece, preferred_element_type=jnp.float32)
            total = part if total is None else total + part
        grad = jnp.stack(parts, axis=0).reshape(n_c, n_z, n_x, micro, row_total, share)
        grad = jnp.where(core == 0, grad, grad[::-1])
        grads.append(grad.transpose(3, 1, 2, 0, 4, 5).reshape(micro, tokens, share))
    gradient = total * scale_factor
    new_weight = (own_weight.astype(jnp.float32) - step_rate * gradient).astype(jnp.bfloat16)
    returned = mirror(grads[1])
    grad_hidden = jnp.stack([grads[0], returned], axis=0)[None]
    return (grad_hidden, new_weight[None])


def solution(mesh):
    n_pipe, n_dp = mesh.devices.shape
    fine = Mesh(mesh.devices.reshape(4, n_pipe // 4, 4, 4, n_dp // 16), PIPE + DP)
    return jax.shard_map(
        shards,
        mesh=fine,
        in_specs=(
            P(PIPE, None, None, DP, None),
            P(PIPE, None, None, None, DP),
            P(PIPE, DP, None),
            P(PIPE, None, None, DP),
        ),
        out_specs=(P(PIPE, None, None, None, DP), P(PIPE, DP, None)),
        check_vma=False,
    )
```

time: 133 us -> 121 us (0.910)
  waiting for transfers between devices: 48.7 us -> 2.61 us
  blocking collectives: 29.5 us -> 50 us
  between operations: 14.2 us -> 0.95 us
  starting transfers between devices: 19.5 us -> 30.9 us
  local copies, waits for them, and re-layouts: 4.04 us -> 14.9 us
  matrix products: 13.5 us -> 17.5 us
    all_gather x2 -> x0, waiting for transfers between devices: 40.7 us -> none  [the longest x1 29.4 us: shards(): lax.all_gather(mirror_rows, ('dx', 'dc'), axis=1)]
    all_gather x1 -> x3, blocking collectives: 29.5 us -> 50 us  [the longest x1 25.3 us: shards(): rows = lax.all_gather(rows, 'dz', axis=1)]
    ppermute x0 -> x2, starting transfers between devices: none -> 15.2 us  [shards(): other = lax.ppermute(own, 'dc', [(0, 1), (1, 0)])]
    another operation x1 -> x11, local copies, waits for them, and re-layouts: 0.03 us -> 6.49 us  [the longest x6 5.72 us: shards(): jnp.stack(parts, axis=0).reshape(n_c, n_z, n_x, micro, row_total, share)]
    ppermute x3 -> x2, waiting for transfers between devices: 7.89 us -> 2.6 us  [mirror(): return lax.ppermute(block, PIPE, route)]
    ppermute x3 -> x2, starting transfers between devices: 19.4 us -> 15.8 us  [mirror(): return lax.ppermute(block, PIPE, route)]
    dot_general x2 -> x4, matrix products: 7.52 us -> 11.1 us  [shards(): part = jnp.dot(part_acts.T, piece, preferred_element_type=jnp.float32)]
    reshape x4, local copies, waits for them, and re-layouts: 0.3 us -> 2.12 us  [shards(): pick_core(acts, 3, which).transpose(1, 2, 0, 3, 4).reshape(-1, share)]
  transfers between devices with their start and end apart: 5 -> 4, of which waited for: 4 -> 1; matrix products, arithmetic and copies ran while one was open for 9% -> 19% of each run, Pallas kernels for 0% -> 0%
where the time goes in v8:
time: 121 us; the launch traced here: 119 us
  blocking collectives  50 us (41%)
  starting transfers between devices  30.9 us (26%)
  matrix products  17.5 us (14%)
  local copies, waits for them, and re-layouts  14.9 us (12%)
  waiting for transfers between devices  2.61 us (2%)
  other arithmetic  2.56 us (2%)
    all_gather x1, blocking collectives, shards(): rows = lax.all_gather(rows, 'dz', axis=1)  25.3 us
    all_gather x2, blocking collectives, shards(): own = lax.all_gather(rows[slot], 'dx', axis=1)  24.7 us
    ppermute x2, starting transfers between devices, mirror(): return lax.ppermute(block, PIPE, route)  15.8 us
    ppermute x2, starting transfers between devices, shards(): other = lax.ppermute(own, 'dc', [(0, 1), (1, 0)])  15.2 us
    dot_general x4, matrix products, shards(): part = jnp.dot(part_acts.T, piece, preferred_element_type=jnp.float32)  11.1 us
    dot_general x4, matrix products, shards(): grad = jnp.dot(piece, own_weight.T, preferred_element_type=jnp.float32)  6.32 us
    another operation x6, local copies, waits for them, and re-layouts, shards(): jnp.stack(parts, axis=0).reshape(n_c, n_z, n_x, micro, row_total, share)  5.72 us
    ppermute x2, waiting for transfers between devices, mirror(): return lax.ppermute(block, PIPE, route)  2.6 us
  transfers between devices with their start and end apart: 4, of which 1 were waited for; matrix products, arithmetic and copies ran while one was open for 19% of the time, Pallas kernels for 0%

profile of v8, /device:TPU:1, one launch (start us, length us, event | category | flops | bytes accessed | tf_op | source)
XLA Modules:
  0.0 119.4 jit_solution(4108868677003273818)
XLA Ops:
  0.6 0.8 iota_compare_fusion
  1.4 1.0 broadcast_select_fusion
  2.5 1.1 fusion.39
  4.2 9.5 %collective-permute-start = (bf16[800,128]{1,0:T(8,128)(2,1)S(1)}, bf16[800,128]{1,0:T(8,128)(2,1)S(1)}, u32[]{:S(2)}, u32[]{:S(2)}) collective-permute-start(bf16[800,128]{1,0:T(8,128)(2,1)S(1)} %pad_maximum_fusion), channel_id=1, source_target_pairs={{0,480},{32,448},{64,416},{96,384},{128,352},{160,320},{192,288},{... | collective-permute-start | bytes 614408 | tf_op jit(solution)/shard_map/ppermute | solution.py:16
  14.2 0.7 reshape.60
  14.9 2.6 %collective-permute-done = bf16[800,128]{1,0:T(8,128)(2,1)S(1)} collective-permute-done((bf16[800,128]{1,0:T(8,128)(2,1)S(1)}, bf16[800,128]{1,0:T(8,128)(2,1)S(1)}, u32[]{:S(2)}, u32[]{:S(2)}) %collective-permute-start) | collective-permute-done | bytes 204832 | tf_op jit(solution)/shard_map/ppermute | solution.py:16
  18.0 25.3 %all_gather.9 = bf16[2,4,8,3584]{3,2,1,0:T(8,128)(2,1)S(1)} all-gather(bf16[2,1,8,3584]{3,2,1,0:T(8,128)(2,1)S(1)} %pad_maximum_fusion.1), channel_id=1, replica_groups=mesh['py'=4,'pz'=4,'dz'=4,'dx'=4,'dc'=2] {'dz'}, dimensions={1}, use_global_device_ids=true | all-gather | bytes 573440 | tf_op jit(solution)/shard_map/all_gather | solution.py:45
  43.3 12.0 %all-gather = bf16[1,4,32,3584]{3,2,1,0:T(8,128)(2,1)} all-gather(bf16[1,4,8,3584]{3,2,1,0:T(8,128)(2,1)S(1)} %get-tuple-element.4), channel_id=2, replica_groups=mesh['py'=4,'pz'=4,'dz'=4,'dx'=4,'dc'=2] {'dx'}, dimensions={2}, use_global_device_ids=true | all-gather | bytes 1146880 | tf_op jit(solution)/shard_map/all_gather | solution.py:51
  55.3 12.8 %all-gather.1 = bf16[1,4,32,3584]{3,2,1,0:T(8,128)(2,1)S(1)} all-gather(bf16[1,4,8,3584]{3,2,1,0:T(8,128)(2,1)S(1)} %get-tuple-element.5), channel_id=3, replica_groups=mesh['py'=4,'pz'=4,'dz'=4,'dx'=4,'dc'=2] {'dx'}, dimensions={2}, use_global_device_ids=true | all-gather | bytes 1146880 | tf_op jit(solution)/shard_map/all_gather | solution.py:51
  68.1 13.3 %collective-permute-start.2 = (bf16[4,4,8,3584]{3,2,1,0:T(8,128)(2,1)S(1)}, bf16[4,4,8,3584]{3,2,1,0:T(8,128)(2,1)}, u32[]{:S(2)}, u32[]{:S(2)}) collective-permute-start(bf16[4,4,8,3584]{3,2,1,0:T(8,128)(2,1)S(1)} %bitcast.79), channel_id=1, source_target_pairs={{0,1},{1,0},{2,3},{3,2},{4,5},{5,4},{6,7},{7,6},{8,9},{9,8},{10,11... | collective-permute-start | bytes 2752520 | tf_op jit(solution)/shard_map/ppermute | solution.py:52
  81.3 1.9 %collective-permute-start.1 = (bf16[4,4,8,3584]{3,2,1,0:T(8,128)(2,1)}, bf16[4,4,8,3584]{3,2,1,0:T(8,128)(2,1)}, u32[]{:S(2)}, u32[]{:S(2)}) collective-permute-start(bf16[4,4,8,3584]{3,2,1,0:T(8,128)(2,1)} %bitcast.3), channel_id=1, source_target_pairs={{0,1},{1,0},{2,3},{3,2},{4,5},{5,4},{6,7},{7,6},{8,9},{9,8},{10,11... | collective-permute-start | bytes 2752520 | tf_op jit(solution)/shard_map/ppermute | solution.py:52
  83.3 1.9 %fusion.33 = bf16[128,288]{0,1:T(8,128)(2,1)S(1)} fusion(bf16[128,3584]{1,0:T(8,128)(2,1)} %bitcast.1, bf16[1,288,3584]{2,1,0:T(8,128)(2,1)S(1)} %copy-done), kind=kOutput, calls=%fused_computation.22 | convolution fusion | flops 264314880 | bytes 3055616 | tf_op jit(solution)/shard_map/dot_general | solution.py:57
  85.1 0.7 fusion.27
  86.0 0.7 reshape.62
  86.7 0.7 reshape.61
  87.7 0.7 stack.37
  88.4 0.9 constant_dynamic-update-slice_fusion.3
  89.3 3.8 %fusion.41 = f32[288,3584]{1,0:T(8,128)} fusion(bf16[128,288]{1,0:T(8,128)(2,1)S(1)} %reshape.59, bf16[128,3584]{1,0:T(8,128)(2,1)} %bitcast.1), kind=kOutput, calls=%fused_computation.47 | convolution fusion | flops 264241152 | bytes 5120000 | tf_op jit(solution)/shard_map/dot_general | solution.py:60
  93.2 1.9 %fusion.24 = bf16[128,288]{0,1:T(8,128)(2,1)S(1)} fusion(bf16[128,3584]{1,0:T(8,128)(2,1)} %bitcast.9, bf16[1,288,3584]{2,1,0:T(8,128)(2,1)S(1)} %copy-done), kind=kOutput, calls=%fused_computation.19 | convolution fusion | flops 264314880 | bytes 3055616 | tf_op jit(solution)/shard_map/dot_general | solution.py:57
  95.1 0.8 copy.13
  95.8 1.6 %stack.38 = bf16[1,4,4,2,4,288]{5,4,3,2,1,0:T(4,128)(2,1)} reshape(bf16[128,288]{1,0:T(8,128)(2,1)} %copy.13) | data formatting | bytes 147456 | tf_op jit(solution)/shard_map/stack | solution.py:62
  97.4 1.9 %fusion.30 = bf16[128,288]{0,1:T(8,128)(2,1)S(1)} fusion(bf16[128,3584]{1,0:T(8,128)(2,1)} %bitcast.4, bf16[1,288,3584]{2,1,0:T(8,128)(2,1)S(1)} %copy-done), kind=kOutput, calls=%fused_computation.21 | convolution fusion | flops 264314880 | bytes 3055616 | tf_op jit(solution)/shard_map/dot_general | solution.py:57
  99.3 0.8 copy.10
  100.0 1.6 %stack.35 = bf16[1,4,4,2,4,288]{5,4,3,2,1,0:T(4,128)(2,1)} reshape(bf16[128,288]{1,0:T(8,128)(2,1)} %copy.10) | data formatting | bytes 147456 | tf_op jit(solution)/shard_map/stack | solution.py:62
  101.6 0.9 constant_dynamic-update-slice_fusion.2
  102.5 0.9 constant_dynamic-update-slice_fusion
  103.8 6.2 %collective-permute-start.3 = (bf16[2,128,288]{2,0,1:T(2,128)(2,1)S(1)}, bf16[2,128,288]{2,0,1:T(2,128)(2,1)S(1)}, u32[]{:S(2)}, u32[]{:S(2)}) collective-permute-start(bf16[2,128,288]{2,0,1:T(2,128)(2,1)S(1)} %bitcast.88), channel_id=1, source_target_pairs={{0,480},{32,448},{64,416},{96,384},{128,352},{160,320},{192,288},{... | collective-permute-start | bytes 442376 | tf_op jit(solution)/shard_map/ppermute | solution.py:16
  110.1 3.2 %convolution_add_fusion.2 = f32[288,3584]{1,0:T(8,128)S(1)} fusion(f32[288,3584]{1,0:T(8,128)} %fusion.41, bf16[128,288]{1,0:T(8,128)(2,1)S(1)} %copy-done.1, bf16[128,3584]{1,0:T(8,128)(2,1)} %bitcast.4), kind=kOutput, calls=%fused_computation.2 | convolution fusion | flops 265273344 | bytes 9248768 | tf_op jit(solution)/shard_map/dot_general | solution.py:60
  113.3 0.7 convolution_add_fusion.1
  114.1 3.4 %fusion.3 = bf16[1,288,3584]{2,1,0:T(8,128)(2,1)} fusion(f32[288,3584]{1,0:T(8,128)S(1)} %convolution_add_fusion.1, bf16[128,288]{1,0:T(8,128)(2,1)S(1)} %copy-done.2, bf16[128,3584]{1,0:T(8,128)(2,1)} %bitcast.9, bf16[1,288,3584]{2,1,0:T(8,128)(2,1)S(1)} %copy-done), kind=kOutput, calls=%fused_computation.6 | convolution fusion | flops 269402112 | bytes 9248768 | tf_op jit(solution)/shard_map/dot_general | solution.py:60
  117.7 0.6 maximum_bitcast_fusion
  118.3 1.1 copy.22
  (38 shorter events, 2.6 us)
Async XLA Ops:
  2.5 80.8 %copy-start = (bf16[1,288,3584]{2,1,0:T(8,128)(2,1)S(1)}, bf16[1,288,3584]{2,1,0:T(8,128)(2,1)}, u32[]{:S(2)}) copy-start(bf16[1,288,3584]{2,1,0:T(8,128)(2,1)} %param.6) | copy-start | bytes 6193156
  4.2 13.4 %collective-permute-start = (bf16[800,128]{1,0:T(8,128)(2,1)S(1)}, bf16[800,128]{1,0:T(8,128)(2,1)S(1)}, u32[]{:S(2)}, u32[]{:S(2)}) collective-permute-start(bf16[800,128]{1,0:T(8,128)(2,1)S(1)} %pad_maximum_fusion), channel_id=1, source_target_pairs={{0,480},{32,448},{64,416},{96,384},{128,352},{160,320},{192,288},{... | collective-permute-start | bytes 614408 | tf_op jit(solution)/shard_map/ppermute | solution.py:16
  68.1 25.1 %collective-permute-start.2 = (bf16[4,4,8,3584]{3,2,1,0:T(8,128)(2,1)S(1)}, bf16[4,4,8,3584]{3,2,1,0:T(8,128)(2,1)}, u32[]{:S(2)}, u32[]{:S(2)}) collective-permute-start(bf16[4,4,8,3584]{3,2,1,0:T(8,128)(2,1)S(1)} %bitcast.79), channel_id=1, source_target_pairs={{0,1},{1,0},{2,3},{3,2},{4,5},{5,4},{6,7},{7,6},{8,9},{9,8},{10,11... | collective-permute-start | bytes 2752520 | tf_op jit(solution)/shard_map/ppermute | solution.py:52
  81.3 16.1 %collective-permute-start.1 = (bf16[4,4,8,3584]{3,2,1,0:T(8,128)(2,1)}, bf16[4,4,8,3584]{3,2,1,0:T(8,128)(2,1)}, u32[]{:S(2)}, u32[]{:S(2)}) collective-permute-start(bf16[4,4,8,3584]{3,2,1,0:T(8,128)(2,1)} %bitcast.3), channel_id=1, source_target_pairs={{0,1},{1,0},{2,3},{3,2},{4,5},{5,4},{6,7},{7,6},{8,9},{9,8},{10,11... | collective-permute-start | bytes 2752520 | tf_op jit(solution)/shard_map/ppermute | solution.py:52
  93.2 16.9 %copy-start.1 = (bf16[128,288]{1,0:T(8,128)(2,1)S(1)}, bf16[128,288]{1,0:T(8,128)(2,1)}, u32[]{:S(2)}) copy-start(bf16[128,288]{1,0:T(8,128)(2,1)} %reshape.60) | copy-start | bytes 221188
  103.8 9.4 %copy-start.3 = (bf16[128,288]{1,0:T(8,128)(2,1)S(1)}, bf16[128,288]{1,0:T(8,128)(2,1)}, u32[]{:S(2)}) copy-start(bf16[128,288]{1,0:T(8,128)(2,1)} %reshape.61) | copy-start | bytes 221188
  103.8 13.9 %collective-permute-start.3 = (bf16[2,128,288]{2,0,1:T(2,128)(2,1)S(1)}, bf16[2,128,288]{2,0,1:T(2,128)(2,1)S(1)}, u32[]{:S(2)}, u32[]{:S(2)}) collective-permute-start(bf16[2,128,288]{2,0,1:T(2,128)(2,1)S(1)} %bitcast.88), channel_id=1, source_target_pairs={{0,480},{32,448},{64,416},{96,384},{128,352},{160,320},{192,288},{... | collective-permute-start | bytes 442376 | tf_op jit(solution)/shard_map/ppermute | solution.py:16
  113.2 0.9 copy-start.2

commit v9 on v7

--- a/solution.py
+++ b/solution.py
@@ -14,6 +14,14 @@
     count = lax.axis_size(PIPE)
     route = [(low, count - 1 - low) for low in range(count)]
     return lax.ppermute(block, PIPE, route)
+
+
+def mirror_pair(rows, acts):
+    lane = 128
+    flat = jnp.concatenate([rows.reshape(-1, lane), acts.reshape(-1, lane)], axis=0)
+    flat = mirror(flat)
+    split_at = rows.size // lane
+    return flat[:split_at].reshape(rows.shape), flat[split_at:].reshape(acts.shape)
 
 
 def gather_rows(block):
@@ -42,7 +50,7 @@
     live_rows = slot_index < counts
     masked = jnp.where(live_rows[..., None], grad_out, jnp.zeros_like(grad_out))
     own_weight = weights[0]
-    mirror_masked, mirror_hidden = mirror((masked[0, 1], hidden[0, 1]))
+    mirror_masked, mirror_hidden = mirror_pair(masked[0, 1], hidden[0, 1])
     both_masked = jnp.stack([masked[0, 0], mirror_masked], axis=0)
     both_hidden = jnp.stack([hidden[0, 0], mirror_hidden], axis=0)
     piece = gather_rows(both_masked.reshape(-1, full_width)).reshape(-1, full_width)

time: 111 us -> 108 us (0.973)
  the two profiles are of different devices: /device:TPU:1 before, /device:TPU:33 now
where the time goes in v9:
time: 108 us; the launch traced here: 107 us
  blocking collectives  54.7 us (51%)
  starting transfers between devices  19.7 us (18%)
  waiting for transfers between devices  13.5 us (12%)
  other arithmetic  6.66 us (6%)
  local copies, waits for them, and re-layouts  6.11 us (6%)
  matrix products  5.89 us (5%)
    all_gather x1, blocking collectives, gather_rows(): out = lax.all_gather(block, 'dz', axis=0)  31.4 us
    all_gather x1, blocking collectives, gather_rows(): lax.all_gather(out[..., :half], 'dx', axis=1)  12.6 us
    ppermute x2, starting transfers between devices, mirror(): return lax.ppermute(block, PIPE, route)  12 us
    ppermute x2, waiting for transfers between devices, mirror(): return lax.ppermute(block, PIPE, route)  10.9 us
    all_gather x1, blocking collectives, gather_rows(): lax.all_gather(out[..., half:], 'dx', axis=1)  10.7 us
    ppermute x1, starting transfers between devices, gather_rows(): other = lax.ppermute(out, 'dc', [(0, 1), (1, 0)])  7.7 us
    dot_general x1, matrix products, shards(): total = jnp.dot(acts.T, piece, preferred_element_type=jnp.float32)  4.64 us
    another operation x2, other arithmetic, gather_rows(): return jnp.stack([out, other], axis=0)  3.65 us
  transfers between devices with their start and end apart: 3, of which 3 were waited for; matrix products, arithmetic and copies ran while one was open for 6% of the time, Pallas kernels for 0%

profile of v9, /device:TPU:33, one launch (start us, length us, event | category | flops | bytes accessed | tf_op | source)
XLA Modules:
  0.0 107.4 jit_solution(3136634327815967515)
XLA Ops:
  0.6 1.0 fusion.15
  1.6 0.2 copy.17
  1.8 0.3 reshape_squeeze.7
  2.2 0.8 iota_compare_fusion
  2.9 1.0 broadcast_select_fusion
  4.0 6.0 %collective-permute-start = (bf16[800,128]{1,0:T(8,128)(2,1)S(1)}, bf16[800,128]{1,0:T(8,128)(2,1)S(1)}, u32[]{:S(2)}, u32[]{:S(2)}) collective-permute-start(bf16[800,128]{1,0:T(8,128)(2,1)S(1)} %pad_maximum_fusion.2), channel_id=1, source_target_pairs={{0,480},{32,448},{64,416},{96,384},{128,352},{160,320},{192,288},{... | collective-permute-start | bytes 614408 | tf_op jit(solution)/shard_map/ppermute | solution.py:16
  10.0 8.1 %collective-permute-done = bf16[800,128]{1,0:T(8,128)(2,1)S(1)} collective-permute-done((bf16[800,128]{1,0:T(8,128)(2,1)S(1)}, bf16[800,128]{1,0:T(8,128)(2,1)S(1)}, u32[]{:S(2)}, u32[]{:S(2)}) %collective-permute-start) | collective-permute-done | bytes 204832 | tf_op jit(solution)/shard_map/ppermute | solution.py:16
  18.3 31.4 %all_gather.15 = bf16[4,16,3584]{2,1,0:T(8,128)(2,1)S(1)} all-gather(bf16[1,16,3584]{2,1,0:T(8,128)(2,1)S(1)} %all_gather_reshape.3), channel_id=1, replica_groups=mesh['py'=4,'pz'=4,'dz'=4,'dx'=4,'dc'=2] {'dz'}, dimensions={0}, use_global_device_ids=true | all-gather | bytes 573440 | tf_op jit(solution)/shard_map/all_gather | solution.py:29
  49.8 12.6 %all-gather = bf16[4,64,1792]{2,1,0:T(8,128)(2,1)S(1)} all-gather(bf16[4,16,1792]{2,1,0:T(8,128)(2,1)S(1)} %get-tuple-element.8), channel_id=2, replica_groups=mesh['py'=4,'pz'=4,'dz'=4,'dx'=4,'dc'=2] {'dx'}, dimensions={1}, use_global_device_ids=true | all-gather | bytes 1146880 | tf_op jit(solution)/shard_map/all_gather | solution.py:31
  62.4 10.7 %all-gather.1 = bf16[4,64,1792]{2,1,0:T(8,128)(2,1)S(1)} all-gather(bf16[4,16,1792]{2,1,0:T(8,128)(2,1)S(1)} %get-tuple-element.9), channel_id=3, replica_groups=mesh['py'=4,'pz'=4,'dz'=4,'dx'=4,'dc'=2] {'dx'}, dimensions={1}, use_global_device_ids=true | all-gather | bytes 1146880 | tf_op jit(solution)/shard_map/all_gather | solution.py:31
  73.0 1.7 %fusion.12 = (bf16[1,4,4,16,3584]{4,3,2,1,0:T(8,128)(2,1)S(1)}, bf16[4,4,16,3584]{3,2,1,0:T(8,128)(2,1)}) fusion(bf16[4,4,16,1792]{3,2,1,0:T(8,128)(2,1)S(1)} %bitcast.37, bf16[4,4,16,1792]{3,2,1,0:T(8,128)(2,1)S(1)} %bitcast.36), kind=kLoop, calls=%fused_computation.20 | loop fusion | flops 3670016 | bytes 5505024 | tf_op jit(solution)/shard_map/stack | solution.py:34
  74.7 7.7 %collective-permute-start.1 = (bf16[4,4,16,3584]{3,2,1,0:T(8,128)(2,1)}, bf16[4,4,16,3584]{3,2,1,0:T(8,128)(2,1)}, u32[]{:S(2)}, u32[]{:S(2)}) collective-permute-start(bf16[4,4,16,3584]{3,2,1,0:T(8,128)(2,1)} %get-tuple-element.7), channel_id=1, source_target_pairs={{0,1},{1,0},{2,3},{3,2},{4,5},{5,4},{6,7},{7,6},{8,9},{9,8},{10,11... | collective-permute-start | bytes 5505032 | tf_op jit(solution)/shard_map/ppermute | solution.py:33
  82.4 0.2 copy.21
  82.7 0.3 stack.32
  83.0 0.2 maximum_bitcast_fusion.1
  83.2 0.2 reverse_select_fusion
  83.4 0.2 reshape.33
  83.6 2.5 %collective-permute-done.1 = bf16[4,4,16,3584]{3,2,1,0:T(8,128)(2,1)} collective-permute-done((bf16[4,4,16,3584]{3,2,1,0:T(8,128)(2,1)}, bf16[4,4,16,3584]{3,2,1,0:T(8,128)(2,1)}, u32[]{:S(2)}, u32[]{:S(2)}) %collective-permute-start.1) | collective-permute-done | bytes 1835040 | tf_op jit(solution)/shard_map/ppermute | solution.py:33
  86.2 2.0 %pad_maximum_fusion = bf16[2,4,4,16,3584]{4,3,2,1,0:T(8,128)(2,1)S(1)} fusion(bf16[1,4,4,16,3584]{4,3,2,1,0:T(8,128)(2,1)} %bitcast.5, bf16[1,4,4,16,3584]{4,3,2,1,0:T(8,128)(2,1)S(1)} %get-tuple-element.6), kind=kLoop, calls=%fused_computation.4 | loop fusion | flops 1835008 | bytes 7340032 | tf_op jit(solution)/shard_map/stack | solution.py:34
  88.1 1.8 %copy-done = bf16[2,4,4,16,3584]{4,3,2,1,0:T(8,128)(2,1)} copy-done((bf16[2,4,4,16,3584]{4,3,2,1,0:T(8,128)(2,1)}, bf16[2,4,4,16,3584]{4,3,2,1,0:T(8,128)(2,1)S(1)}, u32[]{:S(2)}) %copy-start) | copy-done | bytes 3670040
  89.9 1.3 %fusion.8 = bf16[512,288]{0,1:T(8,128)(2,1)S(1)} fusion(bf16[512,3584]{1,0:T(8,128)(2,1)S(1)} %bitcast.34, bf16[1,288,3584]{2,1,0:T(8,128)(2,1)S(1)} %copy-done.1), kind=kOutput, calls=%fused_computation.9 | convolution fusion | flops 1057259520 | bytes 6029312 | tf_op jit(solution)/shard_map/dot_general | solution.py:59
  91.2 0.2 copy.18
  91.4 0.1 reshape.32
  91.5 0.2 fusion.11
  91.7 0.1 fusion.14
  91.9 0.2 copy.20
  92.0 6.0 %collective-permute-start.2 = (bf16[2,128,288]{2,0,1:T(2,128)(2,1)S(1)}, bf16[2,128,288]{2,0,1:T(2,128)(2,1)S(1)}, u32[]{:S(2)}, u32[]{:S(2)}) collective-permute-start(bf16[2,128,288]{2,0,1:T(2,128)(2,1)S(1)} %bitcast.40), channel_id=1, source_target_pairs={{0,480},{32,448},{64,416},{96,384},{128,352},{160,320},{192,288},{... | collective-permute-start | bytes 442376 | tf_op jit(solution)/shard_map/ppermute | solution.py:16
  98.1 4.6 %fusion.2 = bf16[1,288,3584]{2,1,0:T(8,128)(2,1)} fusion(bf16[512,288]{1,0:T(8,128)(2,1)S(1)} %reshape.33, bf16[512,3584]{1,0:T(8,128)(2,1)} %bitcast.35, bf16[1,288,3584]{2,1,0:T(8,128)(2,1)S(1)} %copy-done.2), kind=kOutput, calls=%fused_computation.3 | convolution fusion | flops 1061093376 | bytes 8093696 | tf_op jit(solution)/shard_map/dot_general | solution.py:63
  102.7 0.2 copy.19
  102.9 2.8 %collective-permute-done.2 = bf16[2,128,288]{2,0,1:T(2,128)(2,1)S(1)} collective-permute-done((bf16[2,128,288]{2,0,1:T(2,128)(2,1)S(1)}, bf16[2,128,288]{2,0,1:T(2,128)(2,1)S(1)}, u32[]{:S(2)}, u32[]{:S(2)}) %collective-permute-start.2) | collective-permute-done | bytes 147488 | tf_op jit(solution)/shard_map/ppermute | solution.py:16
  105.7 0.6 maximum_bitcast_fusion
  106.3 1.1 %copy.24 = bf16[1,2,2,128,288]{3,4,2,1,0:T(8,128)(2,1)} copy(bf16[1,2,2,128,288]{4,2,3,1,0:T(2,128)(2,1)S(1)} %maximum_bitcast_fusion) | data formatting | bytes 589824
  (15 shorter events, 0.4 us)
Async XLA Ops:
  4.0 14.1 %collective-permute-start = (bf16[800,128]{1,0:T(8,128)(2,1)S(1)}, bf16[800,128]{1,0:T(8,128)(2,1)S(1)}, u32[]{:S(2)}, u32[]{:S(2)}) collective-permute-start(bf16[800,128]{1,0:T(8,128)(2,1)S(1)} %pad_maximum_fusion.2), channel_id=1, source_target_pairs={{0,480},{32,448},{64,416},{96,384},{128,352},{160,320},{192,288},{... | collective-permute-start | bytes 614408 | tf_op jit(solution)/shard_map/ppermute | solution.py:16
  74.7 11.4 %collective-permute-start.1 = (bf16[4,4,16,3584]{3,2,1,0:T(8,128)(2,1)}, bf16[4,4,16,3584]{3,2,1,0:T(8,128)(2,1)}, u32[]{:S(2)}, u32[]{:S(2)}) collective-permute-start(bf16[4,4,16,3584]{3,2,1,0:T(8,128)(2,1)} %get-tuple-element.7), channel_id=1, source_target_pairs={{0,1},{1,0},{2,3},{3,2},{4,5},{5,4},{6,7},{7,6},{8,9},{9,8},{10,11... | collective-permute-start | bytes 5505032 | tf_op jit(solution)/shard_map/ppermute | solution.py:33
  86.1 3.8 %copy-start.1 = (bf16[1,288,3584]{2,1,0:T(8,128)(2,1)S(1)}, bf16[1,288,3584]{2,1,0:T(8,128)(2,1)}, u32[]{:S(2)}) copy-start(bf16[1,288,3584]{2,1,0:T(8,128)(2,1)} %param.6) | copy-start | bytes 6193156
  88.1 1.8 %copy-start = (bf16[2,4,4,16,3584]{4,3,2,1,0:T(8,128)(2,1)}, bf16[2,4,4,16,3584]{4,3,2,1,0:T(8,128)(2,1)S(1)}, u32[]{:S(2)}) copy-start(bf16[2,4,4,16,3584]{4,3,2,1,0:T(8,128)(2,1)S(1)} %pad_maximum_fusion) | copy-start | bytes 11010052
  89.9 8.1 %copy-start.2 = (bf16[1,288,3584]{2,1,0:T(8,128)(2,1)S(1)}, bf16[1,288,3584]{2,1,0:T(8,128)(2,1)}, u32[]{:S(2)}) copy-start(bf16[1,288,3584]{2,1,0:T(8,128)(2,1)} %param.6) | copy-start | bytes 6193156
  92.0 13.6 %collective-permute-start.2 = (bf16[2,128,288]{2,0,1:T(2,128)(2,1)S(1)}, bf16[2,128,288]{2,0,1:T(2,128)(2,1)S(1)}, u32[]{:S(2)}, u32[]{:S(2)}) collective-permute-start(bf16[2,128,288]{2,0,1:T(2,128)(2,1)S(1)} %bitcast.40), channel_id=1, source_target_pairs={{0,480},{32,448},{64,416},{96,384},{128,352},{160,320},{192,288},{... | collective-permute-start | bytes 442376 | tf_op jit(solution)/shard_map/ppermute | solution.py:16

commit v10 on v9

--- a/solution.py
+++ b/solution.py
@@ -31,7 +31,7 @@
         [lax.all_gather(out[..., :half], "dx", axis=1), lax.all_gather(out[..., half:], "dx", axis=1)], axis=-1
     )
     other = lax.ppermute(out, "dc", [(0, 1), (1, 0)])
-    return jnp.stack([out, other], axis=0)
+    return out, other
 
 
 def own_first(array):
@@ -53,14 +53,18 @@
     mirror_masked, mirror_hidden = mirror_pair(masked[0, 1], hidden[0, 1])
     both_masked = jnp.stack([masked[0, 0], mirror_masked], axis=0)
     both_hidden = jnp.stack([hidden[0, 0], mirror_hidden], axis=0)
-    piece = gather_rows(both_masked.reshape(-1, full_width)).reshape(-1, full_width)
+    pieces = [piece.reshape(-1, full_width) for piece in gather_rows(both_masked.reshape(-1, full_width))]
     acts = both_hidden.reshape(2, micro, n_z, n_x, n_c, row_total, share).transpose(4, 2, 3, 0, 1, 5, 6)
-    acts = own_first(acts).reshape(-1, share)
-    grad = jnp.dot(piece, own_weight.T, preferred_element_type=jnp.float32)
-    grad = (grad * scale_factor).astype(jnp.bfloat16)
-    grad = own_first(grad.reshape(n_c, n_z, n_x, 2, micro, row_total, share))
+    acts = own_first(acts).reshape(n_c, -1, share)
+    grads = []
+    total = None
+    for index, piece in enumerate(pieces):
+        grad = jnp.dot(piece, own_weight.T, preferred_element_type=jnp.float32)
+        grads.append((grad * scale_factor).astype(jnp.bfloat16))
+        part = jnp.dot(acts[index].T, piece, preferred_element_type=jnp.float32)
+        total = part if total is None else total + part
+    grad = own_first(jnp.stack(grads, axis=0).reshape(n_c, n_z, n_x, 2, micro, row_total, share))
     grad = grad.transpose(3, 4, 1, 2, 0, 5, 6).reshape(2, micro, tokens, share)
-    total = jnp.dot(acts.T, piece, preferred_element_type=jnp.float32)
     gradient = total * scale_factor
     new_weight = (own_weight.astype(jnp.float32) - step_rate * gradient).astype(jnp.bfloat16)
     returned = mirror(grad[1])

time: 108 us -> 105 us (0.972)
  matrix products: 5.89 us -> 9.64 us
  other arithmetic: 6.66 us -> 3.21 us
  waiting for transfers between devices: 13.5 us -> 11.2 us
  local copies, waits for them, and re-layouts: 6.11 us -> 4.72 us
    dot_general x1 -> x2, matrix products: 1.25 us -> 5.16 us  [shards(): grad = jnp.dot(piece, own_weight.T, preferred_element_type=jnp.float32)]
    another operation x2 -> x0, other arithmetic: 3.65 us -> none  [gather_rows(): return jnp.stack([out, other], axis=0)]
    ppermute x1, waiting for transfers between devices: 2.55 us -> 0.1 us  [gather_rows(): other = lax.ppermute(out, 'dc', [(0, 1), (1, 0)])]
    unnamed x7 -> x4, local copies, waits for them, and re-layouts: 2.9 us -> 1.17 us
    dot_general x1 -> x2, matrix products: 4.64 us -> 4.48 us  [shards(): part = jnp.dot(acts[index].T, piece, preferred_element_type=jnp.float32)]
  transfers between devices with their start and end apart: 3 -> 3, of which waited for: 3 -> 3; matrix products, arithmetic and copies ran while one was open for 6% -> 8% of each run, Pallas kernels for 0% -> 0%
where the time goes in v10:
time: 105 us; the launch traced here: 104 us
  blocking collectives  54.7 us (52%)
  starting transfers between devices  19.9 us (19%)
  waiting for transfers between devices  11.2 us (11%)
  matrix products  9.64 us (9%)
  local copies, waits for them, and re-layouts  4.72 us (4%)
  other arithmetic  3.21 us (3%)
    all_gather x1, blocking collectives, gather_rows(): out = lax.all_gather(block, 'dz', axis=0)  31.4 us
    all_gather x1, blocking collectives, gather_rows(): lax.all_gather(out[..., :half], 'dx', axis=1)  12.6 us
    ppermute x2, starting transfers between devices, mirror(): return lax.ppermute(block, PIPE, route)  12.1 us
    ppermute x2, waiting for transfers between devices, mirror(): return lax.ppermute(block, PIPE, route)  11.1 us
    all_gather x1, blocking collectives, gather_rows(): lax.all_gather(out[..., half:], 'dx', axis=1)  10.7 us
    ppermute x1, starting transfers between devices, gather_rows(): other = lax.ppermute(out, 'dc', [(0, 1), (1, 0)])  7.71 us
    dot_general x2, matrix products, shards(): grad = jnp.dot(piece, own_weight.T, preferred_element_type=jnp.float32)  5.16 us
    dot_general x2, matrix products, shards(): part = jnp.dot(acts[index].T, piece, preferred_element_type=jnp.float32)  4.48 us
  transfers between devices with their start and end apart: 3, of which 3 were waited for; matrix products, arithmetic and copies ran while one was open for 8% of the time, Pallas kernels for 0%

profile of v10, /device:TPU:33, one launch (start us, length us, event | category | flops | bytes accessed | tf_op | source)
XLA Modules:
  0.0 104.2 jit_solution(14136898800093196920)
XLA Ops:
  0.6 0.8 iota_compare_fusion
  1.4 1.0 broadcast_select_fusion
  2.5 1.0 fusion.24
  3.5 0.2 copy.18
  3.7 0.3 reshape_squeeze.7
  4.0 6.0 %collective-permute-start = (bf16[800,128]{1,0:T(8,128)(2,1)S(1)}, bf16[800,128]{1,0:T(8,128)(2,1)S(1)}, u32[]{:S(2)}, u32[]{:S(2)}) collective-permute-start(bf16[800,128]{1,0:T(8,128)(2,1)S(1)} %pad_maximum_fusion.1), channel_id=1, source_target_pairs={{0,480},{32,448},{64,416},{96,384},{128,352},{160,320},{192,288},{... | collective-permute-start | bytes 614408 | tf_op jit(solution)/shard_map/ppermute | solution.py:16
  10.0 8.1 %collective-permute-done = bf16[800,128]{1,0:T(8,128)(2,1)S(1)} collective-permute-done((bf16[800,128]{1,0:T(8,128)(2,1)S(1)}, bf16[800,128]{1,0:T(8,128)(2,1)S(1)}, u32[]{:S(2)}, u32[]{:S(2)}) %collective-permute-start) | collective-permute-done | bytes 204832 | tf_op jit(solution)/shard_map/ppermute | solution.py:16
  18.3 31.4 %all_gather.15 = bf16[4,16,3584]{2,1,0:T(8,128)(2,1)S(1)} all-gather(bf16[1,16,3584]{2,1,0:T(8,128)(2,1)S(1)} %all_gather_reshape.3), channel_id=1, replica_groups=mesh['py'=4,'pz'=4,'dz'=4,'dx'=4,'dc'=2] {'dz'}, dimensions={0}, use_global_device_ids=true | all-gather | bytes 573440 | tf_op jit(solution)/shard_map/all_gather | solution.py:29
  49.8 12.6 %all-gather = bf16[4,64,1792]{2,1,0:T(8,128)(2,1)S(1)} all-gather(bf16[4,16,1792]{2,1,0:T(8,128)(2,1)S(1)} %get-tuple-element.6), channel_id=2, replica_groups=mesh['py'=4,'pz'=4,'dz'=4,'dx'=4,'dc'=2] {'dx'}, dimensions={1}, use_global_device_ids=true | all-gather | bytes 1146880 | tf_op jit(solution)/shard_map/all_gather | solution.py:31
  62.4 10.7 %all-gather.1 = bf16[4,64,1792]{2,1,0:T(8,128)(2,1)S(1)} all-gather(bf16[4,16,1792]{2,1,0:T(8,128)(2,1)S(1)} %get-tuple-element.7), channel_id=3, replica_groups=mesh['py'=4,'pz'=4,'dz'=4,'dx'=4,'dc'=2] {'dx'}, dimensions={1}, use_global_device_ids=true | all-gather | bytes 1146880 | tf_op jit(solution)/shard_map/all_gather | solution.py:31
  73.0 0.2 pad_maximum_fusion
  73.2 7.7 %collective-permute-start.1 = (bf16[4,4,16,3584]{3,2,1,0:T(8,128)(2,1)S(1)}, bf16[4,4,16,3584]{3,2,1,0:T(8,128)(2,1)}, u32[]{:S(2)}, u32[]{:S(2)}) collective-permute-start(bf16[4,4,16,3584]{3,2,1,0:T(8,128)(2,1)S(1)} %pad_maximum_fusion), channel_id=1, source_target_pairs={{0,1},{1,0},{2,3},{3,2},{4,5},{5,4},{6,7},{7,6},{8,9},{9,8},{10,11... | collective-permute-start | bytes 5505032 | tf_op jit(solution)/shard_map/ppermute | solution.py:33
  81.0 0.2 copy.23
  81.3 0.3 stack.32
  81.5 2.3 %fusion.17 = bf16[256,288]{0,1:T(8,128)(2,1)S(1)} fusion(bf16[256,3584]{1,0:T(8,128)(2,1)S(1)} %bitcast.41, bf16[1,288,3584]{2,1,0:T(8,128)(2,1)} %param.6), kind=kOutput, calls=%fused_computation.13 | convolution fusion | flops 528629760 | bytes 4046848 | tf_op jit(solution)/shard_map/dot_general | solution.py:62
  83.9 0.2 copy.19
  84.2 0.2 maximum_bitcast_fusion.1
  84.4 0.1 collective-permute-done.1
  84.5 2.9 %fusion.14 = bf16[256,288]{0,1:T(8,128)(2,1)S(1)} fusion(bf16[256,3584]{1,0:T(8,128)(2,1)} %bitcast.6, bf16[1,288,3584]{2,1,0:T(8,128)(2,1)} %param.6), kind=kOutput, calls=%fused_computation.12 | convolution fusion | flops 528629760 | bytes 4046848 | tf_op jit(solution)/shard_map/dot_general | solution.py:62
  87.3 0.2 copy.20
  87.6 0.1 constant_dynamic-update-slice_fusion
  87.7 0.4 reverse_select_fusion
  88.1 0.1 fusion.22
  88.4 0.1 fusion.23
  88.5 0.2 copy.22
  88.7 6.1 %collective-permute-start.2 = (bf16[2,128,288]{2,0,1:T(2,128)(2,1)S(1)}, bf16[2,128,288]{2,0,1:T(2,128)(2,1)S(1)}, u32[]{:S(2)}, u32[]{:S(2)}) collective-permute-start(bf16[2,128,288]{2,0,1:T(2,128)(2,1)S(1)} %bitcast.47), channel_id=1, source_target_pairs={{0,480},{32,448},{64,416},{96,384},{128,352},{160,320},{192,288},{... | collective-permute-start | bytes 442376 | tf_op jit(solution)/shard_map/ppermute | solution.py:16
  94.9 0.7 fusion.25
  95.6 3.8 %fusion.3 = bf16[1,288,3584]{2,1,0:T(8,128)(2,1)} fusion(f32[288,3584]{1,0:T(8,128)S(1)} %fusion.25, bf16[256,288]{1,0:T(8,128)(2,1)S(1)} %squeeze.15, bf16[256,3584]{1,0:T(8,128)(2,1)} %bitcast.6, bf16[1,288,3584]{2,1,0:T(8,128)(2,1)S(1)} %copy-done), kind=kOutput, calls=%fused_computation.4 | convolution fusion | flops 533643264 | bytes 10240000 | tf_op jit(solution)/shard_map/dot_general | solution.py:64
  99.4 0.2 copy.21
  99.5 3.0 %collective-permute-done.2 = bf16[2,128,288]{2,0,1:T(2,128)(2,1)S(1)} collective-permute-done((bf16[2,128,288]{2,0,1:T(2,128)(2,1)S(1)}, bf16[2,128,288]{2,0,1:T(2,128)(2,1)S(1)}, u32[]{:S(2)}, u32[]{:S(2)}) %collective-permute-start.2) | collective-permute-done | bytes 147488 | tf_op jit(solution)/shard_map/ppermute | solution.py:16
  102.5 0.6 maximum_bitcast_fusion
  103.1 1.1 %copy.26 = bf16[1,2,2,128,288]{3,4,2,1,0:T(8,128)(2,1)} copy(bf16[1,2,2,128,288]{4,2,3,1,0:T(2,128)(2,1)S(1)} %maximum_bitcast_fusion) | data formatting | bytes 589824
  (17 shorter events, 0.7 us)
Async XLA Ops:
  4.0 14.1 %collective-permute-start = (bf16[800,128]{1,0:T(8,128)(2,1)S(1)}, bf16[800,128]{1,0:T(8,128)(2,1)S(1)}, u32[]{:S(2)}, u32[]{:S(2)}) collective-permute-start(bf16[800,128]{1,0:T(8,128)(2,1)S(1)} %pad_maximum_fusion.1), channel_id=1, source_target_pairs={{0,480},{32,448},{64,416},{96,384},{128,352},{160,320},{192,288},{... | collective-permute-start | bytes 614408 | tf_op jit(solution)/shard_map/ppermute | solution.py:16
  73.2 11.2 %collective-permute-start.1 = (bf16[4,4,16,3584]{3,2,1,0:T(8,128)(2,1)S(1)}, bf16[4,4,16,3584]{3,2,1,0:T(8,128)(2,1)}, u32[]{:S(2)}, u32[]{:S(2)}) collective-permute-start(bf16[4,4,16,3584]{3,2,1,0:T(8,128)(2,1)S(1)} %pad_maximum_fusion), channel_id=1, source_target_pairs={{0,1},{1,0},{2,3},{3,2},{4,5},{5,4},{6,7},{7,6},{8,9},{9,8},{10,11... | collective-permute-start | bytes 5505032 | tf_op jit(solution)/shard_map/ppermute | solution.py:33
  88.7 6.9 %copy-start = (bf16[1,288,3584]{2,1,0:T(8,128)(2,1)S(1)}, bf16[1,288,3584]{2,1,0:T(8,128)(2,1)}, u32[]{:S(2)}) copy-start(bf16[1,288,3584]{2,1,0:T(8,128)(2,1)} %param.6) | copy-start | bytes 6193156
  88.7 13.8 %collective-permute-start.2 = (bf16[2,128,288]{2,0,1:T(2,128)(2,1)S(1)}, bf16[2,128,288]{2,0,1:T(2,128)(2,1)S(1)}, u32[]{:S(2)}, u32[]{:S(2)}) collective-permute-start(bf16[2,128,288]{2,0,1:T(2,128)(2,1)S(1)} %bitcast.47), channel_id=1, source_target_pairs={{0,480},{32,448},{64,416},{96,384},{128,352},{160,320},{192,288},{... | collective-permute-start | bytes 442376 | tf_op jit(solution)/shard_map/ppermute | solution.py:16

commit v11 on v10

--- a/solution.py
+++ b/solution.py
@@ -24,16 +24,6 @@
     return flat[:split_at].reshape(rows.shape), flat[split_at:].reshape(acts.shape)
 
 
-def gather_rows(block):
-    half = block.shape[-1] // 2
-    out = lax.all_gather(block, "dz", axis=0)
-    out = jnp.concatenate(
-        [lax.all_gather(out[..., :half], "dx", axis=1), lax.all_gather(out[..., half:], "dx", axis=1)], axis=-1
-    )
-    other = lax.ppermute(out, "dc", [(0, 1), (1, 0)])
-    return out, other
-
-
 def own_first(array):
     return jnp.where(lax.axis_index("dc") == 0, array, array[::-1])
 
@@ -50,11 +40,16 @@
     live_rows = slot_index < counts
     masked = jnp.where(live_rows[..., None], grad_out, jnp.zeros_like(grad_out))
     own_weight = weights[0]
-    mirror_masked, mirror_hidden = mirror_pair(masked[0, 1], hidden[0, 1])
-    both_masked = jnp.stack([masked[0, 0], mirror_masked], axis=0)
+    own_rows = jnp.stack([masked[0, 0], masked[0, 1]], axis=0).reshape(2, -1, full_width)
+    own_rows = lax.all_gather(own_rows, "dz", axis=1)
+    mirror_rows, mirror_hidden = mirror_pair(own_rows[1], hidden[0, 1])
+    both_rows = jnp.stack(
+        [lax.all_gather(own_rows[0], "dx", axis=1), lax.all_gather(mirror_rows, "dx", axis=1)], axis=0
+    )
+    other_rows = lax.ppermute(both_rows, "dc", [(0, 1), (1, 0)])
     both_hidden = jnp.stack([hidden[0, 0], mirror_hidden], axis=0)
-    pieces = [piece.reshape(-1, full_width) for piece in gather_rows(both_masked.reshape(-1, full_width))]
-    acts = both_hidden.reshape(2, micro, n_z, n_x, n_c, row_total, share).transpose(4, 2, 3, 0, 1, 5, 6)
+    pieces = [both_rows.reshape(-1, full_width), other_rows.reshape(-1, full_width)]
+    acts = both_hidden.reshape(2, micro, n_z, n_x, n_c, row_total, share).transpose(4, 0, 2, 3, 1, 5, 6)
     acts = own_first(acts).reshape(n_c, -1, share)
     grads = []
     total = None
@@ -63,8 +58,8 @@
         grads.append((grad * scale_factor).astype(jnp.bfloat16))
         part = jnp.dot(acts[index].T, piece, preferred_element_type=jnp.float32)
         total = part if total is None else total + part
-    grad = own_first(jnp.stack(grads, axis=0).reshape(n_c, n_z, n_x, 2, micro, row_total, share))
-    grad = grad.transpose(3, 4, 1, 2, 0, 5, 6).reshape(2, micro, tokens, share)
+    grad = own_first(jnp.stack(grads, axis=0).reshape(n_c, 2, n_z, n_x, micro, row_total, share))
+    grad = grad.transpose(1, 4, 2, 3, 0, 5, 6).reshape(2, micro, tokens, share)
     gradient = total * scale_factor
     new_weight = (own_weight.astype(jnp.float32) - step_rate * gradient).astype(jnp.bfloat16)
     returned = mirror(grad[1])

time: 105 us -> 98 us (0.933)
  the two profiles are of different devices: /device:TPU:33 before, /device:TPU:1 now
where the time goes in v11:
time: 98 us; the launch traced here: 97.7 us
  blocking collectives  54.1 us (55%)
  starting transfers between devices  20.4 us (21%)
  matrix products  9.65 us (10%)
  local copies, waits for them, and re-layouts  5.27 us (5%)
  waiting for transfers between devices  4.27 us (4%)
  other arithmetic  3.12 us (3%)
    all_gather x1, blocking collectives, shards(): own_rows = lax.all_gather(own_rows, 'dz', axis=1)  29.5 us
    all_gather x1, blocking collectives, shards(): lax.all_gather(own_rows[0], 'dx', axis=1)  12.5 us
    all_gather x1, blocking collectives, shards(): lax.all_gather(mirror_rows, 'dx', axis=1)  12.1 us
    ppermute x1, starting transfers between devices, shards(): other_rows = lax.ppermute(both_rows, 'dc', [(0, 1), (1, 0)])  11 us
    ppermute x2, starting transfers between devices, mirror(): return lax.ppermute(block, PIPE, route)  9.37 us
    dot_general x2, matrix products, shards(): grad = jnp.dot(piece, own_weight.T, preferred_element_type=jnp.float32)  5.18 us
    dot_general x2, matrix products, shards(): part = jnp.dot(acts[index].T, piece, preferred_element_type=jnp.float32)  4.48 us
    ppermute x2, waiting for transfers between devices, mirror(): return lax.ppermute(block, PIPE, route)  4.18 us
  transfers between devices with their start and end apart: 3, of which 2 were waited for; matrix products, arithmetic and copies ran while one was open for 8% of the time, Pallas kernels for 0%

profile of v11, /device:TPU:1, one launch (start us, length us, event | category | flops | bytes accessed | tf_op | source)
XLA Modules:
  0.0 97.7 jit_solution(13387137621817129531)
XLA Ops:
  0.6 0.8 iota_compare_fusion
  1.4 1.0 %broadcast_select_fusion = bf16[1,2,2,4,3584]{4,3,2,1,0:T(4,128)(2,1)S(1)} fusion(bf16[1,2,2,4,3584]{4,3,2,1,0:T(4,128)(2,1)} %param.4, pred[2,2,4]{2,1,0:T(4,128)(4,1)S(1)} %iota_compare_fusion), kind=kLoop, calls=%fused_computation.21 | loop fusion | flops 57344 | bytes 229392 | tf_op jit(solution)/shard_map/jit(_where)/select_n | solution.py:41
  2.5 1.0 %fusion.24 = (bf16[1,1,2,128,288]{3,4,2,1,0:T(8,128)(2,1)S(1)}, bf16[1,1,2,128,288]{3,4,2,1,0:T(8,128)(2,1)S(1)}) fusion(bf16[1,2,2,128,288]{3,4,2,1,0:T(8,128)(2,1)} %param.5), kind=kLoop, calls=%fused_computation.28 | loop fusion | bytes 589824 | tf_op jit(solution)/shard_map/slice | solution.py:50
  3.5 0.2 copy.20
  3.7 0.3 reshape_squeeze.7
  4.1 29.5 %all_gather.9 = bf16[2,4,8,3584]{3,2,1,0:T(8,128)(2,1)S(1)} all-gather(bf16[2,1,8,3584]{3,2,1,0:T(8,128)(2,1)S(1)} %pad_maximum_fusion.2), channel_id=1, replica_groups=mesh['py'=4,'pz'=4,'dz'=4,'dx'=4,'dc'=2] {'dz'}, dimensions={1}, use_global_device_ids=true | all-gather | bytes 573440 | tf_op jit(solution)/shard_map/all_gather | solution.py:44
  33.6 0.3 reshape_squeeze.6
  34.0 6.1 %collective-permute-start = (bf16[1472,128]{1,0:T(8,128)(2,1)S(1)}, bf16[1472,128]{1,0:T(8,128)(2,1)S(1)}, u32[]{:S(2)}, u32[]{:S(2)}) collective-permute-start(bf16[1472,128]{1,0:T(8,128)(2,1)S(1)} %pad_maximum_fusion.1), channel_id=1, source_target_pairs={{0,480},{32,448},{64,416},{96,384},{128,352},{160,320},{192,288},{... | collective-permute-start | bytes 1130504 | tf_op jit(solution)/shard_map/ppermute | solution.py:16
  40.1 12.5 %all-gather = bf16[1,4,32,3584]{3,2,1,0:T(8,128)(2,1)S(1)} all-gather(bf16[1,4,8,3584]{3,2,1,0:T(8,128)(2,1)S(1)} %get-tuple-element.6), channel_id=2, replica_groups=mesh['py'=4,'pz'=4,'dz'=4,'dx'=4,'dc'=2] {'dx'}, dimensions={2}, use_global_device_ids=true | all-gather | bytes 1146880 | tf_op jit(solution)/shard_map/all_gather | solution.py:47
  52.6 0.3 all_gather_reshape.4
  52.8 12.1 %all_gather.11 = bf16[4,4,8,3584]{3,2,1,0:T(8,128)(2,1)S(1)} all-gather(bf16[4,1,8,3584]{3,2,1,0:T(8,128)(2,1)S(1)} %all_gather_reshape.4), channel_id=1, replica_groups=mesh['py'=4,'pz'=4,'dz'=4,'dx'=4,'dc'=2] {'dx'}, dimensions={1}, use_global_device_ids=true | all-gather | bytes 1146880 | tf_op jit(solution)/shard_map/all_gather | solution.py:47
  64.9 0.2 pad_maximum_fusion
  65.1 11.0 %collective-permute-start.1 = (bf16[2,4,4,8,3584]{4,3,2,1,0:T(8,128)(2,1)S(1)}, bf16[2,4,4,8,3584]{4,3,2,1,0:T(8,128)(2,1)}, u32[]{:S(2)}, u32[]{:S(2)}) collective-permute-start(bf16[2,4,4,8,3584]{4,3,2,1,0:T(8,128)(2,1)S(1)} %pad_maximum_fusion), channel_id=1, source_target_pairs={{0,1},{1,0},{2,3},{3,2},{4,5},{5,4},{6,7},{7,6},{8,9},{9,8},{10,11... | collective-permute-start | bytes 5505032 | tf_op jit(solution)/shard_map/ppermute | solution.py:49
  76.1 0.2 copy.25
  76.5 0.3 stack.50
  76.7 2.3 %fusion.17 = bf16[256,288]{0,1:T(8,128)(2,1)S(1)} fusion(bf16[256,3584]{1,0:T(8,128)(2,1)S(1)} %bitcast.41, bf16[1,288,3584]{2,1,0:T(8,128)(2,1)} %param.6), kind=kOutput, calls=%fused_computation.13 | convolution fusion | flops 528629760 | bytes 4046848 | tf_op jit(solution)/shard_map/dot_general | solution.py:57
  79.1 0.2 copy.21
  79.4 0.2 maximum_bitcast_fusion.1
  79.7 2.9 %fusion.14 = bf16[256,288]{0,1:T(8,128)(2,1)S(1)} fusion(bf16[256,3584]{1,0:T(8,128)(2,1)} %bitcast.5, bf16[1,288,3584]{2,1,0:T(8,128)(2,1)} %param.6), kind=kOutput, calls=%fused_computation.12 | convolution fusion | flops 528629760 | bytes 4046848 | tf_op jit(solution)/shard_map/dot_general | solution.py:57
  82.5 0.2 copy.22
  82.8 0.1 constant_dynamic-update-slice_fusion
  82.9 0.4 reverse_select_fusion
  83.2 0.1 fusion.22
  83.6 0.1 fusion.23
  83.7 0.2 copy.24
  83.9 3.3 %collective-permute-start.2 = (bf16[2,128,288]{2,0,1:T(2,128)(2,1)S(1)}, bf16[2,128,288]{2,0,1:T(2,128)(2,1)S(1)}, u32[]{:S(2)}, u32[]{:S(2)}) collective-permute-start(bf16[2,128,288]{2,0,1:T(2,128)(2,1)S(1)} %bitcast.47), channel_id=1, source_target_pairs={{0,480},{32,448},{64,416},{96,384},{128,352},{160,320},{192,288},{... | collective-permute-start | bytes 442376 | tf_op jit(solution)/shard_map/ppermute | solution.py:16
  87.2 0.7 fusion.26
  87.9 3.8 %fusion.3 = bf16[1,288,3584]{2,1,0:T(8,128)(2,1)} fusion(f32[288,3584]{1,0:T(8,128)S(1)} %fusion.26, bf16[256,288]{1,0:T(8,128)(2,1)S(1)} %squeeze.15, bf16[256,3584]{1,0:T(8,128)(2,1)} %bitcast.5, bf16[1,288,3584]{2,1,0:T(8,128)(2,1)S(1)} %copy-done), kind=kOutput, calls=%fused_computation.4 | convolution fusion | flops 533643264 | bytes 10240000 | tf_op jit(solution)/shard_map/dot_general | solution.py:59
  91.6 0.2 copy.23
  91.8 4.2 %collective-permute-done.2 = bf16[2,128,288]{2,0,1:T(2,128)(2,1)S(1)} collective-permute-done((bf16[2,128,288]{2,0,1:T(2,128)(2,1)S(1)}, bf16[2,128,288]{2,0,1:T(2,128)(2,1)S(1)}, u32[]{:S(2)}, u32[]{:S(2)}) %collective-permute-start.2) | collective-permute-done | bytes 147488 | tf_op jit(solution)/shard_map/ppermute | solution.py:16
  96.0 0.6 maximum_bitcast_fusion
  96.6 1.1 %copy.28 = bf16[1,2,2,128,288]{3,4,2,1,0:T(8,128)(2,1)} copy(bf16[1,2,2,128,288]{4,2,3,1,0:T(2,128)(2,1)S(1)} %maximum_bitcast_fusion) | data formatting | bytes 589824
  (18 shorter events, 0.7 us)
Async XLA Ops:
  34.0 18.6 %collective-permute-start = (bf16[1472,128]{1,0:T(8,128)(2,1)S(1)}, bf16[1472,128]{1,0:T(8,128)(2,1)S(1)}, u32[]{:S(2)}, u32[]{:S(2)}) collective-permute-start(bf16[1472,128]{1,0:T(8,128)(2,1)S(1)} %pad_maximum_fusion.1), channel_id=1, source_target_pairs={{0,480},{32,448},{64,416},{96,384},{128,352},{160,320},{192,288},{... | collective-permute-start | bytes 1130504 | tf_op jit(solution)/shard_map/ppermute | solution.py:16
  65.1 14.6 %collective-permute-start.1 = (bf16[2,4,4,8,3584]{4,3,2,1,0:T(8,128)(2,1)S(1)}, bf16[2,4,4,8,3584]{4,3,2,1,0:T(8,128)(2,1)}, u32[]{:S(2)}, u32[]{:S(2)}) collective-permute-start(bf16[2,4,4,8,3584]{4,3,2,1,0:T(8,128)(2,1)S(1)} %pad_maximum_fusion), channel_id=1, source_target_pairs={{0,1},{1,0},{2,3},{3,2},{4,5},{5,4},{6,7},{7,6},{8,9},{9,8},{10,11... | collective-permute-start | bytes 5505032 | tf_op jit(solution)/shard_map/ppermute | solution.py:49
  83.9 4.0 %copy-start = (bf16[1,288,3584]{2,1,0:T(8,128)(2,1)S(1)}, bf16[1,288,3584]{2,1,0:T(8,128)(2,1)}, u32[]{:S(2)}) copy-start(bf16[1,288,3584]{2,1,0:T(8,128)(2,1)} %param.6) | copy-start | bytes 6193156
  83.9 12.1 %collective-permute-start.2 = (bf16[2,128,288]{2,0,1:T(2,128)(2,1)S(1)}, bf16[2,128,288]{2,0,1:T(2,128)(2,1)S(1)}, u32[]{:S(2)}, u32[]{:S(2)}) collective-permute-start(bf16[2,128,288]{2,0,1:T(2,128)(2,1)S(1)} %bitcast.47), channel_id=1, source_target_pairs={{0,480},{32,448},{64,416},{96,384},{128,352},{160,320},{192,288},{... | collective-permute-start | bytes 442376 | tf_op jit(solution)/shard_map/ppermute | solution.py:16

commit v12 on v11

--- a/solution.py
+++ b/solution.py
@@ -54,8 +54,11 @@
     grads = []
     total = None
     for index, piece in enumerate(pieces):
-        grad = jnp.dot(piece, own_weight.T, preferred_element_type=jnp.float32)
-        grads.append((grad * scale_factor).astype(jnp.bfloat16))
+        grad = [
+            jnp.dot(rows, own_weight.T, preferred_element_type=jnp.float32)
+            for rows in piece.reshape(2, -1, full_width)[::-1]
+        ]
+        grads.append((jnp.stack(grad[::-1], axis=0) * scale_factor).astype(jnp.bfloat16))
         part = jnp.dot(acts[index].T, piece, preferred_element_type=jnp.float32)
         total = part if total is None else total + part
     grad = own_first(jnp.stack(grads, axis=0).reshape(n_c, 2, n_z, n_x, micro, row_total, share))

time: 98 us -> 119 us (1.21)
  local copies, waits for them, and re-layouts: 5.27 us -> 15 us
  matrix products: 9.65 us -> 18 us
  other arithmetic: 3.12 us -> 4.87 us
    another operation x3 -> x5, local copies, waits for them, and re-layouts: 0.22 us -> 6.58 us  [shards(): jnp.stack(grads, axis=0).reshape(n_c, 2, n_z, n_x, micro, row_total, share)]
    dot_general x2 -> x4, matrix products: 5.18 us -> 10.1 us  [shards(): jnp.dot(rows, own_weight.T, preferred_element_type=jnp.float32)]
    dot_general x2, matrix products: 4.48 us -> 7.92 us  [shards(): part = jnp.dot(acts[index].T, piece, preferred_element_type=jnp.float32)]
    squeeze x2, local copies, waits for them, and re-layouts: 0.18 us -> 1.77 us  [shards(): part = jnp.dot(acts[index].T, piece, preferred_element_type=jnp.float32)]
    another operation x1, other arithmetic: 0.17 us -> 1.39 us  [shards(): jnp.stack([lax.all_gather(own_rows[0], 'dx', axis=1), lax.all_gather(mirr...]
  transfers between devices with their start and end apart: 3 -> 3, of which waited for: 2 -> 1; matrix products, arithmetic and copies ran while one was open for 8% -> 14% of each run, Pallas kernels for 0% -> 0%
where the time goes in v12:
time: 119 us; the launch traced here: 118 us
  blocking collectives  53.6 us (45%)
  starting transfers between devices  20.7 us (17%)
  matrix products  18 us (15%)
  local copies, waits for them, and re-layouts  15 us (13%)
  waiting for transfers between devices  5.31 us (4%)
  other arithmetic  4.87 us (4%)
    all_gather x1, blocking collectives, shards(): own_rows = lax.all_gather(own_rows, 'dz', axis=1)  29.5 us
    all_gather x1, blocking collectives, shards(): lax.all_gather(own_rows[0], 'dx', axis=1)  12.5 us
    all_gather x1, blocking collectives, shards(): lax.all_gather(mirror_rows, 'dx', axis=1)  11.7 us
    ppermute x1, starting transfers between devices, shards(): other_rows = lax.ppermute(both_rows, 'dc', [(0, 1), (1, 0)])  11.4 us
    dot_general x4, matrix products, shards(): jnp.dot(rows, own_weight.T, preferred_element_type=jnp.float32)  10.1 us
    ppermute x2, starting transfers between devices, mirror(): return lax.ppermute(block, PIPE, route)  9.24 us
    dot_general x2, matrix products, shards(): part = jnp.dot(acts[index].T, piece, preferred_element_type=jnp.float32)  7.92 us
    ppermute x2, waiting for transfers between devices, mirror(): return lax.ppermute(block, PIPE, route)  5.31 us
  transfers between devices with their start and end apart: 3, of which 1 were waited for; matrix products, arithmetic and copies ran while one was open for 14% of the time, Pallas kernels for 0%

profile of v12, /device:TPU:1, one launch (start us, length us, event | category | flops | bytes accessed | tf_op | source)
XLA Modules:
  0.0 118.4 jit_solution(7599358986425065852)
XLA Ops:
  0.6 0.8 iota_compare_fusion
  1.4 1.0 broadcast_select_fusion
  2.5 1.0 fusion.31
  3.7 0.3 reshape_squeeze.7
  4.1 29.5 %all_gather.9 = bf16[2,4,8,3584]{3,2,1,0:T(8,128)(2,1)S(1)} all-gather(bf16[2,1,8,3584]{3,2,1,0:T(8,128)(2,1)S(1)} %pad_maximum_fusion.3), channel_id=1, replica_groups=mesh['py'=4,'pz'=4,'dz'=4,'dx'=4,'dc'=2] {'dz'}, dimensions={1}, use_global_device_ids=true | all-gather | bytes 573440 | tf_op jit(solution)/shard_map/all_gather | solution.py:44
  33.6 0.3 reshape_squeeze.6
  34.0 6.1 %collective-permute-start = (bf16[1472,128]{1,0:T(8,128)(2,1)S(1)}, bf16[1472,128]{1,0:T(8,128)(2,1)S(1)}, u32[]{:S(2)}, u32[]{:S(2)}) collective-permute-start(bf16[1472,128]{1,0:T(8,128)(2,1)S(1)} %pad_maximum_fusion.2), channel_id=1, source_target_pairs={{0,480},{32,448},{64,416},{96,384},{128,352},{160,320},{192,288},{... | collective-permute-start | bytes 1130504 | tf_op jit(solution)/shard_map/ppermute | solution.py:16
  40.1 12.5 %all-gather = bf16[1,4,32,3584]{3,2,1,0:T(8,128)(2,1)S(1)} all-gather(bf16[1,4,8,3584]{3,2,1,0:T(8,128)(2,1)S(1)} %get-tuple-element.6), channel_id=2, replica_groups=mesh['py'=4,'pz'=4,'dz'=4,'dx'=4,'dc'=2] {'dx'}, dimensions={2}, use_global_device_ids=true | all-gather | bytes 1146880 | tf_op jit(solution)/shard_map/all_gather | solution.py:47
  52.5 0.8 copy-done.3
  53.3 0.3 all_gather_reshape.4
  53.6 11.7 %all_gather.11 = bf16[4,4,8,3584]{3,2,1,0:T(8,128)(2,1)S(1)} all-gather(bf16[4,1,8,3584]{3,2,1,0:T(8,128)(2,1)S(1)} %bitcast.70), channel_id=1, replica_groups=mesh['py'=4,'pz'=4,'dz'=4,'dx'=4,'dc'=2] {'dx'}, dimensions={1}, use_global_device_ids=true | all-gather | bytes 1146880 | tf_op jit(solution)/shard_map/all_gather | solution.py:47
  65.3 1.4 %pad_maximum_fusion = bf16[2,4,4,8,3584]{4,3,2,1,0:T(8,128)(2,1)} fusion(bf16[1,4,4,8,3584]{4,3,2,1,0:T(8,128)(2,1)S(1)} %bitcast.68, bf16[1,4,4,8,3584]{4,3,2,1,0:T(8,128)(2,1)S(1)} %bitcast.69), kind=kLoop, calls=%fused_computation.13 | loop fusion | flops 917504 | bytes 3670016 | tf_op jit(solution)/shard_map/stack | solution.py:46
  66.7 11.4 %collective-permute-start.1 = (bf16[2,4,4,8,3584]{4,3,2,1,0:T(8,128)(2,1)}, bf16[2,4,4,8,3584]{4,3,2,1,0:T(8,128)(2,1)}, u32[]{:S(2)}, u32[]{:S(2)}) collective-permute-start(bf16[2,4,4,8,3584]{4,3,2,1,0:T(8,128)(2,1)} %pad_maximum_fusion), channel_id=1, source_target_pairs={{0,1},{1,0},{2,3},{3,2},{4,5},{5,4},{6,7},{7,6},{8,9},{9,8},{10,11... | collective-permute-start | bytes 5505032 | tf_op jit(solution)/shard_map/ppermute | solution.py:49
  78.6 3.4 %fusion.12 = f32[1,1,4,4,2,4,288]{6,5,4,3,2,1,0:T(4,128)} fusion(bf16[4,4,2,4,3584]{4,3,2,1,0:T(4,128)(2,1)S(1)} %reshape.154, bf16[1,288,3584]{2,1,0:T(8,128)(2,1)} %param.6), kind=kOutput, calls=%fused_computation.14 | convolution fusion | flops 264241152 | bytes 3129344 | tf_op jit(solution)/shard_map/dot_general | solution.py:58
  82.3 0.7 slice-done
  82.9 0.3 stack.68
  83.6 0.8 fusion.29
  84.4 1.0 squeeze.15
  85.4 0.8 squeeze.14
  86.2 1.2 fusion.15
  87.4 4.2 %fusion.33 = f32[288,3584]{1,0:T(8,128)} fusion(bf16[256,288]{1,0:T(8,128)(2,1)S(1)} %copy-done.2, bf16[256,3584]{1,0:T(8,128)(2,1)} %bitcast.20), kind=kOutput, calls=%fused_computation.38 | convolution fusion | flops 528482304 | bytes 6111232 | tf_op jit(solution)/shard_map/dot_general | solution.py:62
  91.5 2.5 %fusion.27 = (bf16[1,4,4,8,3584]{4,3,2,1,0:T(8,128)(2,1)}, bf16[1,4,4,8,3584]{4,3,2,1,0:T(8,128)(2,1)S(1)}) fusion(bf16[2,4,4,8,3584]{4,3,2,1,0:T(8,128)(2,1)} %collective-permute-done.1), kind=kLoop, calls=%fused_computation.32 | loop fusion | bytes 3670016 | tf_op jit(solution)/shard_map/unstack | solution.py:59
  94.0 2.5 %reshape.156 = bf16[4,4,2,4,3584]{4,3,2,1,0:T(4,128)(2,1)} reshape(bf16[1,4,4,8,3584]{4,3,2,1,0:T(8,128)(2,1)} %get-tuple-element.4) | data formatting | bytes 1835008 | tf_op jit(solution)/shard_map/reshape.87
  96.6 3.0 %fusion.18 = f32[1,1,4,4,2,4,288]{6,5,4,3,2,1,0:T(4,128)} fusion(bf16[4,4,2,4,3584]{4,3,2,1,0:T(4,128)(2,1)} %reshape.156, bf16[1,288,3584]{2,1,0:T(8,128)(2,1)S(1)} %copy-done.1), kind=kOutput, calls=%fused_computation.16 | convolution fusion | flops 264241152 | bytes 3129344 | tf_op jit(solution)/shard_map/dot_general | solution.py:58
  99.6 1.1 reshape.157
  100.7 2.5 %fusion.21 = f32[1,1,4,4,2,4,288]{6,5,4,3,2,1,0:T(4,128)S(1)} fusion(bf16[4,4,2,4,3584]{4,3,2,1,0:T(4,128)(2,1)} %reshape.157, bf16[1,288,3584]{2,1,0:T(8,128)(2,1)S(1)} %copy-done.1), kind=kOutput, calls=%fused_computation.17 | convolution fusion | flops 264241152 | bytes 3129344 | tf_op jit(solution)/shard_map/dot_general | solution.py:58
  103.5 0.3 pad_maximum_fusion.1
  104.3 3.1 %collective-permute-start.2 = (bf16[2,128,288]{2,0,1:T(2,128)(2,1)S(1)}, bf16[2,128,288]{2,0,1:T(2,128)(2,1)S(1)}, u32[]{:S(2)}, u32[]{:S(2)}) collective-permute-start(bf16[2,128,288]{2,0,1:T(2,128)(2,1)S(1)} %bitcast.73), channel_id=1, source_target_pairs={{0,480},{32,448},{64,416},{96,384},{128,352},{160,320},{192,288},{... | collective-permute-start | bytes 442376 | tf_op jit(solution)/shard_map/ppermute | solution.py:16
  107.5 3.8 %fusion.3 = bf16[1,288,3584]{2,1,0:T(8,128)(2,1)} fusion(f32[288,3584]{1,0:T(8,128)S(1)} %copy-done, bf16[256,288]{1,0:T(8,128)(2,1)S(1)} %squeeze.15, bf16[256,3584]{1,0:T(8,128)(2,1)} %bitcast.21, bf16[1,288,3584]{2,1,0:T(8,128)(2,1)S(1)} %copy-done.1), kind=kOutput, calls=%fused_computation.4 | convolution fusion | flops 533643264 | bytes 10240000 | tf_op jit(solution)/shard_map/dot_general | solution.py:62
  111.4 5.3 %collective-permute-done.2 = bf16[2,128,288]{2,0,1:T(2,128)(2,1)S(1)} collective-permute-done((bf16[2,128,288]{2,0,1:T(2,128)(2,1)S(1)}, bf16[2,128,288]{2,0,1:T(2,128)(2,1)S(1)}, u32[]{:S(2)}, u32[]{:S(2)}) %collective-permute-start.2) | collective-permute-done | bytes 147488 | tf_op jit(solution)/shard_map/ppermute | solution.py:16
  116.7 0.6 maximum_bitcast_fusion
  117.3 1.1 copy.13
  (33 shorter events, 2.3 us)
Async XLA Ops:
  34.0 18.6 %collective-permute-start = (bf16[1472,128]{1,0:T(8,128)(2,1)S(1)}, bf16[1472,128]{1,0:T(8,128)(2,1)S(1)}, u32[]{:S(2)}, u32[]{:S(2)}) collective-permute-start(bf16[1472,128]{1,0:T(8,128)(2,1)S(1)} %pad_maximum_fusion.2), channel_id=1, source_target_pairs={{0,480},{32,448},{64,416},{96,384},{128,352},{160,320},{192,288},{... | collective-permute-start | bytes 1130504 | tf_op jit(solution)/shard_map/ppermute | solution.py:16
  52.5 0.8 copy-start.3
  66.7 24.9 %collective-permute-start.1 = (bf16[2,4,4,8,3584]{4,3,2,1,0:T(8,128)(2,1)}, bf16[2,4,4,8,3584]{4,3,2,1,0:T(8,128)(2,1)}, u32[]{:S(2)}, u32[]{:S(2)}) collective-permute-start(bf16[2,4,4,8,3584]{4,3,2,1,0:T(8,128)(2,1)} %pad_maximum_fusion), channel_id=1, source_target_pairs={{0,1},{1,0},{2,3},{3,2},{4,5},{5,4},{6,7},{7,6},{8,9},{9,8},{10,11... | collective-permute-start | bytes 5505032 | tf_op jit(solution)/shard_map/ppermute | solution.py:49
  82.0 0.9 slice-start
  82.2 3.9 %copy-start.1 = (bf16[1,288,3584]{2,1,0:T(8,128)(2,1)S(1)}, bf16[1,288,3584]{2,1,0:T(8,128)(2,1)}, u32[]{:S(2)}) copy-start(bf16[1,288,3584]{2,1,0:T(8,128)(2,1)} %param.6) | copy-start | bytes 6193156
  86.2 1.2 copy-start.2
  100.7 2.5 %copy-start.4 = (f32[1,1,4,4,2,4,288]{6,5,4,3,2,1,0:T(4,128)S(1)}, f32[1,1,4,4,2,4,288]{6,5,4,3,2,1,0:T(4,128)}, u32[]{:S(2)}) copy-start(f32[1,1,4,4,2,4,288]{6,5,4,3,2,1,0:T(4,128)} %fusion.12) | copy-start | bytes 442372
  100.7 2.5 %copy-start.5 = (f32[1,1,4,4,2,4,288]{6,5,4,3,2,1,0:T(4,128)S(1)}, f32[1,1,4,4,2,4,288]{6,5,4,3,2,1,0:T(4,128)}, u32[]{:S(2)}) copy-start(f32[1,1,4,4,2,4,288]{6,5,4,3,2,1,0:T(4,128)} %fusion.18) | copy-start | bytes 442372
  100.7 6.7 %copy-start = (f32[288,3584]{1,0:T(8,128)S(1)}, f32[288,3584]{1,0:T(8,128)}, u32[]{:S(2)}) copy-start(f32[288,3584]{1,0:T(8,128)} %fusion.33) | copy-start | bytes 12386308
  104.3 12.4 %collective-permute-start.2 = (bf16[2,128,288]{2,0,1:T(2,128)(2,1)S(1)}, bf16[2,128,288]{2,0,1:T(2,128)(2,1)S(1)}, u32[]{:S(2)}, u32[]{:S(2)}) collective-permute-start(bf16[2,128,288]{2,0,1:T(2,128)(2,1)S(1)} %bitcast.73), channel_id=1, source_target_pairs={{0,480},{32,448},{64,416},{96,384},{128,352},{160,320},{192,288},{... | collective-permute-start | bytes 442376 | tf_op jit(solution)/shard_map/ppermute | solution.py:16

commit v13 on v11

--- a/solution.py
+++ b/solution.py
@@ -42,7 +42,8 @@
     own_weight = weights[0]
     own_rows = jnp.stack([masked[0, 0], masked[0, 1]], axis=0).reshape(2, -1, full_width)
     own_rows = lax.all_gather(own_rows, "dz", axis=1)
-    mirror_rows, mirror_hidden = mirror_pair(own_rows[1], hidden[0, 1])
+    mirror_rows, mirror_hidden = mirror_pair(own_rows[1], jnp.swapaxes(hidden[0, 1], -1, -2))
+    mirror_hidden = jnp.swapaxes(mirror_hidden, -1, -2)
     both_rows = jnp.stack(
         [lax.all_gather(own_rows[0], "dx", axis=1), lax.all_gather(mirror_rows, "dx", axis=1)], axis=0
     )

time: 98 us -> 97.5 us (level)
  transfers between devices with their start and end apart: 3 -> 3, of which waited for: 2 -> 1; matrix products, arithmetic and copies ran while one was open for 8% -> 8% of each run, Pallas kernels for 0% -> 0%
where the time goes in v13:
time: 97.5 us; the launch traced here: 97.2 us
  blocking collectives  54.1 us (55%)
  starting transfers between devices  20.4 us (21%)
  matrix products  9.64 us (10%)
  local copies, waits for them, and re-layouts  4.74 us (5%)
  waiting for transfers between devices  4.2 us (4%)
  other arithmetic  3.23 us (3%)
    all_gather x1, blocking collectives, shards(): own_rows = lax.all_gather(own_rows, 'dz', axis=1)  29.5 us
    all_gather x1, blocking collectives, shards(): lax.all_gather(own_rows[0], 'dx', axis=1)  12.5 us
    all_gather x1, blocking collectives, shards(): lax.all_gather(mirror_rows, 'dx', axis=1)  12.1 us
    ppermute x1, starting transfers between devices, shards(): other_rows = lax.ppermute(both_rows, 'dc', [(0, 1), (1, 0)])  11 us
    ppermute x2, starting transfers between devices, mirror(): return lax.ppermute(block, PIPE, route)  9.38 us
    dot_general x2, matrix products, shards(): grad = jnp.dot(piece, own_weight.T, preferred_element_type=jnp.float32)  5.16 us
    dot_general x2, matrix products, shards(): part = jnp.dot(acts[index].T, piece, preferred_element_type=jnp.float32)  4.47 us
    ppermute x2, waiting for transfers between devices, mirror(): return lax.ppermute(block, PIPE, route)  4.2 us
  transfers between devices with their start and end apart: 3, of which 1 were waited for; matrix products, arithmetic and copies ran while one was open for 8% of the time, Pallas kernels for 0%

profile of v13, /device:TPU:1, one launch (start us, length us, event | category | flops | bytes accessed | tf_op | source)
XLA Modules:
  0.0 97.2 jit_solution(8489947700395359013)
XLA Ops:
  0.6 0.8 iota_compare_fusion
  1.4 1.0 %broadcast_select_fusion = bf16[1,2,2,4,3584]{4,3,2,1,0:T(4,128)(2,1)S(1)} fusion(bf16[1,2,2,4,3584]{4,3,2,1,0:T(4,128)(2,1)} %param.4, pred[2,2,4]{2,1,0:T(4,128)(4,1)S(1)} %iota_compare_fusion), kind=kLoop, calls=%fused_computation.21 | loop fusion | flops 57344 | bytes 229392 | tf_op jit(solution)/shard_map/jit(_where)/select_n | solution.py:41
  2.5 1.0 %fusion.24 = (bf16[1,1,2,128,288]{3,4,2,1,0:T(8,128)(2,1)S(1)}, bf16[1,1,2,128,288]{3,4,2,1,0:T(8,128)(2,1)S(1)}) fusion(bf16[1,2,2,128,288]{3,4,2,1,0:T(8,128)(2,1)} %param.5), kind=kLoop, calls=%fused_computation.28 | loop fusion | bytes 589824 | tf_op jit(solution)/shard_map/slice | solution.py:51
  3.5 29.5 %all_gather.9 = bf16[2,4,8,3584]{3,2,1,0:T(8,128)(2,1)S(1)} all-gather(bf16[2,1,8,3584]{3,2,1,0:T(8,128)(2,1)S(1)} %pad_maximum_fusion.2), channel_id=1, replica_groups=mesh['py'=4,'pz'=4,'dz'=4,'dx'=4,'dc'=2] {'dz'}, dimensions={1}, use_global_device_ids=true | all-gather | bytes 573440 | tf_op jit(solution)/shard_map/all_gather | solution.py:44
  33.1 0.3 reshape_squeeze.3
  33.4 6.1 %collective-permute-start = (bf16[1472,128]{1,0:T(8,128)(2,1)S(1)}, bf16[1472,128]{1,0:T(8,128)(2,1)S(1)}, u32[]{:S(2)}, u32[]{:S(2)}) collective-permute-start(bf16[1472,128]{1,0:T(8,128)(2,1)S(1)} %pad_maximum_fusion.1), channel_id=1, source_target_pairs={{0,480},{32,448},{64,416},{96,384},{128,352},{160,320},{192,288},{... | collective-permute-start | bytes 1130504 | tf_op jit(solution)/shard_map/ppermute | solution.py:16
  39.6 12.5 %all-gather = bf16[1,4,32,3584]{3,2,1,0:T(8,128)(2,1)S(1)} all-gather(bf16[1,4,8,3584]{3,2,1,0:T(8,128)(2,1)S(1)} %get-tuple-element.8), channel_id=2, replica_groups=mesh['py'=4,'pz'=4,'dz'=4,'dx'=4,'dc'=2] {'dx'}, dimensions={2}, use_global_device_ids=true | all-gather | bytes 1146880 | tf_op jit(solution)/shard_map/all_gather | solution.py:48
  52.0 0.3 all_gather_reshape.4
  52.3 12.1 %all_gather.11 = bf16[4,4,8,3584]{3,2,1,0:T(8,128)(2,1)S(1)} all-gather(bf16[4,1,8,3584]{3,2,1,0:T(8,128)(2,1)S(1)} %bitcast.53), channel_id=1, replica_groups=mesh['py'=4,'pz'=4,'dz'=4,'dx'=4,'dc'=2] {'dx'}, dimensions={1}, use_global_device_ids=true | all-gather | bytes 1146880 | tf_op jit(solution)/shard_map/all_gather | solution.py:48
  64.4 0.2 pad_maximum_fusion
  64.6 11.0 %collective-permute-start.1 = (bf16[2,4,4,8,3584]{4,3,2,1,0:T(8,128)(2,1)S(1)}, bf16[2,4,4,8,3584]{4,3,2,1,0:T(8,128)(2,1)}, u32[]{:S(2)}, u32[]{:S(2)}) collective-permute-start(bf16[2,4,4,8,3584]{4,3,2,1,0:T(8,128)(2,1)S(1)} %pad_maximum_fusion), channel_id=1, source_target_pairs={{0,1},{1,0},{2,3},{3,2},{4,5},{5,4},{6,7},{7,6},{8,9},{9,8},{10,11... | collective-permute-start | bytes 5505032 | tf_op jit(solution)/shard_map/ppermute | solution.py:50
  75.6 0.2 copy.34
  75.9 0.2 copy.35
  76.2 2.3 %fusion.17 = bf16[256,288]{0,1:T(8,128)(2,1)S(1)} fusion(bf16[256,3584]{1,0:T(8,128)(2,1)S(1)} %bitcast.49, bf16[1,288,3584]{2,1,0:T(8,128)(2,1)} %param.6), kind=kOutput, calls=%fused_computation.13 | convolution fusion | flops 528629760 | bytes 4046848 | tf_op jit(solution)/shard_map/dot_general | solution.py:58
  78.5 0.2 copy.30
  78.8 0.3 maximum_bitcast_fusion.1
  79.2 2.9 %fusion.14 = bf16[256,288]{0,1:T(8,128)(2,1)S(1)} fusion(bf16[256,3584]{1,0:T(8,128)(2,1)} %bitcast.9, bf16[1,288,3584]{2,1,0:T(8,128)(2,1)} %param.6), kind=kOutput, calls=%fused_computation.12 | convolution fusion | flops 528629760 | bytes 4046848 | tf_op jit(solution)/shard_map/dot_general | solution.py:58
  82.0 0.2 copy.31
  82.3 0.1 constant_dynamic-update-slice_fusion
  82.4 0.4 reverse_select_fusion
  82.7 0.1 fusion.22
  82.9 0.1 squeeze.19
  83.0 0.1 squeeze.18
  83.1 0.1 fusion.23
  83.2 0.2 copy.33
  83.4 3.3 %collective-permute-start.2 = (bf16[2,128,288]{2,0,1:T(2,128)(2,1)S(1)}, bf16[2,128,288]{2,0,1:T(2,128)(2,1)S(1)}, u32[]{:S(2)}, u32[]{:S(2)}) collective-permute-start(bf16[2,128,288]{2,0,1:T(2,128)(2,1)S(1)} %bitcast.59), channel_id=1, source_target_pairs={{0,480},{32,448},{64,416},{96,384},{128,352},{160,320},{192,288},{... | collective-permute-start | bytes 442376 | tf_op jit(solution)/shard_map/ppermute | solution.py:16
  86.7 0.7 fusion.26
  87.4 3.8 %fusion.3 = bf16[1,288,3584]{2,1,0:T(8,128)(2,1)} fusion(f32[288,3584]{1,0:T(8,128)S(1)} %fusion.26, bf16[256,288]{1,0:T(8,128)(2,1)S(1)} %squeeze.19, bf16[256,3584]{1,0:T(8,128)(2,1)} %bitcast.9, bf16[1,288,3584]{2,1,0:T(8,128)(2,1)S(1)} %copy-done), kind=kOutput, calls=%fused_computation.4 | convolution fusion | flops 533643264 | bytes 10240000 | tf_op jit(solution)/shard_map/dot_general | solution.py:60
  91.1 0.2 copy.32
  91.3 4.2 %collective-permute-done.2 = bf16[2,128,288]{2,0,1:T(2,128)(2,1)S(1)} collective-permute-done((bf16[2,128,288]{2,0,1:T(2,128)(2,1)S(1)}, bf16[2,128,288]{2,0,1:T(2,128)(2,1)S(1)}, u32[]{:S(2)}, u32[]{:S(2)}) %collective-permute-start.2) | collective-permute-done | bytes 147488 | tf_op jit(solution)/shard_map/ppermute | solution.py:16
  95.5 0.6 maximum_bitcast_fusion
  96.1 1.1 %copy.38 = bf16[1,2,2,128,288]{3,4,2,1,0:T(8,128)(2,1)} copy(bf16[1,2,2,128,288]{4,2,3,1,0:T(2,128)(2,1)S(1)} %maximum_bitcast_fusion) | data formatting | bytes 589824
  (17 shorter events, 0.5 us)
Async XLA Ops:
  33.4 18.6 %collective-permute-start = (bf16[1472,128]{1,0:T(8,128)(2,1)S(1)}, bf16[1472,128]{1,0:T(8,128)(2,1)S(1)}, u32[]{:S(2)}, u32[]{:S(2)}) collective-permute-start(bf16[1472,128]{1,0:T(8,128)(2,1)S(1)} %pad_maximum_fusion.1), channel_id=1, source_target_pairs={{0,480},{32,448},{64,416},{96,384},{128,352},{160,320},{192,288},{... | collective-permute-start | bytes 1130504 | tf_op jit(solution)/shard_map/ppermute | solution.py:16
  64.6 14.6 %collective-permute-start.1 = (bf16[2,4,4,8,3584]{4,3,2,1,0:T(8,128)(2,1)S(1)}, bf16[2,4,4,8,3584]{4,3,2,1,0:T(8,128)(2,1)}, u32[]{:S(2)}, u32[]{:S(2)}) collective-permute-start(bf16[2,4,4,8,3584]{4,3,2,1,0:T(8,128)(2,1)S(1)} %pad_maximum_fusion), channel_id=1, source_target_pairs={{0,1},{1,0},{2,3},{3,2},{4,5},{5,4},{6,7},{7,6},{8,9},{9,8},{10,11... | collective-permute-start | bytes 5505032 | tf_op jit(solution)/shard_map/ppermute | solution.py:50
  83.4 4.0 %copy-start = (bf16[1,288,3584]{2,1,0:T(8,128)(2,1)S(1)}, bf16[1,288,3584]{2,1,0:T(8,128)(2,1)}, u32[]{:S(2)}) copy-start(bf16[1,288,3584]{2,1,0:T(8,128)(2,1)} %param.6) | copy-start | bytes 6193156
  83.4 12.1 %collective-permute-start.2 = (bf16[2,128,288]{2,0,1:T(2,128)(2,1)S(1)}, bf16[2,128,288]{2,0,1:T(2,128)(2,1)S(1)}, u32[]{:S(2)}, u32[]{:S(2)}) collective-permute-start(bf16[2,128,288]{2,0,1:T(2,128)(2,1)S(1)} %bitcast.59), channel_id=1, source_target_pairs={{0,480},{32,448},{64,416},{96,384},{128,352},{160,320},{192,288},{... | collective-permute-start | bytes 442376 | tf_op jit(solution)/shard_map/ppermute | solution.py:16

commit v14 on v13

--- a/solution.py
+++ b/solution.py
@@ -36,9 +36,8 @@
     share = hidden.shape[4]
     n_z, n_x, n_c = (lax.axis_size(name) for name in DP)
     scale_factor = float(full_width) ** (-0.5)
-    slot_index = lax.broadcasted_iota(jnp.int32, (1, 1, 1, row_total), 3)
-    live_rows = slot_index < counts
-    masked = jnp.where(live_rows[..., None], grad_out, jnp.zeros_like(grad_out))
+    slot_index = lax.broadcasted_iota(jnp.int32, grad_out.shape, 3)
+    masked = jnp.where(slot_index < counts[..., None], grad_out, jnp.zeros_like(grad_out))
     own_weight = weights[0]
     own_rows = jnp.stack([masked[0, 0], masked[0, 1]], axis=0).reshape(2, -1, full_width)
     own_rows = lax.all_gather(own_rows, "dz", axis=1)

time: 97.5 us -> 96.8 us (level)
  no operation moved by 1% of the time
where the time goes in v14:
time: 96.8 us; the launch traced here: 96.4 us
  blocking collectives  54.1 us (56%)
  starting transfers between devices  20.4 us (21%)
  matrix products  9.64 us (10%)
  local copies, waits for them, and re-layouts  4.74 us (5%)
  waiting for transfers between devices  4.2 us (4%)
  other arithmetic  2.47 us (3%)
    all_gather x1, blocking collectives, shards(): own_rows = lax.all_gather(own_rows, 'dz', axis=1)  29.5 us
    all_gather x1, blocking collectives, shards(): lax.all_gather(own_rows[0], 'dx', axis=1)  12.5 us
    all_gather x1, blocking collectives, shards(): lax.all_gather(mirror_rows, 'dx', axis=1)  12.1 us
    ppermute x1, starting transfers between devices, shards(): other_rows = lax.ppermute(both_rows, 'dc', [(0, 1), (1, 0)])  11 us
    ppermute x2, starting transfers between devices, mirror(): return lax.ppermute(block, PIPE, route)  9.38 us
    dot_general x2, matrix products, shards(): grad = jnp.dot(piece, own_weight.T, preferred_element_type=jnp.float32)  5.16 us
    dot_general x2, matrix products, shards(): part = jnp.dot(acts[index].T, piece, preferred_element_type=jnp.float32)  4.47 us
    ppermute x2, waiting for transfers between devices, mirror(): return lax.ppermute(block, PIPE, route)  4.2 us
  transfers between devices with their start and end apart: 3, of which 1 were waited for; matrix products, arithmetic and copies ran while one was open for 8% of the time, Pallas kernels for 0%

profile of v14, /device:TPU:1, one launch (start us, length us, event | category | flops | bytes accessed | tf_op | source)
XLA Modules:
  0.0 96.4 jit_solution(12530157885831694721)
XLA Ops:
  0.6 1.0 %fusion.21 = bf16[1,2,2,4,3584]{4,3,2,1,0:T(4,128)(2,1)S(1)} fusion(bf16[1,2,2,4,3584]{4,3,2,1,0:T(4,128)(2,1)} %param.4, s32[2,2]{1,0:T(2,128)} %bitcast.61), kind=kLoop, calls=%fused_computation.21 | loop fusion | flops 114688 | bytes 229392 | tf_op jit(solution)/shard_map/jit(_where)/select_n | solution.py:40
  1.7 1.0 %fusion.25 = (bf16[1,1,2,128,288]{3,4,2,1,0:T(8,128)(2,1)S(1)}, bf16[1,1,2,128,288]{3,4,2,1,0:T(8,128)(2,1)S(1)}) fusion(bf16[1,2,2,128,288]{3,4,2,1,0:T(8,128)(2,1)} %param.5), kind=kLoop, calls=%fused_computation.28 | loop fusion | bytes 589824 | tf_op jit(solution)/shard_map/slice | solution.py:50
  2.8 29.5 %all_gather.9 = bf16[2,4,8,3584]{3,2,1,0:T(8,128)(2,1)S(1)} all-gather(bf16[2,1,8,3584]{3,2,1,0:T(8,128)(2,1)S(1)} %pad_maximum_fusion.2), channel_id=1, replica_groups=mesh['py'=4,'pz'=4,'dz'=4,'dx'=4,'dc'=2] {'dz'}, dimensions={1}, use_global_device_ids=true | all-gather | bytes 573440 | tf_op jit(solution)/shard_map/all_gather | solution.py:43
  32.3 0.3 reshape_squeeze.3
  32.7 6.1 %collective-permute-start = (bf16[1472,128]{1,0:T(8,128)(2,1)S(1)}, bf16[1472,128]{1,0:T(8,128)(2,1)S(1)}, u32[]{:S(2)}, u32[]{:S(2)}) collective-permute-start(bf16[1472,128]{1,0:T(8,128)(2,1)S(1)} %pad_maximum_fusion.1), channel_id=1, source_target_pairs={{0,480},{32,448},{64,416},{96,384},{128,352},{160,320},{192,288},{... | collective-permute-start | bytes 1130504 | tf_op jit(solution)/shard_map/ppermute | solution.py:16
  38.8 12.5 %all-gather = bf16[1,4,32,3584]{3,2,1,0:T(8,128)(2,1)S(1)} all-gather(bf16[1,4,8,3584]{3,2,1,0:T(8,128)(2,1)S(1)} %get-tuple-element.8), channel_id=2, replica_groups=mesh['py'=4,'pz'=4,'dz'=4,'dx'=4,'dc'=2] {'dx'}, dimensions={2}, use_global_device_ids=true | all-gather | bytes 1146880 | tf_op jit(solution)/shard_map/all_gather | solution.py:47
  51.3 0.3 all_gather_reshape.4
  51.6 12.1 %all_gather.11 = bf16[4,4,8,3584]{3,2,1,0:T(8,128)(2,1)S(1)} all-gather(bf16[4,1,8,3584]{3,2,1,0:T(8,128)(2,1)S(1)} %bitcast.53), channel_id=1, replica_groups=mesh['py'=4,'pz'=4,'dz'=4,'dx'=4,'dc'=2] {'dx'}, dimensions={1}, use_global_device_ids=true | all-gather | bytes 1146880 | tf_op jit(solution)/shard_map/all_gather | solution.py:47
  63.7 0.2 pad_maximum_fusion
  63.8 11.0 %collective-permute-start.1 = (bf16[2,4,4,8,3584]{4,3,2,1,0:T(8,128)(2,1)S(1)}, bf16[2,4,4,8,3584]{4,3,2,1,0:T(8,128)(2,1)}, u32[]{:S(2)}, u32[]{:S(2)}) collective-permute-start(bf16[2,4,4,8,3584]{4,3,2,1,0:T(8,128)(2,1)S(1)} %pad_maximum_fusion), channel_id=1, source_target_pairs={{0,1},{1,0},{2,3},{3,2},{4,5},{5,4},{6,7},{7,6},{8,9},{9,8},{10,11... | collective-permute-start | bytes 5505032 | tf_op jit(solution)/shard_map/ppermute | solution.py:49
  74.9 0.2 copy.34
  75.1 0.1 copy.36
  75.2 0.2 copy.35
  75.5 2.3 %fusion.17 = bf16[256,288]{0,1:T(8,128)(2,1)S(1)} fusion(bf16[256,3584]{1,0:T(8,128)(2,1)S(1)} %bitcast.49, bf16[1,288,3584]{2,1,0:T(8,128)(2,1)} %param.6), kind=kOutput, calls=%fused_computation.13 | convolution fusion | flops 528629760 | bytes 4046848 | tf_op jit(solution)/shard_map/dot_general | solution.py:57
  77.8 0.2 copy.30
  78.1 0.3 maximum_bitcast_fusion.1
  78.4 2.9 %fusion.14 = bf16[256,288]{0,1:T(8,128)(2,1)S(1)} fusion(bf16[256,3584]{1,0:T(8,128)(2,1)} %bitcast.9, bf16[1,288,3584]{2,1,0:T(8,128)(2,1)} %param.6), kind=kOutput, calls=%fused_computation.12 | convolution fusion | flops 528629760 | bytes 4046848 | tf_op jit(solution)/shard_map/dot_general | solution.py:57
  81.3 0.2 copy.31
  81.5 0.1 constant_dynamic-update-slice_fusion
  81.6 0.4 reverse_select_fusion
  82.0 0.1 fusion.23
  82.1 0.1 squeeze.19
  82.2 0.1 squeeze.18
  82.3 0.1 fusion.24
  82.4 0.2 copy.33
  82.6 3.3 %collective-permute-start.2 = (bf16[2,128,288]{2,0,1:T(2,128)(2,1)S(1)}, bf16[2,128,288]{2,0,1:T(2,128)(2,1)S(1)}, u32[]{:S(2)}, u32[]{:S(2)}) collective-permute-start(bf16[2,128,288]{2,0,1:T(2,128)(2,1)S(1)} %bitcast.59), channel_id=1, source_target_pairs={{0,480},{32,448},{64,416},{96,384},{128,352},{160,320},{192,288},{... | collective-permute-start | bytes 442376 | tf_op jit(solution)/shard_map/ppermute | solution.py:16
  85.9 0.7 fusion.27
  86.6 3.8 %fusion.3 = bf16[1,288,3584]{2,1,0:T(8,128)(2,1)} fusion(f32[288,3584]{1,0:T(8,128)S(1)} %fusion.27, bf16[256,288]{1,0:T(8,128)(2,1)S(1)} %squeeze.19, bf16[256,3584]{1,0:T(8,128)(2,1)} %bitcast.9, bf16[1,288,3584]{2,1,0:T(8,128)(2,1)S(1)} %copy-done), kind=kOutput, calls=%fused_computation.4 | convolution fusion | flops 533643264 | bytes 10240000 | tf_op jit(solution)/shard_map/dot_general | solution.py:59
  90.4 0.2 copy.32
  90.5 4.2 %collective-permute-done.2 = bf16[2,128,288]{2,0,1:T(2,128)(2,1)S(1)} collective-permute-done((bf16[2,128,288]{2,0,1:T(2,128)(2,1)S(1)}, bf16[2,128,288]{2,0,1:T(2,128)(2,1)S(1)}, u32[]{:S(2)}, u32[]{:S(2)}) %collective-permute-start.2) | collective-permute-done | bytes 147488 | tf_op jit(solution)/shard_map/ppermute | solution.py:16
  94.7 0.6 maximum_bitcast_fusion
  95.3 1.1 %copy.38 = bf16[1,2,2,128,288]{3,4,2,1,0:T(8,128)(2,1)} copy(bf16[1,2,2,128,288]{4,2,3,1,0:T(2,128)(2,1)S(1)} %maximum_bitcast_fusion) | data formatting | bytes 589824
  (16 shorter events, 0.5 us)
Async XLA Ops:
  32.7 18.6 %collective-permute-start = (bf16[1472,128]{1,0:T(8,128)(2,1)S(1)}, bf16[1472,128]{1,0:T(8,128)(2,1)S(1)}, u32[]{:S(2)}, u32[]{:S(2)}) collective-permute-start(bf16[1472,128]{1,0:T(8,128)(2,1)S(1)} %pad_maximum_fusion.1), channel_id=1, source_target_pairs={{0,480},{32,448},{64,416},{96,384},{128,352},{160,320},{192,288},{... | collective-permute-start | bytes 1130504 | tf_op jit(solution)/shard_map/ppermute | solution.py:16
  63.8 14.6 %collective-permute-start.1 = (bf16[2,4,4,8,3584]{4,3,2,1,0:T(8,128)(2,1)S(1)}, bf16[2,4,4,8,3584]{4,3,2,1,0:T(8,128)(2,1)}, u32[]{:S(2)}, u32[]{:S(2)}) collective-permute-start(bf16[2,4,4,8,3584]{4,3,2,1,0:T(8,128)(2,1)S(1)} %pad_maximum_fusion), channel_id=1, source_target_pairs={{0,1},{1,0},{2,3},{3,2},{4,5},{5,4},{6,7},{7,6},{8,9},{9,8},{10,11... | collective-permute-start | bytes 5505032 | tf_op jit(solution)/shard_map/ppermute | solution.py:49
  82.6 4.0 %copy-start = (bf16[1,288,3584]{2,1,0:T(8,128)(2,1)S(1)}, bf16[1,288,3584]{2,1,0:T(8,128)(2,1)}, u32[]{:S(2)}) copy-start(bf16[1,288,3584]{2,1,0:T(8,128)(2,1)} %param.6) | copy-start | bytes 6193156
  82.6 12.1 %collective-permute-start.2 = (bf16[2,128,288]{2,0,1:T(2,128)(2,1)S(1)}, bf16[2,128,288]{2,0,1:T(2,128)(2,1)S(1)}, u32[]{:S(2)}, u32[]{:S(2)}) collective-permute-start(bf16[2,128,288]{2,0,1:T(2,128)(2,1)S(1)} %bitcast.59), channel_id=1, source_target_pairs={{0,480},{32,448},{64,416},{96,384},{128,352},{160,320},{192,288},{... | collective-permute-start | bytes 442376 | tf_op jit(solution)/shard_map/ppermute | solution.py:16

commit v15 on v14

--- a/solution.py
+++ b/solution.py
@@ -1,6 +1,10 @@
+import functools
+
 import jax
 import jax.numpy as jnp
 from jax import lax
+from jax.experimental import pallas as pl
+from jax.experimental.pallas import tpu as pltpu
 from jax.sharding import Mesh
 from jax.sharding import PartitionSpec as P
 
@@ -28,6 +32,30 @@
     return jnp.where(lax.axis_index("dc") == 0, array, array[::-1])
 
 
+def update_kernel(own_ref, other_ref, acts_ref, weight_ref, out_ref, *, scale, rate):
+    part = jnp.dot(acts_ref[0], own_ref[...], preferred_element_type=jnp.float32)
+    part = part + jnp.dot(acts_ref[1], other_ref[...], preferred_element_type=jnp.float32)
+    out_ref[...] = (weight_ref[...].astype(jnp.float32) - rate * (part * scale)).astype(out_ref.dtype)
+
+
+def update(own, other, acts_t, weight, scale, rate, chunk=512):
+    rows, width = own.shape
+    share = weight.shape[0]
+    return pl.pallas_call(
+        functools.partial(update_kernel, scale=scale, rate=rate),
+        grid=(width // chunk,),
+        in_specs=[
+            pl.BlockSpec((rows, chunk), lambda i: (0, i)),
+            pl.BlockSpec((rows, chunk), lambda i: (0, i)),
+            pl.BlockSpec((2, share, rows), lambda i: (0, 0, 0)),
+            pl.BlockSpec((share, chunk), lambda i: (0, i)),
+        ],
+        out_specs=pl.BlockSpec((share, chunk), lambda i: (0, i)),
+        out_shape=jax.ShapeDtypeStruct((share, width), weight.dtype),
+        compiler_params=pltpu.CompilerParams(dimension_semantics=("parallel",)),
+    )(own, other, acts_t, weight)
+
+
 def shards(grad_out, hidden, weights, counts):
     row_total = grad_out.shape[3]
     full_width = grad_out.shape[4]
@@ -52,16 +80,12 @@
     acts = both_hidden.reshape(2, micro, n_z, n_x, n_c, row_total, share).transpose(4, 0, 2, 3, 1, 5, 6)
     acts = own_first(acts).reshape(n_c, -1, share)
     grads = []
-    total = None
-    for index, piece in enumerate(pieces):
+    for piece in pieces:
         grad = jnp.dot(piece, own_weight.T, preferred_element_type=jnp.float32)
         grads.append((grad * scale_factor).astype(jnp.bfloat16))
-        part = jnp.dot(acts[index].T, piece, preferred_element_type=jnp.float32)
-        total = part if total is None else total + part
     grad = own_first(jnp.stack(grads, axis=0).reshape(n_c, 2, n_z, n_x, micro, row_total, share))
     grad = grad.transpose(1, 4, 2, 3, 0, 5, 6).reshape(2, micro, tokens, share)
-    gradient = total * scale_factor
-    new_weight = (own_weight.astype(jnp.float32) - step_rate * gradient).astype(jnp.bfloat16)
+    new_weight = update(pieces[0], pieces[1], jnp.swapaxes(acts, 1, 2), own_weight, scale_factor, step_rate)
     returned = mirror(grad[1])
     grad_hidden = jnp.stack([grad[0], returned], axis=0)[None]
     return (grad_hidden, new_weight[None])

time: 96.8 us -> 95.5 us (0.987)
  Pallas kernels: 0 us -> 7.19 us
  matrix products: 9.64 us -> 5.17 us
  waiting for transfers between devices: 4.2 us -> 0.02 us
    pallas_call x0 -> x1, Pallas kernels: none -> 7.19 us  [update(): pl.pallas_call(functools.partial(update_kernel, scale=scale, rate=rate),...]
    dot_general x2 -> x0, matrix products: 4.47 us -> none  [shards(): part = jnp.dot(acts[index].T, piece, preferred_element_type=jnp.float32)]
    ppermute x2, waiting for transfers between devices: 4.2 us -> 0.02 us  [mirror(): return lax.ppermute(block, PIPE, route)]
    reshape x0 -> x1, local copies, waits for them, and re-layouts: none -> 1.09 us  [shards(): acts = own_first(acts).reshape(n_c, -1, share)]
    slice x2, local copies, waits for them, and re-layouts: 1.2 us -> 0.21 us  [shards(): both_hidden = jnp.stack([hidden[0, 0], mirror_hidden], axis=0)]
  transfers between devices with their start and end apart: 3 -> 3, of which waited for: 1 -> 0; matrix products, arithmetic and copies ran while one was open for 8% -> 5% of each run, Pallas kernels for 0% -> 8%
where the time goes in v15:
time: 95.5 us; the launch traced here: 95.1 us
  blocking collectives  54.1 us (57%)
  starting transfers between devices  20.2 us (21%)
  Pallas kernels  7.19 us (8%)
  matrix products  5.17 us (5%)
  local copies, waits for them, and re-layouts  4.94 us (5%)
  other arithmetic  2.52 us (3%)
    all_gather x1, blocking collectives, shards(): own_rows = lax.all_gather(own_rows, 'dz', axis=1)  29.5 us
    all_gather x1, blocking collectives, shards(): lax.all_gather(own_rows[0], 'dx', axis=1)  12.5 us
    all_gather x1, blocking collectives, shards(): lax.all_gather(mirror_rows, 'dx', axis=1)  12.1 us
    ppermute x1, starting transfers between devices, shards(): other_rows = lax.ppermute(both_rows, 'dc', [(0, 1), (1, 0)])  11 us
    ppermute x2, starting transfers between devices, mirror(): return lax.ppermute(block, PIPE, route)  9.23 us
    pallas_call x1, Pallas kernels, update(): pl.pallas_call(functools.partial(update_kernel, scale=scale, rate=rate),...  7.19 us
    dot_general x2, matrix products, shards(): grad = jnp.dot(piece, own_weight.T, preferred_element_type=jnp.float32)  5.17 us
  transfers between devices with their start and end apart: 3, of which 0 were waited for; matrix products, arithmetic and copies ran while one was open for 5% of the time, Pallas kernels for 8%

profile of v15, /device:TPU:1, one launch (start us, length us, event | category | flops | bytes accessed | tf_op | source)
XLA Modules:
  0.0 95.1 jit_solution(11078441654954424829)
XLA Ops:
  0.6 1.1 %fusion.3 = bf16[1,2,2,4,3584]{4,3,2,1,0:T(4,128)(2,1)S(1)} fusion(bf16[1,2,2,4,3584]{4,3,2,1,0:T(4,128)(2,1)} %param.4, s32[2,2]{1,0:T(2,128)} %bitcast.53), kind=kLoop, calls=%fused_computation.12 | loop fusion | flops 114688 | bytes 229392 | tf_op jit(solution)/shard_map/jit(_where)/select_n | solution.py:68
  1.8 29.5 %all_gather.9 = bf16[2,4,8,3584]{3,2,1,0:T(8,128)(2,1)S(1)} all-gather(bf16[2,1,8,3584]{3,2,1,0:T(8,128)(2,1)S(1)} %pad_maximum_fusion.2), channel_id=1, replica_groups=mesh['py'=4,'pz'=4,'dz'=4,'dx'=4,'dc'=2] {'dz'}, dimensions={1}, use_global_device_ids=true | all-gather | bytes 573440 | tf_op jit(solution)/shard_map/all_gather | solution.py:71
  31.4 0.3 reshape_squeeze.3
  31.8 6.1 %collective-permute-start = (bf16[1472,128]{1,0:T(8,128)(2,1)S(1)}, bf16[1472,128]{1,0:T(8,128)(2,1)S(1)}, u32[]{:S(2)}, u32[]{:S(2)}) collective-permute-start(bf16[1472,128]{1,0:T(8,128)(2,1)S(1)} %pad_maximum_fusion.1), channel_id=1, source_target_pairs={{0,480},{32,448},{64,416},{96,384},{128,352},{160,320},{192,288},{... | collective-permute-start | bytes 1130504 | tf_op jit(solution)/shard_map/ppermute | solution.py:20
  37.9 12.5 %all-gather = bf16[1,4,32,3584]{3,2,1,0:T(8,128)(2,1)S(1)} all-gather(bf16[1,4,8,3584]{3,2,1,0:T(8,128)(2,1)S(1)} %get-tuple-element.6), channel_id=2, replica_groups=mesh['py'=4,'pz'=4,'dz'=4,'dx'=4,'dc'=2] {'dx'}, dimensions={2}, use_global_device_ids=true | all-gather | bytes 1146880 | tf_op jit(solution)/shard_map/all_gather | solution.py:75
  50.4 0.3 all_gather_reshape.4
  50.7 12.1 %all_gather.11 = bf16[4,4,8,3584]{3,2,1,0:T(8,128)(2,1)S(1)} all-gather(bf16[4,1,8,3584]{3,2,1,0:T(8,128)(2,1)S(1)} %bitcast.45), channel_id=1, replica_groups=mesh['py'=4,'pz'=4,'dz'=4,'dx'=4,'dc'=2] {'dx'}, dimensions={1}, use_global_device_ids=true | all-gather | bytes 1146880 | tf_op jit(solution)/shard_map/all_gather | solution.py:75
  62.7 0.2 pad_maximum_fusion
  62.9 11.0 %collective-permute-start.1 = (bf16[2,4,4,8,3584]{4,3,2,1,0:T(8,128)(2,1)S(1)}, bf16[2,4,4,8,3584]{4,3,2,1,0:T(8,128)(2,1)}, u32[]{:S(2)}, u32[]{:S(2)}) collective-permute-start(bf16[2,4,4,8,3584]{4,3,2,1,0:T(8,128)(2,1)S(1)} %pad_maximum_fusion), channel_id=1, source_target_pairs={{0,1},{1,0},{2,3},{3,2},{4,5},{5,4},{6,7},{7,6},{8,9},{9,8},{10,11... | collective-permute-start | bytes 5505032 | tf_op jit(solution)/shard_map/ppermute | solution.py:77
  74.0 0.2 copy.27
  74.2 0.1 copy.29
  74.3 2.3 %fusion = bf16[256,288]{0,1:T(8,128)(2,1)S(1)} fusion(bf16[256,3584]{1,0:T(8,128)(2,1)S(1)} %bitcast.37, bf16[1,288,3584]{2,1,0:T(8,128)(2,1)} %param.6), kind=kOutput, calls=%fused_computation.3 | convolution fusion | flops 528629760 | bytes 4046848 | tf_op jit(solution)/shard_map/dot_general | solution.py:84
  76.6 0.2 copy.23
  76.7 0.1 stack.45
  76.8 0.2 copy.28
  77.0 0.1 copy.30
  77.1 0.1 constant_dynamic-update-slice_fusion.1
  77.2 0.3 maximum_bitcast_fusion.1
  77.5 2.9 %fusion.1 = bf16[256,288]{0,1:T(8,128)(2,1)S(1)} fusion(bf16[256,3584]{1,0:T(8,128)(2,1)} %bitcast.9.other_ref, bf16[1,288,3584]{2,1,0:T(8,128)(2,1)} %param.6), kind=kOutput, calls=%fused_computation.4 | convolution fusion | flops 528629760 | bytes 4046848 | tf_op jit(solution)/shard_map/dot_general | solution.py:84
  80.4 0.2 copy.24
  80.5 0.1 stack.46
  80.6 0.1 constant_dynamic-update-slice_fusion
  80.7 0.4 reverse_select_fusion
  81.1 0.1 fusion.7
  81.2 0.2 copy.26
  81.4 3.1 %collective-permute-start.2 = (bf16[2,128,288]{2,0,1:T(2,128)(2,1)S(1)}, bf16[2,128,288]{2,0,1:T(2,128)(2,1)S(1)}, u32[]{:S(2)}, u32[]{:S(2)}) collective-permute-start(bf16[2,128,288]{2,0,1:T(2,128)(2,1)S(1)} %bitcast.51), channel_id=1, source_target_pairs={{0,480},{32,448},{64,416},{96,384},{128,352},{160,320},{192,288},{... | collective-permute-start | bytes 442376 | tf_op jit(solution)/shard_map/ppermute | solution.py:20
  84.5 0.2 copy.25
  84.7 0.4 copy.31
  85.1 1.1 %copy.32 = bf16[2,256,288]{1,2,0:T(8,128)(2,1)} copy(bf16[2,256,288]{2,0,1:T(2,128)(2,1)S(1)} %bitcast.43) | data formatting | bytes 589824 | tf_op jit(solution)/shard_map/reshape | solution.py:81
  86.2 7.2 %shard_map.59 = bf16[288,3584]{1,0:T(8,128)(2,1)} custom-call(bf16[256,3584]{1,0:T(8,128)(2,1)} %bitcast.38, bf16[256,3584]{1,0:T(8,128)(2,1)} %bitcast.9.other_ref, bf16[2,288,256]{2,1,0:T(8,128)(2,1)} %bitcast.44, bf16[288,3584]{1,0:T(8,128)(2,1)} %bitcast.41), custom_call_target="tpu_custom_call" | custom-call | tf_op jit(solution)/shard_map/pallas_call | solution.py:44
  93.4 0.6 maximum_bitcast_fusion
  94.0 1.1 %copy.33 = bf16[1,2,2,128,288]{3,4,2,1,0:T(8,128)(2,1)} copy(bf16[1,2,2,128,288]{4,2,3,1,0:T(2,128)(2,1)S(1)} %maximum_bitcast_fusion) | data formatting | bytes 589824
  (16 shorter events, 0.2 us)
Async XLA Ops:
  0.6 31.1 %copy-start.1 = (bf16[1,2,2,128,288]{3,4,2,1,0:T(8,128)(2,1)S(1)}, bf16[1,2,2,128,288]{3,4,2,1,0:T(8,128)(2,1)}, u32[]{:S(2)}) copy-start(bf16[1,2,2,128,288]{3,4,2,1,0:T(8,128)(2,1)} %param.5) | copy-start | bytes 884740
  31.8 18.6 %collective-permute-start = (bf16[1472,128]{1,0:T(8,128)(2,1)S(1)}, bf16[1472,128]{1,0:T(8,128)(2,1)S(1)}, u32[]{:S(2)}, u32[]{:S(2)}) collective-permute-start(bf16[1472,128]{1,0:T(8,128)(2,1)S(1)} %pad_maximum_fusion.1), channel_id=1, source_target_pairs={{0,480},{32,448},{64,416},{96,384},{128,352},{160,320},{192,288},{... | collective-permute-start | bytes 1130504 | tf_op jit(solution)/shard_map/ppermute | solution.py:20
  62.9 13.7 %copy-start = (bf16[2,4,4,8,3584]{4,3,2,1,0:T(8,128)(2,1)}, bf16[2,4,4,8,3584]{4,3,2,1,0:T(8,128)(2,1)S(1)}, u32[]{:S(2)}) copy-start(bf16[2,4,4,8,3584]{4,3,2,1,0:T(8,128)(2,1)S(1)} %pad_maximum_fusion) | copy-start | bytes 5505028
  62.9 14.6 %collective-permute-start.1 = (bf16[2,4,4,8,3584]{4,3,2,1,0:T(8,128)(2,1)S(1)}, bf16[2,4,4,8,3584]{4,3,2,1,0:T(8,128)(2,1)}, u32[]{:S(2)}, u32[]{:S(2)}) collective-permute-start(bf16[2,4,4,8,3584]{4,3,2,1,0:T(8,128)(2,1)S(1)} %pad_maximum_fusion), channel_id=1, source_target_pairs={{0,1},{1,0},{2,3},{3,2},{4,5},{5,4},{6,7},{7,6},{8,9},{9,8},{10,11... | collective-permute-start | bytes 5505032 | tf_op jit(solution)/shard_map/ppermute | solution.py:77
  81.4 12.0 %collective-permute-start.2 = (bf16[2,128,288]{2,0,1:T(2,128)(2,1)S(1)}, bf16[2,128,288]{2,0,1:T(2,128)(2,1)S(1)}, u32[]{:S(2)}, u32[]{:S(2)}) collective-permute-start(bf16[2,128,288]{2,0,1:T(2,128)(2,1)S(1)} %bitcast.51), channel_id=1, source_target_pairs={{0,480},{32,448},{64,416},{96,384},{128,352},{160,320},{192,288},{... | collective-permute-start | bytes 442376 | tf_op jit(solution)/shard_map/ppermute | solution.py:20

commit v16 on v15

--- a/solution.py
+++ b/solution.py
@@ -5,6 +5,7 @@
 from jax import lax
 from jax.experimental import pallas as pl
 from jax.experimental.pallas import tpu as pltpu
+from jax.experimental.layout import Layout, with_layout_constraint
 from jax.sharding import Mesh
 from jax.sharding import PartitionSpec as P
 
@@ -88,6 +89,7 @@
     new_weight = update(pieces[0], pieces[1], jnp.swapaxes(acts, 1, 2), own_weight, scale_factor, step_rate)
     returned = mirror(grad[1])
     grad_hidden = jnp.stack([grad[0], returned], axis=0)[None]
+    grad_hidden = with_layout_constraint(grad_hidden, Layout(major_to_minor=(0, 1, 2, 4, 3)))
     return (grad_hidden, new_weight[None])
 
 

time: 95.5 us -> 95 us (level)
    unnamed x6 -> x5, local copies, waits for them, and re-layouts: 1.17 us -> 0.08 us
  transfers between devices with their start and end apart: 3 -> 3, of which waited for: 0 -> 0; matrix products, arithmetic and copies ran while one was open for 5% -> 6% of each run, Pallas kernels for 8% -> 8%
where the time goes in v16:
time: 95 us; the launch traced here: 94.6 us
  blocking collectives  54.1 us (57%)
  starting transfers between devices  20.2 us (21%)
  Pallas kernels  7.19 us (8%)
  matrix products  5.17 us (5%)
  local copies, waits for them, and re-layouts  4.27 us (4%)
  other arithmetic  2.66 us (3%)
    all_gather x1, blocking collectives, shards(): own_rows = lax.all_gather(own_rows, 'dz', axis=1)  29.5 us
    all_gather x1, blocking collectives, shards(): lax.all_gather(own_rows[0], 'dx', axis=1)  12.5 us
    all_gather x1, blocking collectives, shards(): lax.all_gather(mirror_rows, 'dx', axis=1)  12.1 us
    ppermute x1, starting transfers between devices, shards(): other_rows = lax.ppermute(both_rows, 'dc', [(0, 1), (1, 0)])  11 us
    ppermute x2, starting transfers between devices, mirror(): return lax.ppermute(block, PIPE, route)  9.23 us
    pallas_call x1, Pallas kernels, update(): pl.pallas_call(functools.partial(update_kernel, scale=scale, rate=rate),...  7.19 us
    dot_general x2, matrix products, shards(): grad = jnp.dot(piece, own_weight.T, preferred_element_type=jnp.float32)  5.17 us
  transfers between devices with their start and end apart: 3, of which 0 were waited for; matrix products, arithmetic and copies ran while one was open for 6% of the time, Pallas kernels for 8%

profile of v16, /device:TPU:1, one launch (start us, length us, event | category | flops | bytes accessed | tf_op | source)
XLA Modules:
  0.0 94.6 jit_solution(17005189295250283859)
XLA Ops:
  0.6 1.1 %fusion.3 = bf16[1,2,2,4,3584]{4,3,2,1,0:T(4,128)(2,1)S(1)} fusion(bf16[1,2,2,4,3584]{4,3,2,1,0:T(4,128)(2,1)} %param.4, s32[2,2]{1,0:T(2,128)} %bitcast.53), kind=kLoop, calls=%fused_computation.12 | loop fusion | flops 114688 | bytes 229392 | tf_op jit(solution)/shard_map/jit(_where)/select_n | solution.py:69
  1.8 29.5 %all_gather.9 = bf16[2,4,8,3584]{3,2,1,0:T(8,128)(2,1)S(1)} all-gather(bf16[2,1,8,3584]{3,2,1,0:T(8,128)(2,1)S(1)} %pad_maximum_fusion.2), channel_id=1, replica_groups=mesh['py'=4,'pz'=4,'dz'=4,'dx'=4,'dc'=2] {'dz'}, dimensions={1}, use_global_device_ids=true | all-gather | bytes 573440 | tf_op jit(solution)/shard_map/all_gather | solution.py:72
  31.4 0.3 reshape_squeeze.3
  31.8 6.1 %collective-permute-start = (bf16[1472,128]{1,0:T(8,128)(2,1)S(1)}, bf16[1472,128]{1,0:T(8,128)(2,1)S(1)}, u32[]{:S(2)}, u32[]{:S(2)}) collective-permute-start(bf16[1472,128]{1,0:T(8,128)(2,1)S(1)} %pad_maximum_fusion.1), channel_id=1, source_target_pairs={{0,480},{32,448},{64,416},{96,384},{128,352},{160,320},{192,288},{... | collective-permute-start | bytes 1130504 | tf_op jit(solution)/shard_map/ppermute | solution.py:21
  37.9 12.5 %all-gather = bf16[1,4,32,3584]{3,2,1,0:T(8,128)(2,1)S(1)} all-gather(bf16[1,4,8,3584]{3,2,1,0:T(8,128)(2,1)S(1)} %get-tuple-element.2), channel_id=2, replica_groups=mesh['py'=4,'pz'=4,'dz'=4,'dx'=4,'dc'=2] {'dx'}, dimensions={2}, use_global_device_ids=true | all-gather | bytes 1146880 | tf_op jit(solution)/shard_map/all_gather | solution.py:76
  50.4 0.3 all_gather_reshape.4
  50.7 12.1 %all_gather.11 = bf16[4,4,8,3584]{3,2,1,0:T(8,128)(2,1)S(1)} all-gather(bf16[4,1,8,3584]{3,2,1,0:T(8,128)(2,1)S(1)} %bitcast.45), channel_id=1, replica_groups=mesh['py'=4,'pz'=4,'dz'=4,'dx'=4,'dc'=2] {'dx'}, dimensions={1}, use_global_device_ids=true | all-gather | bytes 1146880 | tf_op jit(solution)/shard_map/all_gather | solution.py:76
  62.7 0.2 pad_maximum_fusion
  62.9 11.0 %collective-permute-start.1 = (bf16[2,4,4,8,3584]{4,3,2,1,0:T(8,128)(2,1)S(1)}, bf16[2,4,4,8,3584]{4,3,2,1,0:T(8,128)(2,1)}, u32[]{:S(2)}, u32[]{:S(2)}) collective-permute-start(bf16[2,4,4,8,3584]{4,3,2,1,0:T(8,128)(2,1)S(1)} %pad_maximum_fusion), channel_id=1, source_target_pairs={{0,1},{1,0},{2,3},{3,2},{4,5},{5,4},{6,7},{7,6},{8,9},{9,8},{10,11... | collective-permute-start | bytes 5505032 | tf_op jit(solution)/shard_map/ppermute | solution.py:78
  74.0 0.2 copy.30
  74.2 0.1 copy.32
  74.3 2.3 %fusion = bf16[256,288]{0,1:T(8,128)(2,1)S(1)} fusion(bf16[256,3584]{1,0:T(8,128)(2,1)S(1)} %bitcast.37, bf16[1,288,3584]{2,1,0:T(8,128)(2,1)} %param.6), kind=kOutput, calls=%fused_computation.3 | convolution fusion | flops 528629760 | bytes 4046848 | tf_op jit(solution)/shard_map/dot_general | solution.py:85
  76.6 0.2 copy.24
  76.7 0.1 stack.45
  76.8 0.2 copy.31
  77.0 0.1 copy.33
  77.1 0.1 constant_dynamic-update-slice_fusion.1
  77.2 0.3 maximum_bitcast_fusion
  77.5 2.9 %fusion.1 = bf16[256,288]{0,1:T(8,128)(2,1)S(1)} fusion(bf16[256,3584]{1,0:T(8,128)(2,1)} %bitcast.9.other_ref, bf16[1,288,3584]{2,1,0:T(8,128)(2,1)} %param.6), kind=kOutput, calls=%fused_computation.4 | convolution fusion | flops 528629760 | bytes 4046848 | tf_op jit(solution)/shard_map/dot_general | solution.py:85
  80.4 0.2 copy.25
  80.6 0.1 constant_dynamic-update-slice_fusion
  80.7 0.4 reverse_select_fusion
  81.1 0.1 fusion.7
  81.2 0.2 copy.27
  81.4 0.2 copy.28
  81.6 3.1 %collective-permute-start.2 = (bf16[2,128,288]{1,2,0:T(8,128)(2,1)S(1)}, bf16[2,128,288]{1,2,0:T(8,128)(2,1)S(1)}, u32[]{:S(2)}, u32[]{:S(2)}) collective-permute-start(bf16[2,128,288]{1,2,0:T(8,128)(2,1)S(1)} %copy.28), channel_id=1, source_target_pairs={{0,480},{32,448},{64,416},{96,384},{128,352},{160,320},{192,288},{... | collective-permute-start | bytes 442376 | tf_op jit(solution)/shard_map/ppermute | solution.py:21
  84.7 0.2 copy.26
  84.9 0.2 copy.29
  85.1 0.4 copy.34
  85.5 1.1 %copy.35 = bf16[2,256,288]{1,2,0:T(8,128)(2,1)} copy(bf16[2,256,288]{2,0,1:T(2,128)(2,1)S(1)} %bitcast.43) | data formatting | bytes 589824 | tf_op jit(solution)/shard_map/reshape | solution.py:82
  86.6 7.2 %shard_map.59 = bf16[288,3584]{1,0:T(8,128)(2,1)} custom-call(bf16[256,3584]{1,0:T(8,128)(2,1)} %bitcast.38, bf16[256,3584]{1,0:T(8,128)(2,1)} %bitcast.9.other_ref, bf16[2,288,256]{2,1,0:T(8,128)(2,1)} %bitcast.44, bf16[288,3584]{1,0:T(8,128)(2,1)} %bitcast.41), custom_call_target="tpu_custom_call" | custom-call | tf_op jit(solution)/shard_map/pallas_call | solution.py:45
  93.8 0.7 maximum_bitcast_fusion.1
  (17 shorter events, 0.3 us)
Async XLA Ops:
  0.6 31.1 %copy-start.1 = (bf16[1,2,2,128,288]{3,4,2,1,0:T(8,128)(2,1)S(1)}, bf16[1,2,2,128,288]{3,4,2,1,0:T(8,128)(2,1)}, u32[]{:S(2)}) copy-start(bf16[1,2,2,128,288]{3,4,2,1,0:T(8,128)(2,1)} %param.5) | copy-start | bytes 884740
  31.8 18.6 %collective-permute-start = (bf16[1472,128]{1,0:T(8,128)(2,1)S(1)}, bf16[1472,128]{1,0:T(8,128)(2,1)S(1)}, u32[]{:S(2)}, u32[]{:S(2)}) collective-permute-start(bf16[1472,128]{1,0:T(8,128)(2,1)S(1)} %pad_maximum_fusion.1), channel_id=1, source_target_pairs={{0,480},{32,448},{64,416},{96,384},{128,352},{160,320},{192,288},{... | collective-permute-start | bytes 1130504 | tf_op jit(solution)/shard_map/ppermute | solution.py:21
  62.9 13.7 %copy-start = (bf16[2,4,4,8,3584]{4,3,2,1,0:T(8,128)(2,1)}, bf16[2,4,4,8,3584]{4,3,2,1,0:T(8,128)(2,1)S(1)}, u32[]{:S(2)}) copy-start(bf16[2,4,4,8,3584]{4,3,2,1,0:T(8,128)(2,1)S(1)} %pad_maximum_fusion) | copy-start | bytes 5505028
  62.9 14.6 %collective-permute-start.1 = (bf16[2,4,4,8,3584]{4,3,2,1,0:T(8,128)(2,1)S(1)}, bf16[2,4,4,8,3584]{4,3,2,1,0:T(8,128)(2,1)}, u32[]{:S(2)}, u32[]{:S(2)}) collective-permute-start(bf16[2,4,4,8,3584]{4,3,2,1,0:T(8,128)(2,1)S(1)} %pad_maximum_fusion), channel_id=1, source_target_pairs={{0,1},{1,0},{2,3},{3,2},{4,5},{5,4},{6,7},{7,6},{8,9},{9,8},{10,11... | collective-permute-start | bytes 5505032 | tf_op jit(solution)/shard_map/ppermute | solution.py:78
  81.6 12.2 %collective-permute-start.2 = (bf16[2,128,288]{1,2,0:T(8,128)(2,1)S(1)}, bf16[2,128,288]{1,2,0:T(8,128)(2,1)S(1)}, u32[]{:S(2)}, u32[]{:S(2)}) collective-permute-start(bf16[2,128,288]{1,2,0:T(8,128)(2,1)S(1)} %copy.28), channel_id=1, source_target_pairs={{0,480},{32,448},{64,416},{96,384},{128,352},{160,320},{192,288},{... | collective-permute-start | bytes 442376 | tf_op jit(solution)/shard_map/ppermute | solution.py:21

commit v17 on v16

--- a/solution.py
+++ b/solution.py
@@ -34,12 +34,13 @@
 
 
 def update_kernel(own_ref, other_ref, acts_ref, weight_ref, out_ref, *, scale, rate):
-    part = jnp.dot(acts_ref[0], own_ref[...], preferred_element_type=jnp.float32)
-    part = part + jnp.dot(acts_ref[1], other_ref[...], preferred_element_type=jnp.float32)
+    rows_first = (((0,), (0,)), ((), ()))
+    part = lax.dot_general(acts_ref[0], own_ref[...], rows_first, preferred_element_type=jnp.float32)
+    part = part + lax.dot_general(acts_ref[1], other_ref[...], rows_first, preferred_element_type=jnp.float32)
     out_ref[...] = (weight_ref[...].astype(jnp.float32) - rate * (part * scale)).astype(out_ref.dtype)
 
 
-def update(own, other, acts_t, weight, scale, rate, chunk=512):
+def update(own, other, acts, weight, scale, rate, chunk=896):
     rows, width = own.shape
     share = weight.shape[0]
     return pl.pallas_call(
@@ -48,13 +49,13 @@
         in_specs=[
             pl.BlockSpec((rows, chunk), lambda i: (0, i)),
             pl.BlockSpec((rows, chunk), lambda i: (0, i)),
-            pl.BlockSpec((2, share, rows), lambda i: (0, 0, 0)),
+            pl.BlockSpec((2, rows, share), lambda i: (0, 0, 0)),
             pl.BlockSpec((share, chunk), lambda i: (0, i)),
         ],
         out_specs=pl.BlockSpec((share, chunk), lambda i: (0, i)),
         out_shape=jax.ShapeDtypeStruct((share, width), weight.dtype),
         compiler_params=pltpu.CompilerParams(dimension_semantics=("parallel",)),
-    )(own, other, acts_t, weight)
+    )(own, other, acts, weight)
 
 
 def shards(grad_out, hidden, weights, counts):
@@ -86,7 +87,7 @@
         grads.append((grad * scale_factor).astype(jnp.bfloat16))
     grad = own_first(jnp.stack(grads, axis=0).reshape(n_c, 2, n_z, n_x, micro, row_total, share))
     grad = grad.transpose(1, 4, 2, 3, 0, 5, 6).reshape(2, micro, tokens, share)
-    new_weight = update(pieces[0], pieces[1], jnp.swapaxes(acts, 1, 2), own_weight, scale_factor, step_rate)
+    new_weight = update(pieces[0], pieces[1], acts, own_weight, scale_factor, step_rate)
     returned = mirror(grad[1])
     grad_hidden = jnp.stack([grad[0], returned], axis=0)[None]
     grad_hidden = with_layout_constraint(grad_hidden, Layout(major_to_minor=(0, 1, 2, 4, 3)))

time: 95 us -> 93.6 us (0.985)
  Pallas kernels: 7.19 us -> 5.61 us
    pallas_call x1, Pallas kernels: 7.19 us -> 5.61 us  [update(): pl.pallas_call(functools.partial(update_kernel, scale=scale, rate=rate),...]
  transfers between devices with their start and end apart: 3 -> 3, of which waited for: 0 -> 1; matrix products, arithmetic and copies ran while one was open for 6% -> 5% of each run, Pallas kernels for 8% -> 6%
where the time goes in v17:
time: 93.6 us; the launch traced here: 93.3 us
  blocking collectives  54.1 us (58%)
  starting transfers between devices  20.2 us (22%)
  Pallas kernels  5.61 us (6%)
  matrix products  5.17 us (6%)
  local copies, waits for them, and re-layouts  3.98 us (4%)
  other arithmetic  2.66 us (3%)
    all_gather x1, blocking collectives, shards(): own_rows = lax.all_gather(own_rows, 'dz', axis=1)  29.5 us
    all_gather x1, blocking collectives, shards(): lax.all_gather(own_rows[0], 'dx', axis=1)  12.5 us
    all_gather x1, blocking collectives, shards(): lax.all_gather(mirror_rows, 'dx', axis=1)  12.1 us
    ppermute x1, starting transfers between devices, shards(): other_rows = lax.ppermute(both_rows, 'dc', [(0, 1), (1, 0)])  11 us
    ppermute x2, starting transfers between devices, mirror(): return lax.ppermute(block, PIPE, route)  9.23 us
    pallas_call x1, Pallas kernels, update(): pl.pallas_call(functools.partial(update_kernel, scale=scale, rate=rate),...  5.61 us
    dot_general x2, matrix products, shards(): grad = jnp.dot(piece, own_weight.T, preferred_element_type=jnp.float32)  5.17 us
  transfers between devices with their start and end apart: 3, of which 1 were waited for; matrix products, arithmetic and copies ran while one was open for 5% of the time, Pallas kernels for 6%

profile of v17, /device:TPU:1, one launch (start us, length us, event | category | flops | bytes accessed | tf_op | source)
XLA Modules:
  0.0 93.3 jit_solution(9105662557436034559)
XLA Ops:
  0.6 1.1 %fusion.3 = bf16[1,2,2,4,3584]{4,3,2,1,0:T(4,128)(2,1)S(1)} fusion(bf16[1,2,2,4,3584]{4,3,2,1,0:T(4,128)(2,1)} %param.4, s32[2,2]{1,0:T(2,128)} %bitcast.51), kind=kLoop, calls=%fused_computation.12 | loop fusion | flops 114688 | bytes 229392 | tf_op jit(solution)/shard_map/jit(_where)/select_n | solution.py:70
  1.8 29.5 %all_gather.9 = bf16[2,4,8,3584]{3,2,1,0:T(8,128)(2,1)S(1)} all-gather(bf16[2,1,8,3584]{3,2,1,0:T(8,128)(2,1)S(1)} %pad_maximum_fusion.2), channel_id=1, replica_groups=mesh['py'=4,'pz'=4,'dz'=4,'dx'=4,'dc'=2] {'dz'}, dimensions={1}, use_global_device_ids=true | all-gather | bytes 573440 | tf_op jit(solution)/shard_map/all_gather | solution.py:73
  31.4 0.3 reshape_squeeze.3
  31.8 6.1 %collective-permute-start = (bf16[1472,128]{1,0:T(8,128)(2,1)S(1)}, bf16[1472,128]{1,0:T(8,128)(2,1)S(1)}, u32[]{:S(2)}, u32[]{:S(2)}) collective-permute-start(bf16[1472,128]{1,0:T(8,128)(2,1)S(1)} %pad_maximum_fusion.1), channel_id=1, source_target_pairs={{0,480},{32,448},{64,416},{96,384},{128,352},{160,320},{192,288},{... | collective-permute-start | bytes 1130504 | tf_op jit(solution)/shard_map/ppermute | solution.py:21
  37.9 12.5 %all-gather = bf16[1,4,32,3584]{3,2,1,0:T(8,128)(2,1)S(1)} all-gather(bf16[1,4,8,3584]{3,2,1,0:T(8,128)(2,1)S(1)} %get-tuple-element.2), channel_id=2, replica_groups=mesh['py'=4,'pz'=4,'dz'=4,'dx'=4,'dc'=2] {'dx'}, dimensions={2}, use_global_device_ids=true | all-gather | bytes 1146880 | tf_op jit(solution)/shard_map/all_gather | solution.py:77
  50.4 0.3 all_gather_reshape.4
  50.7 12.1 %all_gather.11 = bf16[4,4,8,3584]{3,2,1,0:T(8,128)(2,1)S(1)} all-gather(bf16[4,1,8,3584]{3,2,1,0:T(8,128)(2,1)S(1)} %bitcast.43), channel_id=1, replica_groups=mesh['py'=4,'pz'=4,'dz'=4,'dx'=4,'dc'=2] {'dx'}, dimensions={1}, use_global_device_ids=true | all-gather | bytes 1146880 | tf_op jit(solution)/shard_map/all_gather | solution.py:77
  62.7 0.2 pad_maximum_fusion
  62.9 11.0 %collective-permute-start.1 = (bf16[2,4,4,8,3584]{4,3,2,1,0:T(8,128)(2,1)S(1)}, bf16[2,4,4,8,3584]{4,3,2,1,0:T(8,128)(2,1)}, u32[]{:S(2)}, u32[]{:S(2)}) collective-permute-start(bf16[2,4,4,8,3584]{4,3,2,1,0:T(8,128)(2,1)S(1)} %pad_maximum_fusion), channel_id=1, source_target_pairs={{0,1},{1,0},{2,3},{3,2},{4,5},{5,4},{6,7},{7,6},{8,9},{9,8},{10,11... | collective-permute-start | bytes 5505032 | tf_op jit(solution)/shard_map/ppermute | solution.py:79
  74.0 0.2 copy.32
  74.2 0.1 copy.34
  74.3 2.3 %fusion = bf16[256,288]{0,1:T(8,128)(2,1)S(1)} fusion(bf16[256,3584]{1,0:T(8,128)(2,1)S(1)} %bitcast.36, bf16[1,288,3584]{2,1,0:T(8,128)(2,1)} %param.6), kind=kOutput, calls=%fused_computation.3 | convolution fusion | flops 528629760 | bytes 4046848 | tf_op jit(solution)/shard_map/dot_general | solution.py:86
  76.6 0.2 copy.26
  76.8 0.2 copy.33
  77.0 0.1 copy.35
  77.1 0.1 constant_dynamic-update-slice_fusion.1
  77.2 0.3 maximum_bitcast_fusion
  77.5 2.9 %fusion.1 = bf16[256,288]{0,1:T(8,128)(2,1)S(1)} fusion(bf16[256,3584]{1,0:T(8,128)(2,1)} %bitcast.9.other_ref, bf16[1,288,3584]{2,1,0:T(8,128)(2,1)} %param.6), kind=kOutput, calls=%fused_computation.4 | convolution fusion | flops 528629760 | bytes 4046848 | tf_op jit(solution)/shard_map/dot_general | solution.py:86
  80.4 0.2 copy.27
  80.6 0.1 constant_dynamic-update-slice_fusion
  80.7 0.4 reverse_select_fusion
  81.1 0.1 fusion.7
  81.2 0.2 copy.29
  81.4 0.2 copy.30
  81.6 3.1 %collective-permute-start.2 = (bf16[2,128,288]{1,2,0:T(8,128)(2,1)S(1)}, bf16[2,128,288]{1,2,0:T(8,128)(2,1)S(1)}, u32[]{:S(2)}, u32[]{:S(2)}) collective-permute-start(bf16[2,128,288]{1,2,0:T(8,128)(2,1)S(1)} %copy.30), channel_id=1, source_target_pairs={{0,480},{32,448},{64,416},{96,384},{128,352},{160,320},{192,288},{... | collective-permute-start | bytes 442376 | tf_op jit(solution)/shard_map/ppermute | solution.py:21
  84.7 0.2 copy.28
  84.9 0.2 copy.31
  85.1 0.4 copy.36
  85.5 0.8 copy.37.acts_ref
  86.3 5.6 %shard_map.59 = bf16[288,3584]{1,0:T(8,128)(2,1)} custom-call(bf16[256,3584]{1,0:T(8,128)(2,1)} %bitcast.37, bf16[256,3584]{1,0:T(8,128)(2,1)} %bitcast.9.other_ref, bf16[2,256,288]{2,1,0:T(8,128)(2,1)} %copy.37.acts_ref, bf16[288,3584]{1,0:T(8,128)(2,1)} %bitcast.40), custom_call_target="tpu_custom_call" | custom-call | tf_op jit(solution)/shard_map/pallas_call | solution.py:46
  91.9 0.6 collective-permute-done.2
  92.6 0.7 maximum_bitcast_fusion.1
  (17 shorter events, 0.3 us)
Async XLA Ops:
  0.6 31.1 %copy-start.1 = (bf16[1,2,2,128,288]{3,4,2,1,0:T(8,128)(2,1)S(1)}, bf16[1,2,2,128,288]{3,4,2,1,0:T(8,128)(2,1)}, u32[]{:S(2)}) copy-start(bf16[1,2,2,128,288]{3,4,2,1,0:T(8,128)(2,1)} %param.5) | copy-start | bytes 884740
  31.8 18.6 %collective-permute-start = (bf16[1472,128]{1,0:T(8,128)(2,1)S(1)}, bf16[1472,128]{1,0:T(8,128)(2,1)S(1)}, u32[]{:S(2)}, u32[]{:S(2)}) collective-permute-start(bf16[1472,128]{1,0:T(8,128)(2,1)S(1)} %pad_maximum_fusion.1), channel_id=1, source_target_pairs={{0,480},{32,448},{64,416},{96,384},{128,352},{160,320},{192,288},{... | collective-permute-start | bytes 1130504 | tf_op jit(solution)/shard_map/ppermute | solution.py:21
  62.9 13.7 %copy-start = (bf16[2,4,4,8,3584]{4,3,2,1,0:T(8,128)(2,1)}, bf16[2,4,4,8,3584]{4,3,2,1,0:T(8,128)(2,1)S(1)}, u32[]{:S(2)}) copy-start(bf16[2,4,4,8,3584]{4,3,2,1,0:T(8,128)(2,1)S(1)} %pad_maximum_fusion) | copy-start | bytes 5505028
  62.9 14.6 %collective-permute-start.1 = (bf16[2,4,4,8,3584]{4,3,2,1,0:T(8,128)(2,1)S(1)}, bf16[2,4,4,8,3584]{4,3,2,1,0:T(8,128)(2,1)}, u32[]{:S(2)}, u32[]{:S(2)}) collective-permute-start(bf16[2,4,4,8,3584]{4,3,2,1,0:T(8,128)(2,1)S(1)} %pad_maximum_fusion), channel_id=1, source_target_pairs={{0,1},{1,0},{2,3},{3,2},{4,5},{5,4},{6,7},{7,6},{8,9},{9,8},{10,11... | collective-permute-start | bytes 5505032 | tf_op jit(solution)/shard_map/ppermute | solution.py:79
  81.6 10.9 %collective-permute-start.2 = (bf16[2,128,288]{1,2,0:T(8,128)(2,1)S(1)}, bf16[2,128,288]{1,2,0:T(8,128)(2,1)S(1)}, u32[]{:S(2)}, u32[]{:S(2)}) collective-permute-start(bf16[2,128,288]{1,2,0:T(8,128)(2,1)S(1)} %copy.30), channel_id=1, source_target_pairs={{0,480},{32,448},{64,416},{96,384},{128,352},{160,320},{192,288},{... | collective-permute-start | bytes 442376 | tf_op jit(solution)/shard_map/ppermute | solution.py:21

commit v18 on v17

--- a/solution.py
+++ b/solution.py
@@ -58,6 +58,36 @@
     )(own, other, acts, weight)
 
 
+def grad_kernel(rows_ref, weight_ref, out_ref, acc_ref, *, scale):
+    step = pl.program_id(0)
+
+    @pl.when(step == 0)
+    def _():
+        acc_ref[...] = jnp.zeros_like(acc_ref)
+
+    acc_ref[...] += lax.dot_general(
+        rows_ref[...], weight_ref[...], (((1,), (1,)), ((), ())), preferred_element_type=jnp.float32
+    )
+
+    @pl.when(step == pl.num_programs(0) - 1)
+    def _():
+        out_ref[...] = (acc_ref[...] * scale).astype(out_ref.dtype)
+
+
+def row_grad(rows, weight, scale, chunk=896):
+    count, width = rows.shape
+    share = weight.shape[0]
+    return pl.pallas_call(
+        functools.partial(grad_kernel, scale=scale),
+        grid=(width // chunk,),
+        in_specs=[pl.BlockSpec((count, chunk), lambda i: (0, i)), pl.BlockSpec((share, chunk), lambda i: (0, i))],
+        out_specs=pl.BlockSpec((count, share), lambda i: (0, 0)),
+        out_shape=jax.ShapeDtypeStruct((count, share), rows.dtype),
+        scratch_shapes=[pltpu.VMEM((count, share), jnp.float32)],
+        compiler_params=pltpu.CompilerParams(dimension_semantics=("arbitrary",)),
+    )(rows, weight)
+
+
 def shards(grad_out, hidden, weights, counts):
     row_total = grad_out.shape[3]
     full_width = grad_out.shape[4]
@@ -81,10 +111,7 @@
     pieces = [both_rows.reshape(-1, full_width), other_rows.reshape(-1, full_width)]
     acts = both_hidden.reshape(2, micro, n_z, n_x, n_c, row_total, share).transpose(4, 0, 2, 3, 1, 5, 6)
     acts = own_first(acts).reshape(n_c, -1, share)
-    grads = []
-    for piece in pieces:
-        grad = jnp.dot(piece, own_weight.T, preferred_element_type=jnp.float32)
-        grads.append((grad * scale_factor).astype(jnp.bfloat16))
+    grads = [row_grad(piece, own_weight, scale_factor) for piece in pieces]
     grad = own_first(jnp.stack(grads, axis=0).reshape(n_c, 2, n_z, n_x, micro, row_total, share))
     grad = grad.transpose(1, 4, 2, 3, 0, 5, 6).reshape(2, micro, tokens, share)
     new_weight = update(pieces[0], pieces[1], acts, own_weight, scale_factor, step_rate)

time: 93.6 us -> 99.4 us (1.062)
  Pallas kernels: 5.61 us -> 14.6 us
  matrix products: 5.17 us -> 0 us
  local copies, waits for them, and re-layouts: 3.98 us -> 5.5 us
    pallas_call x0 -> x2, Pallas kernels: none -> 8.98 us  [row_grad(): pl.pallas_call(functools.partial(grad_kernel, scale=scale), grid=(width /...]
    dot_general x2 -> x0, matrix products: 5.17 us -> none  [shards(): grad = jnp.dot(piece, own_weight.T, preferred_element_type=jnp.float32)]
    another operation x3, local copies, waits for them, and re-layouts: 0.22 us -> 2.06 us  [shards(): jnp.stack(grads, axis=0).reshape(n_c, 2, n_z, n_x, micro, row_total, share)]
  transfers between devices with their start and end apart: 3 -> 3, of which waited for: 1 -> 1; matrix products, arithmetic and copies ran while one was open for 5% -> 4% of each run, Pallas kernels for 6% -> 10%
where the time goes in v18:
time: 99.4 us; the launch traced here: 99 us
  blocking collectives  54.1 us (54%)
  starting transfers between devices  20.3 us (20%)
  Pallas kernels  14.6 us (15%)
  local copies, waits for them, and re-layouts  5.5 us (6%)
  other arithmetic  2.66 us (3%)
  waiting for transfers between devices  1 us (1%)
    all_gather x1, blocking collectives, shards(): own_rows = lax.all_gather(own_rows, 'dz', axis=1)  29.5 us
    all_gather x1, blocking collectives, shards(): lax.all_gather(own_rows[0], 'dx', axis=1)  12.5 us
    all_gather x1, blocking collectives, shards(): lax.all_gather(mirror_rows, 'dx', axis=1)  12.1 us
    ppermute x1, starting transfers between devices, shards(): other_rows = lax.ppermute(both_rows, 'dc', [(0, 1), (1, 0)])  11 us
    ppermute x2, starting transfers between devices, mirror(): return lax.ppermute(block, PIPE, route)  9.23 us
    pallas_call x2, Pallas kernels, row_grad(): pl.pallas_call(functools.partial(grad_kernel, scale=scale), grid=(width /...  8.98 us
    pallas_call x1, Pallas kernels, update(): pl.pallas_call(functools.partial(update_kernel, scale=scale, rate=rate),...  5.61 us
    another operation x3, local copies, waits for them, and re-layouts, shards(): jnp.stack(grads, axis=0).reshape(n_c, 2, n_z, n_x, micro, row_total, share)  2.06 us
  transfers between devices with their start and end apart: 3, of which 1 were waited for; matrix products, arithmetic and copies ran while one was open for 4% of the time, Pallas kernels for 10%

profile of v18, /device:TPU:1, one launch (start us, length us, event | category | flops | bytes accessed | tf_op | source)
XLA Modules:
  0.0 99.0 jit_solution(6328762885104444984)
XLA Ops:
  0.6 1.1 %fusion.1 = bf16[1,2,2,4,3584]{4,3,2,1,0:T(4,128)(2,1)S(1)} fusion(bf16[1,2,2,4,3584]{4,3,2,1,0:T(4,128)(2,1)} %param.4, s32[2,2]{1,0:T(2,128)} %bitcast.47), kind=kLoop, calls=%fused_computation.8 | loop fusion | flops 114688 | bytes 229392 | tf_op jit(solution)/shard_map/jit(_where)/select_n | solution.py:100
  1.8 29.5 %all_gather.9 = bf16[2,4,8,3584]{3,2,1,0:T(8,128)(2,1)S(1)} all-gather(bf16[2,1,8,3584]{3,2,1,0:T(8,128)(2,1)S(1)} %pad_maximum_fusion.2), channel_id=1, replica_groups=mesh['py'=4,'pz'=4,'dz'=4,'dx'=4,'dc'=2] {'dz'}, dimensions={1}, use_global_device_ids=true | all-gather | bytes 573440 | tf_op jit(solution)/shard_map/all_gather | solution.py:103
  31.4 0.3 reshape_squeeze.3
  31.8 6.1 %collective-permute-start = (bf16[1472,128]{1,0:T(8,128)(2,1)S(1)}, bf16[1472,128]{1,0:T(8,128)(2,1)S(1)}, u32[]{:S(2)}, u32[]{:S(2)}) collective-permute-start(bf16[1472,128]{1,0:T(8,128)(2,1)S(1)} %pad_maximum_fusion.1), channel_id=1, source_target_pairs={{0,480},{32,448},{64,416},{96,384},{128,352},{160,320},{192,288},{... | collective-permute-start | bytes 1130504 | tf_op jit(solution)/shard_map/ppermute | solution.py:21
  37.9 12.5 %all-gather = bf16[1,4,32,3584]{3,2,1,0:T(8,128)(2,1)S(1)} all-gather(bf16[1,4,8,3584]{3,2,1,0:T(8,128)(2,1)S(1)} %get-tuple-element.2), channel_id=2, replica_groups=mesh['py'=4,'pz'=4,'dz'=4,'dx'=4,'dc'=2] {'dx'}, dimensions={2}, use_global_device_ids=true | all-gather | bytes 1146880 | tf_op jit(solution)/shard_map/all_gather | solution.py:107
  50.4 0.3 all_gather_reshape.4
  50.7 12.1 %all_gather.11 = bf16[4,4,8,3584]{3,2,1,0:T(8,128)(2,1)S(1)} all-gather(bf16[4,1,8,3584]{3,2,1,0:T(8,128)(2,1)S(1)} %bitcast.39), channel_id=1, replica_groups=mesh['py'=4,'pz'=4,'dz'=4,'dx'=4,'dc'=2] {'dx'}, dimensions={1}, use_global_device_ids=true | all-gather | bytes 1146880 | tf_op jit(solution)/shard_map/all_gather | solution.py:107
  62.7 0.2 pad_maximum_fusion
  62.9 11.0 %collective-permute-start.1 = (bf16[2,4,4,8,3584]{4,3,2,1,0:T(8,128)(2,1)S(1)}, bf16[2,4,4,8,3584]{4,3,2,1,0:T(8,128)(2,1)}, u32[]{:S(2)}, u32[]{:S(2)}) collective-permute-start(bf16[2,4,4,8,3584]{4,3,2,1,0:T(8,128)(2,1)S(1)} %pad_maximum_fusion), channel_id=1, source_target_pairs={{0,1},{1,0},{2,3},{3,2},{4,5},{5,4},{6,7},{7,6},{8,9},{9,8},{10,11... | collective-permute-start | bytes 5505032 | tf_op jit(solution)/shard_map/ppermute | solution.py:109
  74.0 0.2 copy.26
  74.2 0.1 copy.28
  74.3 4.5 %shard_map.59 = bf16[256,288]{1,0:T(8,128)(2,1)} custom-call(bf16[256,3584]{1,0:T(8,128)(2,1)} %bitcast.33, bf16[288,3584]{1,0:T(8,128)(2,1)} %bitcast.30), custom_call_target="tpu_custom_call" | custom-call | tf_op jit(solution)/shard_map/pallas_call | solution.py:80
  78.8 1.0 stack.45
  79.8 0.2 copy.27
  80.0 0.1 copy.29
  80.0 0.1 constant_dynamic-update-slice_fusion.1
  80.1 0.3 maximum_bitcast_fusion
  80.4 4.5 %shard_map.60 = bf16[256,288]{1,0:T(8,128)(2,1)} custom-call(bf16[256,3584]{1,0:T(8,128)(2,1)} %bitcast.9.rows_ref.other_ref, bf16[288,3584]{1,0:T(8,128)(2,1)} %bitcast.31), custom_call_target="tpu_custom_call" | custom-call | tf_op jit(solution)/shard_map/pallas_call | solution.py:80
  84.9 1.0 stack.46
  85.9 0.1 constant_dynamic-update-slice_fusion
  86.0 0.4 reverse_select_fusion
  86.4 0.1 fusion.3
  86.5 0.2 copy.23
  86.7 0.2 copy.24
  86.9 3.1 %collective-permute-start.2 = (bf16[2,128,288]{1,2,0:T(8,128)(2,1)S(1)}, bf16[2,128,288]{1,2,0:T(8,128)(2,1)S(1)}, u32[]{:S(2)}, u32[]{:S(2)}) collective-permute-start(bf16[2,128,288]{1,2,0:T(8,128)(2,1)S(1)} %copy.24), channel_id=1, source_target_pairs={{0,480},{32,448},{64,416},{96,384},{128,352},{160,320},{192,288},{... | collective-permute-start | bytes 442376 | tf_op jit(solution)/shard_map/ppermute | solution.py:21
  90.0 0.2 copy.22
  90.2 0.2 copy.25
  90.4 0.4 copy.30
  90.8 0.8 copy.31.acts_ref
  91.6 5.6 %shard_map.61 = bf16[288,3584]{1,0:T(8,128)(2,1)} custom-call(bf16[256,3584]{1,0:T(8,128)(2,1)} %bitcast.34, bf16[256,3584]{1,0:T(8,128)(2,1)} %bitcast.9.rows_ref.other_ref, bf16[2,256,288]{2,1,0:T(8,128)(2,1)} %copy.31.acts_ref, bf16[288,3584]{1,0:T(8,128)(2,1)} %bitcast.32), custom_call_target="tpu_custom_call" | custom-call | tf_op jit(solution)/shard_map/pallas_call | solution.py:46
  97.2 1.0 %collective-permute-done.2 = bf16[2,128,288]{1,2,0:T(8,128)(2,1)S(1)} collective-permute-done((bf16[2,128,288]{1,2,0:T(8,128)(2,1)S(1)}, bf16[2,128,288]{1,2,0:T(8,128)(2,1)S(1)}, u32[]{:S(2)}, u32[]{:S(2)}) %collective-permute-start.2) | collective-permute-done | bytes 147488 | tf_op jit(solution)/shard_map/ppermute | solution.py:21
  98.2 0.7 maximum_bitcast_fusion.1
  (15 shorter events, 0.2 us)
Async XLA Ops:
  0.6 31.1 %copy-start.1 = (bf16[1,2,2,128,288]{3,4,2,1,0:T(8,128)(2,1)S(1)}, bf16[1,2,2,128,288]{3,4,2,1,0:T(8,128)(2,1)}, u32[]{:S(2)}) copy-start(bf16[1,2,2,128,288]{3,4,2,1,0:T(8,128)(2,1)} %param.5) | copy-start | bytes 884740
  31.8 18.6 %collective-permute-start = (bf16[1472,128]{1,0:T(8,128)(2,1)S(1)}, bf16[1472,128]{1,0:T(8,128)(2,1)S(1)}, u32[]{:S(2)}, u32[]{:S(2)}) collective-permute-start(bf16[1472,128]{1,0:T(8,128)(2,1)S(1)} %pad_maximum_fusion.1), channel_id=1, source_target_pairs={{0,480},{32,448},{64,416},{96,384},{128,352},{160,320},{192,288},{... | collective-permute-start | bytes 1130504 | tf_op jit(solution)/shard_map/ppermute | solution.py:21
  62.9 11.3 %copy-start = (bf16[2,4,4,8,3584]{4,3,2,1,0:T(8,128)(2,1)}, bf16[2,4,4,8,3584]{4,3,2,1,0:T(8,128)(2,1)S(1)}, u32[]{:S(2)}) copy-start(bf16[2,4,4,8,3584]{4,3,2,1,0:T(8,128)(2,1)S(1)} %pad_maximum_fusion) | copy-start | bytes 5505028
  62.9 17.5 %collective-permute-start.1 = (bf16[2,4,4,8,3584]{4,3,2,1,0:T(8,128)(2,1)S(1)}, bf16[2,4,4,8,3584]{4,3,2,1,0:T(8,128)(2,1)}, u32[]{:S(2)}, u32[]{:S(2)}) collective-permute-start(bf16[2,4,4,8,3584]{4,3,2,1,0:T(8,128)(2,1)S(1)} %pad_maximum_fusion), channel_id=1, source_target_pairs={{0,1},{1,0},{2,3},{3,2},{4,5},{5,4},{6,7},{7,6},{8,9},{9,8},{10,11... | collective-permute-start | bytes 5505032 | tf_op jit(solution)/shard_map/ppermute | solution.py:109
  86.9 11.3 %collective-permute-start.2 = (bf16[2,128,288]{1,2,0:T(8,128)(2,1)S(1)}, bf16[2,128,288]{1,2,0:T(8,128)(2,1)S(1)}, u32[]{:S(2)}, u32[]{:S(2)}) collective-permute-start(bf16[2,128,288]{1,2,0:T(8,128)(2,1)S(1)} %copy.24), channel_id=1, source_target_pairs={{0,480},{32,448},{64,416},{96,384},{128,352},{160,320},{192,288},{... | collective-permute-start | bytes 442376 | tf_op jit(solution)/shard_map/ppermute | solution.py:21

commit v19 on v17

--- a/solution.py
+++ b/solution.py
@@ -73,10 +73,9 @@
     own_rows = lax.all_gather(own_rows, "dz", axis=1)
     mirror_rows, mirror_hidden = mirror_pair(own_rows[1], jnp.swapaxes(hidden[0, 1], -1, -2))
     mirror_hidden = jnp.swapaxes(mirror_hidden, -1, -2)
-    both_rows = jnp.stack(
-        [lax.all_gather(own_rows[0], "dx", axis=1), lax.all_gather(mirror_rows, "dx", axis=1)], axis=0
-    )
-    other_rows = lax.ppermute(both_rows, "dc", [(0, 1), (1, 0)])
+    slot_rows = [lax.all_gather(own_rows[0], "dx", axis=1), lax.all_gather(mirror_rows, "dx", axis=1)]
+    other_rows = jnp.stack([lax.ppermute(rows, "dc", [(0, 1), (1, 0)]) for rows in slot_rows], axis=0)
+    both_rows = jnp.stack(slot_rows, axis=0)
     both_hidden = jnp.stack([hidden[0, 0], mirror_hidden], axis=0)
     pieces = [both_rows.reshape(-1, full_width), other_rows.reshape(-1, full_width)]
     acts = both_hidden.reshape(2, micro, n_z, n_x, n_c, row_total, share).transpose(4, 0, 2, 3, 1, 5, 6)

time: 93.6 us -> 98.7 us (1.054)
  matrix products: 5.17 us -> 1.44 us
  other arithmetic: 2.66 us -> 5.75 us
  local copies, waits for them, and re-layouts: 3.98 us -> 6.18 us
  starting transfers between devices: 20.2 us -> 21.9 us
  blocking collectives: 54.1 us -> 55.5 us
    dot_general x2, matrix products: 5.17 us -> 1.44 us  [shards(): grad = jnp.dot(piece, own_weight.T, preferred_element_type=jnp.float32)]
    another operation x1 -> x2, other arithmetic: 0.17 us -> 3.27 us  [the longest x1 1.77 us: shards(): jnp.stack([lax.ppermute(rows, 'dc', [(0, 1), (1, 0)]) for rows in slot_ro...]
    ppermute x1 -> x2, starting transfers between devices: 11 us -> 12.7 us  [shards(): lax.ppermute(rows, 'dc', [(0, 1), (1, 0)])]
    unnamed x5 -> x13, local copies, waits for them, and re-layouts: 0.08 us -> 1.61 us
    all_gather x1, blocking collectives: 12.1 us -> 13.5 us  [shards(): lax.all_gather(mirror_rows, 'dx', axis=1)]
  transfers between devices with their start and end apart: 3 -> 4, of which waited for: 1 -> 1; matrix products, arithmetic and copies ran while one was open for 5% -> 6% of each run, Pallas kernels for 6% -> 6%
where the time goes in v19:
time: 98.7 us; the launch traced here: 98.3 us
  blocking collectives  55.5 us (56%)
  starting transfers between devices  21.9 us (22%)
  local copies, waits for them, and re-layouts  6.18 us (6%)
  other arithmetic  5.75 us (6%)
  Pallas kernels  5.61 us (6%)
  matrix products  1.44 us (1%)
    all_gather x1, blocking collectives, shards(): own_rows = lax.all_gather(own_rows, 'dz', axis=1)  29.5 us
    all_gather x1, blocking collectives, shards(): lax.all_gather(mirror_rows, 'dx', axis=1)  13.5 us
    ppermute x2, starting transfers between devices, shards(): lax.ppermute(rows, 'dc', [(0, 1), (1, 0)])  12.7 us
    all_gather x1, blocking collectives, shards(): lax.all_gather(own_rows[0], 'dx', axis=1)  12.5 us
    ppermute x2, starting transfers between devices, mirror(): return lax.ppermute(block, PIPE, route)  9.24 us
    pallas_call x1, Pallas kernels, update(): pl.pallas_call(functools.partial(update_kernel, scale=scale, rate=rate),...  5.61 us
  transfers between devices with their start and end apart: 4, of which 1 were waited for; matrix products, arithmetic and copies ran while one was open for 6% of the time, Pallas kernels for 6%

profile of v19, /device:TPU:1, one launch (start us, length us, event | category | flops | bytes accessed | tf_op | source)
XLA Modules:
  0.0 98.3 jit_solution(2069742739888985250)
XLA Ops:
  0.6 1.1 %fusion.3 = bf16[1,2,2,4,3584]{4,3,2,1,0:T(4,128)(2,1)S(1)} fusion(bf16[1,2,2,4,3584]{4,3,2,1,0:T(4,128)(2,1)} %param.4, s32[2,2]{1,0:T(2,128)} %bitcast.56), kind=kLoop, calls=%fused_computation.13 | loop fusion | flops 114688 | bytes 229392 | tf_op jit(solution)/shard_map/jit(_where)/select_n | solution.py:70
  1.8 29.5 %all_gather.9 = bf16[2,4,8,3584]{3,2,1,0:T(8,128)(2,1)S(1)} all-gather(bf16[2,1,8,3584]{3,2,1,0:T(8,128)(2,1)S(1)} %pad_maximum_fusion.3), channel_id=1, replica_groups=mesh['py'=4,'pz'=4,'dz'=4,'dx'=4,'dc'=2] {'dz'}, dimensions={1}, use_global_device_ids=true | all-gather | bytes 573440 | tf_op jit(solution)/shard_map/all_gather | solution.py:73
  31.4 0.3 reshape_squeeze.3
  31.8 6.1 %collective-permute-start = (bf16[1472,128]{1,0:T(8,128)(2,1)S(1)}, bf16[1472,128]{1,0:T(8,128)(2,1)S(1)}, u32[]{:S(2)}, u32[]{:S(2)}) collective-permute-start(bf16[1472,128]{1,0:T(8,128)(2,1)S(1)} %pad_maximum_fusion.2), channel_id=1, source_target_pairs={{0,480},{32,448},{64,416},{96,384},{128,352},{160,320},{192,288},{... | collective-permute-start | bytes 1130504 | tf_op jit(solution)/shard_map/ppermute | solution.py:21
  37.9 12.5 %all-gather = bf16[1,4,32,3584]{3,2,1,0:T(8,128)(2,1)S(1)} all-gather(bf16[1,4,8,3584]{3,2,1,0:T(8,128)(2,1)S(1)} %get-tuple-element.2), channel_id=2, replica_groups=mesh['py'=4,'pz'=4,'dz'=4,'dx'=4,'dc'=2] {'dx'}, dimensions={2}, use_global_device_ids=true | all-gather | bytes 1146880 | tf_op jit(solution)/shard_map/all_gather | solution.py:76
  50.3 9.2 %collective-permute-start.1 = (bf16[4,4,8,3584]{3,2,1,0:T(8,128)(2,1)S(1)}, bf16[4,4,8,3584]{3,2,1,0:T(8,128)(2,1)}, u32[]{:S(2)}, u32[]{:S(2)}) collective-permute-start(bf16[4,4,8,3584]{3,2,1,0:T(8,128)(2,1)S(1)} %bitcast.43), channel_id=1, source_target_pairs={{0,1},{1,0},{2,3},{3,2},{4,5},{5,4},{6,7},{7,6},{8,9},{9,8},{10,11... | collective-permute-start | bytes 2752520 | tf_op jit(solution)/shard_map/ppermute | solution.py:77
  59.6 0.2 copy.32
  59.8 0.8 copy.34
  60.6 0.3 all_gather_reshape.4
  60.8 13.5 %all_gather.11 = bf16[4,4,8,3584]{3,2,1,0:T(8,128)(2,1)} all-gather(bf16[4,1,8,3584]{3,2,1,0:T(8,128)(2,1)S(1)} %bitcast.48), channel_id=1, replica_groups=mesh['py'=4,'pz'=4,'dz'=4,'dx'=4,'dc'=2] {'dx'}, dimensions={1}, use_global_device_ids=true | all-gather | bytes 1146880 | tf_op jit(solution)/shard_map/all_gather | solution.py:76
  74.3 3.5 %collective-permute-start.2 = (bf16[4,4,8,3584]{3,2,1,0:T(8,128)(2,1)}, bf16[4,4,8,3584]{3,2,1,0:T(8,128)(2,1)}, u32[]{:S(2)}, u32[]{:S(2)}) collective-permute-start(bf16[4,4,8,3584]{3,2,1,0:T(8,128)(2,1)} %all_gather.11), channel_id=1, source_target_pairs={{0,1},{1,0},{2,3},{3,2},{4,5},{5,4},{6,7},{7,6},{8,9},{9,8},{10,11... | collective-permute-start | bytes 2752520 | tf_op jit(solution)/shard_map/ppermute | solution.py:77
  77.8 1.5 %pad_maximum_fusion = bf16[2,4,4,8,3584]{4,3,2,1,0:T(8,128)(2,1)S(1)} fusion(bf16[1,4,4,8,3584]{4,3,2,1,0:T(8,128)(2,1)} %bitcast.6, bf16[1,4,4,8,3584]{4,3,2,1,0:T(8,128)(2,1)S(1)} %bitcast.44), kind=kLoop, calls=%fused_computation | loop fusion | flops 917504 | bytes 3670016 | tf_op jit(solution)/shard_map/stack | solution.py:78
  79.3 0.3 copy-done.2
  79.7 0.7 fusion
  80.4 0.2 copy-done
  80.6 0.2 copy.26
  80.9 0.2 copy.33
  81.2 0.5 copy-done.4
  81.7 0.3 maximum_bitcast_fusion
  82.0 1.8 %pad_maximum_fusion.1 = bf16[2,4,4,8,3584]{4,3,2,1,0:T(8,128)(2,1)S(1)} fusion(bf16[1,4,4,8,3584]{4,3,2,1,0:T(8,128)(2,1)} %bitcast.11, bf16[1,4,4,8,3584]{4,3,2,1,0:T(8,128)(2,1)} %bitcast.10), kind=kLoop, calls=%fused_computation.1 | loop fusion | flops 917504 | bytes 3670016 | tf_op jit(solution)/shard_map/stack | solution.py:77
  83.8 0.3 copy-done.3
  84.2 0.7 fusion.1
  84.9 0.2 copy-done.1
  85.4 0.4 reverse_select_fusion
  86.1 0.2 copy.30
  86.3 3.1 %collective-permute-start.3 = (bf16[2,128,288]{1,2,0:T(8,128)(2,1)S(1)}, bf16[2,128,288]{1,2,0:T(8,128)(2,1)S(1)}, u32[]{:S(2)}, u32[]{:S(2)}) collective-permute-start(bf16[2,128,288]{1,2,0:T(8,128)(2,1)S(1)} %copy.30), channel_id=1, source_target_pairs={{0,480},{32,448},{64,416},{96,384},{128,352},{160,320},{192,288},{... | collective-permute-start | bytes 442376 | tf_op jit(solution)/shard_map/ppermute | solution.py:21
  89.6 0.2 copy.31
  89.8 0.4 copy.36
  90.2 0.8 copy.37.acts_ref
  91.0 5.6 %shard_map.59 = bf16[288,3584]{1,0:T(8,128)(2,1)} custom-call(bf16[256,3584]{1,0:T(8,128)(2,1)} %bitcast.40, bf16[256,3584]{1,0:T(8,128)(2,1)} %bitcast.42, bf16[2,256,288]{2,1,0:T(8,128)(2,1)} %copy.37.acts_ref, bf16[288,3584]{1,0:T(8,128)(2,1)} %bitcast.45), custom_call_target="tpu_custom_call" | custom-call | tf_op jit(solution)/shard_map/pallas_call | solution.py:46
  96.6 0.9 collective-permute-done.3
  97.6 0.7 maximum_bitcast_fusion.1
  (28 shorter events, 1.2 us)
Async XLA Ops:
  0.6 31.1 %copy-start.5 = (bf16[1,2,2,128,288]{3,4,2,1,0:T(8,128)(2,1)S(1)}, bf16[1,2,2,128,288]{3,4,2,1,0:T(8,128)(2,1)}, u32[]{:S(2)}) copy-start(bf16[1,2,2,128,288]{3,4,2,1,0:T(8,128)(2,1)} %param.5) | copy-start | bytes 884740
  31.8 28.8 %collective-permute-start = (bf16[1472,128]{1,0:T(8,128)(2,1)S(1)}, bf16[1472,128]{1,0:T(8,128)(2,1)S(1)}, u32[]{:S(2)}, u32[]{:S(2)}) collective-permute-start(bf16[1472,128]{1,0:T(8,128)(2,1)S(1)} %pad_maximum_fusion.2), channel_id=1, source_target_pairs={{0,480},{32,448},{64,416},{96,384},{128,352},{160,320},{192,288},{... | collective-permute-start | bytes 1130504 | tf_op jit(solution)/shard_map/ppermute | solution.py:21
  50.3 31.7 %collective-permute-start.1 = (bf16[4,4,8,3584]{3,2,1,0:T(8,128)(2,1)S(1)}, bf16[4,4,8,3584]{3,2,1,0:T(8,128)(2,1)}, u32[]{:S(2)}, u32[]{:S(2)}) collective-permute-start(bf16[4,4,8,3584]{3,2,1,0:T(8,128)(2,1)S(1)} %bitcast.43), channel_id=1, source_target_pairs={{0,1},{1,0},{2,3},{3,2},{4,5},{5,4},{6,7},{7,6},{8,9},{9,8},{10,11... | collective-permute-start | bytes 2752520 | tf_op jit(solution)/shard_map/ppermute | solution.py:77
  74.3 7.7 %collective-permute-start.2 = (bf16[4,4,8,3584]{3,2,1,0:T(8,128)(2,1)}, bf16[4,4,8,3584]{3,2,1,0:T(8,128)(2,1)}, u32[]{:S(2)}, u32[]{:S(2)}) collective-permute-start(bf16[4,4,8,3584]{3,2,1,0:T(8,128)(2,1)} %all_gather.11), channel_id=1, source_target_pairs={{0,1},{1,0},{2,3},{3,2},{4,5},{5,4},{6,7},{7,6},{8,9},{9,8},{10,11... | collective-permute-start | bytes 2752520 | tf_op jit(solution)/shard_map/ppermute | solution.py:77
  77.8 1.9 %copy-start.2 = (bf16[1,288,3584]{2,1,0:T(8,128)(2,1)S(1)}, bf16[1,288,3584]{2,1,0:T(8,128)(2,1)}, u32[]{:S(2)}) copy-start(bf16[1,288,3584]{2,1,0:T(8,128)(2,1)} %param.6) | copy-start | bytes 6193156
  79.3 1.3 %copy-start = (bf16[2,4,4,8,3584]{4,3,2,1,0:T(8,128)(2,1)}, bf16[2,4,4,8,3584]{4,3,2,1,0:T(8,128)(2,1)S(1)}, u32[]{:S(2)}) copy-start(bf16[2,4,4,8,3584]{4,3,2,1,0:T(8,128)(2,1)S(1)} %pad_maximum_fusion) | copy-start | bytes 5505028
  80.8 0.9 copy-start.4
  82.0 2.1 %copy-start.3 = (bf16[1,288,3584]{2,1,0:T(8,128)(2,1)S(1)}, bf16[1,288,3584]{2,1,0:T(8,128)(2,1)}, u32[]{:S(2)}) copy-start(bf16[1,288,3584]{2,1,0:T(8,128)(2,1)} %param.6) | copy-start | bytes 6193156
  83.8 1.2 %copy-start.1 = (bf16[2,4,4,8,3584]{4,3,2,1,0:T(8,128)(2,1)}, bf16[2,4,4,8,3584]{4,3,2,1,0:T(8,128)(2,1)S(1)}, u32[]{:S(2)}) copy-start(bf16[2,4,4,8,3584]{4,3,2,1,0:T(8,128)(2,1)S(1)} %pad_maximum_fusion.1) | copy-start | bytes 5505028
  86.3 11.3 %collective-permute-start.3 = (bf16[2,128,288]{1,2,0:T(8,128)(2,1)S(1)}, bf16[2,128,288]{1,2,0:T(8,128)(2,1)S(1)}, u32[]{:S(2)}, u32[]{:S(2)}) collective-permute-start(bf16[2,128,288]{1,2,0:T(8,128)(2,1)S(1)} %copy.30), channel_id=1, source_target_pairs={{0,480},{32,448},{64,416},{96,384},{128,352},{160,320},{192,288},{... | collective-permute-start | bytes 442376 | tf_op jit(solution)/shard_map/ppermute | solution.py:21

commit v20 on v17

--- a/solution.py
+++ b/solution.py
@@ -77,7 +77,7 @@
         [lax.all_gather(own_rows[0], "dx", axis=1), lax.all_gather(mirror_rows, "dx", axis=1)], axis=0
     )
     other_rows = lax.ppermute(both_rows, "dc", [(0, 1), (1, 0)])
-    both_hidden = jnp.stack([hidden[0, 0], mirror_hidden], axis=0)
+    both_hidden = hidden[0].at[1].set(mirror_hidden)
     pieces = [both_rows.reshape(-1, full_width), other_rows.reshape(-1, full_width)]
     acts = both_hidden.reshape(2, micro, n_z, n_x, n_c, row_total, share).transpose(4, 0, 2, 3, 1, 5, 6)
     acts = own_first(acts).reshape(n_c, -1, share)

time: 93.6 us -> 94.5 us (level)
  local copies, waits for them, and re-layouts: 3.98 us -> 5.03 us
    unnamed x5 -> x4, local copies, waits for them, and re-layouts: 0.08 us -> 1.04 us
  transfers between devices with their start and end apart: 3 -> 3, of which waited for: 1 -> 2; matrix products, arithmetic and copies ran while one was open for 5% -> 5% of each run, Pallas kernels for 6% -> 6%
where the time goes in v20:
time: 94.5 us; the launch traced here: 94.1 us
  blocking collectives  54.1 us (57%)
  starting transfers between devices  20.3 us (21%)
  Pallas kernels  5.61 us (6%)
  matrix products  5.17 us (5%)
  local copies, waits for them, and re-layouts  5.03 us (5%)
  other arithmetic  2.31 us (2%)
    all_gather x1, blocking collectives, shards(): own_rows = lax.all_gather(own_rows, 'dz', axis=1)  29.5 us
    all_gather x1, blocking collectives, shards(): lax.all_gather(own_rows[0], 'dx', axis=1)  12.5 us
    all_gather x1, blocking collectives, shards(): lax.all_gather(mirror_rows, 'dx', axis=1)  12.1 us
    ppermute x1, starting transfers between devices, shards(): other_rows = lax.ppermute(both_rows, 'dc', [(0, 1), (1, 0)])  11 us
    ppermute x2, starting transfers between devices, mirror(): return lax.ppermute(block, PIPE, route)  9.24 us
    pallas_call x1, Pallas kernels, update(): pl.pallas_call(functools.partial(update_kernel, scale=scale, rate=rate),...  5.61 us
    dot_general x2, matrix products, shards(): grad = jnp.dot(piece, own_weight.T, preferred_element_type=jnp.float32)  5.17 us
  transfers between devices with their start and end apart: 3, of which 2 were waited for; matrix products, arithmetic and copies ran while one was open for 5% of the time, Pallas kernels for 6%

profile of v20, /device:TPU:1, one launch (start us, length us, event | category | flops | bytes accessed | tf_op | source)
XLA Modules:
  0.0 94.1 jit_solution(1398645829335547565)
XLA Ops:
  0.6 1.0 %copy.26 = bf16[1,2,2,128,288]{3,4,2,1,0:T(8,128)(2,1)S(1)} copy(bf16[1,2,2,128,288]{3,4,2,1,0:T(8,128)(2,1)} %param.7) | data formatting | bytes 589824
  1.6 1.0 %fusion.3 = bf16[1,2,2,4,3584]{4,3,2,1,0:T(4,128)(2,1)S(1)} fusion(bf16[1,2,2,4,3584]{4,3,2,1,0:T(4,128)(2,1)} %param.6, s32[2,2]{1,0:T(2,128)} %bitcast.53), kind=kLoop, calls=%fused_computation.12 | loop fusion | flops 114688 | bytes 229392 | tf_op jit(solution)/shard_map/jit(_where)/select_n | solution.py:70
  2.7 29.5 %all_gather.9 = bf16[2,4,8,3584]{3,2,1,0:T(8,128)(2,1)S(1)} all-gather(bf16[2,1,8,3584]{3,2,1,0:T(8,128)(2,1)S(1)} %pad_maximum_fusion.2), channel_id=1, replica_groups=mesh['py'=4,'pz'=4,'dz'=4,'dx'=4,'dc'=2] {'dz'}, dimensions={1}, use_global_device_ids=true | all-gather | bytes 573440 | tf_op jit(solution)/shard_map/all_gather | solution.py:73
  32.3 0.3 reshape_squeeze.3
  32.7 6.1 %collective-permute-start = (bf16[1472,128]{1,0:T(8,128)(2,1)S(1)}, bf16[1472,128]{1,0:T(8,128)(2,1)S(1)}, u32[]{:S(2)}, u32[]{:S(2)}) collective-permute-start(bf16[1472,128]{1,0:T(8,128)(2,1)S(1)} %pad_maximum_fusion.1), channel_id=1, source_target_pairs={{0,480},{32,448},{64,416},{96,384},{128,352},{160,320},{192,288},{... | collective-permute-start | bytes 1130504 | tf_op jit(solution)/shard_map/ppermute | solution.py:21
  38.8 12.5 %all-gather = bf16[1,4,32,3584]{3,2,1,0:T(8,128)(2,1)S(1)} all-gather(bf16[1,4,8,3584]{3,2,1,0:T(8,128)(2,1)S(1)} %get-tuple-element.14), channel_id=2, replica_groups=mesh['py'=4,'pz'=4,'dz'=4,'dx'=4,'dc'=2] {'dx'}, dimensions={2}, use_global_device_ids=true | all-gather | bytes 1146880 | tf_op jit(solution)/shard_map/all_gather | solution.py:77
  51.3 0.3 all_gather_reshape.4
  51.5 12.1 %all_gather.11 = bf16[4,4,8,3584]{3,2,1,0:T(8,128)(2,1)S(1)} all-gather(bf16[4,1,8,3584]{3,2,1,0:T(8,128)(2,1)S(1)} %all_gather_reshape.4), channel_id=1, replica_groups=mesh['py'=4,'pz'=4,'dz'=4,'dx'=4,'dc'=2] {'dx'}, dimensions={1}, use_global_device_ids=true | all-gather | bytes 1146880 | tf_op jit(solution)/shard_map/all_gather | solution.py:77
  63.6 0.2 pad_maximum_fusion
  63.8 11.0 %collective-permute-start.1 = (bf16[2,4,4,8,3584]{4,3,2,1,0:T(8,128)(2,1)S(1)}, bf16[2,4,4,8,3584]{4,3,2,1,0:T(8,128)(2,1)}, u32[]{:S(2)}, u32[]{:S(2)}) collective-permute-start(bf16[2,4,4,8,3584]{4,3,2,1,0:T(8,128)(2,1)S(1)} %pad_maximum_fusion), channel_id=1, source_target_pairs={{0,1},{1,0},{2,3},{3,2},{4,5},{5,4},{6,7},{7,6},{8,9},{9,8},{10,11... | collective-permute-start | bytes 5505032 | tf_op jit(solution)/shard_map/ppermute | solution.py:79
  74.9 2.3 %fusion = bf16[256,288]{0,1:T(8,128)(2,1)S(1)} fusion(bf16[256,3584]{1,0:T(8,128)(2,1)S(1)} %bitcast.38, bf16[1,288,3584]{2,1,0:T(8,128)(2,1)} %param.8), kind=kOutput, calls=%fused_computation.3 | convolution fusion | flops 528629760 | bytes 4046848 | tf_op jit(solution)/shard_map/dot_general | solution.py:86
  77.2 0.2 copy.11
  77.3 0.1 stack.37
  77.5 0.5 copy.17
  77.9 0.2 copy.22
  78.1 0.1 constant_dynamic-update-slice_fusion.1
  78.2 0.2 collective-permute-done.1
  78.4 2.9 %fusion.1 = bf16[256,288]{0,1:T(8,128)(2,1)S(1)} fusion(bf16[256,3584]{1,0:T(8,128)(2,1)} %bitcast.8.other_ref, bf16[1,288,3584]{2,1,0:T(8,128)(2,1)} %param.8), kind=kOutput, calls=%fused_computation.4 | convolution fusion | flops 528629760 | bytes 4046848 | tf_op jit(solution)/shard_map/dot_general | solution.py:86
  81.2 0.2 copy.12
  81.5 0.1 constant_dynamic-update-slice_fusion
  81.6 0.4 reverse_select_fusion
  81.9 0.1 fusion.7
  82.1 0.2 copy.14
  82.2 0.2 copy.15
  82.5 3.1 %collective-permute-start.2 = (bf16[2,128,288]{1,2,0:T(8,128)(2,1)S(1)}, bf16[2,128,288]{1,2,0:T(8,128)(2,1)S(1)}, u32[]{:S(2)}, u32[]{:S(2)}) collective-permute-start(bf16[2,128,288]{1,2,0:T(8,128)(2,1)S(1)} %copy.15), channel_id=1, source_target_pairs={{0,480},{32,448},{64,416},{96,384},{128,352},{160,320},{192,288},{... | collective-permute-start | bytes 442376 | tf_op jit(solution)/shard_map/ppermute | solution.py:21
  85.6 0.2 copy.13
  85.8 0.2 copy.16
  86.0 0.4 copy.19
  86.4 0.8 copy.20.acts_ref
  87.2 5.6 %shard_map.59 = bf16[288,3584]{1,0:T(8,128)(2,1)} custom-call(bf16[256,3584]{1,0:T(8,128)(2,1)} %bitcast.39, bf16[256,3584]{1,0:T(8,128)(2,1)} %bitcast.8.other_ref, bf16[2,256,288]{2,1,0:T(8,128)(2,1)} %copy.20.acts_ref, bf16[288,3584]{1,0:T(8,128)(2,1)} %bitcast.42), custom_call_target="tpu_custom_call" | custom-call | tf_op jit(solution)/shard_map/pallas_call | solution.py:46
  92.8 0.6 collective-permute-done.2
  93.4 0.7 maximum_bitcast_fusion
  (14 shorter events, 0.3 us)
Async XLA Ops:
  32.7 18.6 %collective-permute-start = (bf16[1472,128]{1,0:T(8,128)(2,1)S(1)}, bf16[1472,128]{1,0:T(8,128)(2,1)S(1)}, u32[]{:S(2)}, u32[]{:S(2)}) collective-permute-start(bf16[1472,128]{1,0:T(8,128)(2,1)S(1)} %pad_maximum_fusion.1), channel_id=1, source_target_pairs={{0,480},{32,448},{64,416},{96,384},{128,352},{160,320},{192,288},{... | collective-permute-start | bytes 1130504 | tf_op jit(solution)/shard_map/ppermute | solution.py:21
  63.8 13.4 %copy-start = (bf16[2,4,4,8,3584]{4,3,2,1,0:T(8,128)(2,1)}, bf16[2,4,4,8,3584]{4,3,2,1,0:T(8,128)(2,1)S(1)}, u32[]{:S(2)}) copy-start(bf16[2,4,4,8,3584]{4,3,2,1,0:T(8,128)(2,1)S(1)} %pad_maximum_fusion) | copy-start | bytes 5505028
  63.8 14.6 %collective-permute-start.1 = (bf16[2,4,4,8,3584]{4,3,2,1,0:T(8,128)(2,1)S(1)}, bf16[2,4,4,8,3584]{4,3,2,1,0:T(8,128)(2,1)}, u32[]{:S(2)}, u32[]{:S(2)}) collective-permute-start(bf16[2,4,4,8,3584]{4,3,2,1,0:T(8,128)(2,1)S(1)} %pad_maximum_fusion), channel_id=1, source_target_pairs={{0,1},{1,0},{2,3},{3,2},{4,5},{5,4},{6,7},{7,6},{8,9},{9,8},{10,11... | collective-permute-start | bytes 5505032 | tf_op jit(solution)/shard_map/ppermute | solution.py:79
  82.5 10.9 %collective-permute-start.2 = (bf16[2,128,288]{1,2,0:T(8,128)(2,1)S(1)}, bf16[2,128,288]{1,2,0:T(8,128)(2,1)S(1)}, u32[]{:S(2)}, u32[]{:S(2)}) collective-permute-start(bf16[2,128,288]{1,2,0:T(8,128)(2,1)S(1)} %copy.15), channel_id=1, source_target_pairs={{0,480},{32,448},{64,416},{96,384},{128,352},{160,320},{192,288},{... | collective-permute-start | bytes 442376 | tf_op jit(solution)/shard_map/ppermute | solution.py:21
